TPU v7x, 32 devices: a whole 2x2x4 slice. The times are simulated.
32 devices in a mesh: win: 2 (over y), rows: 4 (over z), cols: 4 (over x, core).
Axes of the slice: x: 2, y: 2, z: 4, core: 2. Of those that a mesh axis runs over, the one named last changes fastest.
Arguments:
- feat_one: bfloat16 [256, 128, 48], P(('win', 'rows'), 'cols'), parts along dimension 0, may hold values from -6 to 6
- feat_two: bfloat16 [128, 64, 96], P(('win', 'rows'), 'cols'), parts along dimension 0, may hold values from -6 to 6
- feat_three: bfloat16 [64, 32, 192], P(('win', 'rows'), 'cols'), parts along dimension 0, may hold values from -6 to 6
- feat_four: bfloat16 [32, 16, 384], P(('win', 'rows'), 'cols'), parts along dimension 0, may hold values from -6 to 6
- conv_one: bfloat16 [864, 48], P(None, 'cols'), may hold values from -0.3125 to 0.3125
- conv_two: bfloat16 [1728, 96], P(None, 'cols'), may hold values from -0.21875 to 0.21875
- conv_three: bfloat16 [3456, 192], P(None, 'cols'), may hold values from -0.15625 to 0.15625
- conv_four: bfloat16 [6912, 384], P(None, 'cols'), may hold values from -0.109375 to 0.109375
- down_one: bfloat16 [432, 816], P(None, 'cols'), may hold values from -0.3125 to 0.3125
- down_two: bfloat16 [864, 672], P(None, 'cols'), may hold values from -0.21875 to 0.21875
- down_three: bfloat16 [1728, 384], P(None, 'cols'), may hold values from -0.15625 to 0.15625
- lift_two: bfloat16 [96, 48], P(None, 'cols'), may hold values from -0.625 to 0.625
- lift_three: bfloat16 [192, 144], P(None, 'cols'), may hold values from -0.4375 to 0.4375
- lift_four: bfloat16 [384, 336], P(None, 'cols'), may hold values from -0.3125 to 0.3125
- biases: float32 [3840], replicated, may hold values from -3 to 3
Outputs:
- joined_one: bfloat16 [256, 128, 48], P(('win', 'rows'), 'cols'), parts along dimension 0
- joined_two: bfloat16 [128, 64, 96], P(('win', 'rows'), 'cols'), parts along dimension 0
- joined_three: bfloat16 [64, 32, 192], P(('win', 'rows'), 'cols'), parts along dimension 0
- joined_four: bfloat16 [32, 16, 384], P(('win', 'rows'), 'cols'), parts along dimension 0
There are 2 independent parts, one for each index of `win`. A program takes and returns all parts, laid end to end along the dimension named above; an argument that names none is the same for every part. Nothing has to cross between parts.
All inputs are finite; a program needn't handle non-finite values.
Results may differ from a plain program's by a relative error of at most 0.0055.
Values may be sent and summed in bfloat16 or wider, within the bound.
No kernel may reach another device: no remote copies, remote signals or barrier semaphores. Data moves between devices by JAX's collectives and lax.ppermute only.
A program may use at most 64 MiB of HBM per device.

v0:
```python
import jax
import jax.numpy as jnp
from jax import lax
from jax.sharding import PartitionSpec as P

BLOCKS = 1


def extended_2(block, sides, width):
    for axis, dim in sides:
        count = lax.axis_size(axis)
        forward = [(i, i + 1) for i in range(count - 1)]
        backward = [(target, source) for source, target in forward]
        low = lax.ppermute(
            lax.slice_in_dim(block, block.shape[dim] - width, None, axis=dim), axis, forward
        )
        high = lax.ppermute(lax.slice_in_dim(block, 0, width, axis=dim), axis, backward)
        block = jnp.concatenate([low, block, high], axis=dim)
    return block


def shortened(value):
    return jax.tree.map(lambda a: a.astype(jnp.bfloat16) if a.dtype == jnp.float32 else a, value)


def passed_along(block, axis, distance):
    devices = range(lax.axis_size(axis))
    route = [(i - distance, i) for i in devices if i - distance in devices]
    return lax.ppermute(block, axis, route)


def offsets(width, blocks):
    start = 30 * blocks * width
    return (
        start,
        start + 17 * width,
        start + 31 * width,
        start + 39 * width,
        start + 40 * width,
        start + 43 * width,
    )


def patch_conv(extended, weight, stride):
    height = (extended.shape[0] - 3) // stride + 1
    breadth = (extended.shape[1] - 3) // stride + 1
    taps = []
    for row_tap in range(3):
        for col_tap in range(3):
            taps.append(
                lax.slice(
                    extended,
                    (row_tap, col_tap, 0),
                    (
                        row_tap + stride * (height - 1) + 1,
                        col_tap + stride * (breadth - 1) + 1,
                        extended.shape[2],
                    ),
                    (stride, stride, 1),
                )
            )
    stacked = jnp.concatenate(taps, axis=2)
    flat = stacked.reshape(height * breadth, stacked.shape[2])
    return jnp.dot(flat, weight, preferred_element_type=jnp.float32).reshape(
        height, breadth, weight.shape[1]
    )


def extend(feat, margin):
    return extended_2(feat, (("rows", 0), ("cols", 1)), margin)


def inside_mask(height, breadth):
    row_first = lax.axis_index("rows") * height - 1
    col_first = lax.axis_index("cols") * breadth - 1
    row_global = row_first + jnp.arange(height + 2, dtype=jnp.int32)
    col_global = col_first + jnp.arange(breadth + 2, dtype=jnp.int32)
    row_valid = (row_global >= 0) & (row_global < height * lax.axis_size("rows"))
    col_valid = (col_global >= 0) & (col_global < breadth * lax.axis_size("cols"))
    return (row_valid[:, None] & col_valid[None, :])[:, :, None]


def spatial_blocks(feat, weight, biases, base):
    height, breadth, width = feat.shape
    first = weight[0 : 9 * width]
    second = weight[9 * width : 18 * width]
    bias_a = biases[base : base + width]
    bias_b = biases[base + width : base + 2 * width]
    middle = jax.nn.relu(patch_conv(extend(feat, 2), first, 1) + bias_a)
    middle = jnp.where(inside_mask(height, breadth), middle, 0.0).astype(jnp.bfloat16)
    result = patch_conv(middle, second, 1)
    feat = jax.nn.relu(result + bias_b + feat.astype(jnp.float32)).astype(jnp.bfloat16)
    return feat


def rims(items):
    tops = passed_along(shortened(tuple((item[-1:] for item in items))), "rows", 1)
    taller = tuple((jnp.concatenate([top, item], axis=0) for top, item in zip(tops, items)))
    lefts = passed_along(shortened(tuple((item[:, -1:] for item in taller))), "cols", 1)
    return tuple((jnp.concatenate([left, item], axis=1) for left, item in zip(lefts, taller)))


def enlarge(values, factor):
    return jnp.repeat(jnp.repeat(values, factor, axis=0), factor, axis=1)


def point_conv(feat, weight, bias):
    height, breadth, channels = feat.shape
    flat = jnp.dot(
        feat.reshape(height * breadth, channels), weight, preferred_element_type=jnp.float32
    )
    return flat.reshape(height, breadth, weight.shape[1]) + bias


def on_device(
    feat_one,
    feat_two,
    feat_three,
    feat_four,
    conv_one,
    conv_two,
    conv_three,
    conv_four,
    down_one,
    down_two,
    down_three,
    lift_two,
    lift_three,
    lift_four,
    biases,
):
    unit = feat_one.shape[2]
    kernels = (
        lax.all_gather(conv_one, "cols", axis=1, tiled=True),
        lax.all_gather(conv_two, "cols", axis=1, tiled=True),
        lax.all_gather(conv_three, "cols", axis=1, tiled=True),
        lax.all_gather(down_one, "cols", axis=1, tiled=True),
        lax.all_gather(down_two, "cols", axis=1, tiled=True),
        lax.all_gather(down_three, "cols", axis=1, tiled=True),
        lax.all_gather(lift_two, "cols", axis=1, tiled=True),
        lax.all_gather(lift_three, "cols", axis=1, tiled=True),
        lax.all_gather(lift_four, "cols", axis=1, tiled=True),
    )
    w_one, w_two, w_three, w_down1, w_down2, w_down3, w_lift2, w_lift3, w_lift4 = kernels
    y_one = spatial_blocks(feat_one, w_one, biases, 0)
    y_two = spatial_blocks(feat_two, w_two, biases, 2 * BLOCKS * unit)
    y_three = spatial_blocks(feat_three, w_three, biases, 6 * BLOCKS * unit)
    w_four = lax.all_gather(conv_four, "cols", axis=1, tiled=True)
    y_four = spatial_blocks(feat_four, w_four, biases, 14 * BLOCKS * unit)
    off_d1, off_d2, off_d3, off_l2, off_l3, off_l4 = offsets(unit, BLOCKS)
    ext_one, ext_two, ext_three = rims((y_one, y_two, y_three))
    first = patch_conv(ext_one, w_down1[:, : 4 * unit], 2) + biases[off_d1 : off_d1 + 4 * unit]
    d12 = first[:, :, : 2 * unit]
    t13 = jax.nn.relu(first[:, :, 2 * unit : 3 * unit]).astype(jnp.bfloat16)
    t14 = jax.nn.relu(first[:, :, 3 * unit :]).astype(jnp.bfloat16)
    second = patch_conv(ext_two, w_down2[:, : 6 * unit], 2) + biases[off_d2 : off_d2 + 6 * unit]
    d23 = second[:, :, : 4 * unit]
    t24 = jax.nn.relu(second[:, :, 4 * unit :]).astype(jnp.bfloat16)
    d34 = patch_conv(ext_three, w_down3, 2) + biases[off_d3 : off_d3 + 8 * unit]
    e13, e14, e24 = rims((t13, t14, t24))
    d13 = (
        patch_conv(e13, w_down1[:, 4 * unit : 8 * unit], 2)
        + biases[off_d1 + 4 * unit : off_d1 + 8 * unit]
    )
    t14b = jax.nn.relu(
        patch_conv(e14, w_down1[:, 8 * unit : 9 * unit], 2)
        + biases[off_d1 + 8 * unit : off_d1 + 9 * unit]
    ).astype(jnp.bfloat16)
    d24 = (
        patch_conv(e24, w_down2[:, 6 * unit :], 2) + biases[off_d2 + 6 * unit : off_d2 + 14 * unit]
    )
    (e14b,) = rims((t14b,))
    d14 = (
        patch_conv(e14b, w_down1[:, 9 * unit :], 2) + biases[off_d1 + 9 * unit : off_d1 + 17 * unit]
    )
    u_two = point_conv(y_two, w_lift2, biases[off_l2 : off_l2 + unit])
    u_three = point_conv(y_three, w_lift3, biases[off_l3 : off_l3 + 3 * unit])
    u_four = point_conv(y_four, w_lift4, biases[off_l4 : off_l4 + 7 * unit])
    joined_one = (
        y_one.astype(jnp.float32)
        + enlarge(u_two, 2)
        + enlarge(u_three[:, :, :unit], 4)
        + enlarge(u_four[:, :, :unit], 8)
    )
    joined_two = (
        d12
        + y_two.astype(jnp.float32)
        + enlarge(u_three[:, :, unit:], 2)
        + enlarge(u_four[:, :, unit : 3 * unit], 4)
    )
    joined_three = d13 + d23 + y_three.astype(jnp.float32) + enlarge(u_four[:, :, 3 * unit :], 2)
    joined_four = d14 + d24 + d34 + y_four.astype(jnp.float32)
    return (
        jax.nn.relu(joined_one).astype(jnp.bfloat16),
        jax.nn.relu(joined_two).astype(jnp.bfloat16),
        jax.nn.relu(joined_three).astype(jnp.bfloat16),
        jax.nn.relu(joined_four).astype(jnp.bfloat16),
    )


def solution(mesh):
    placed = (
        P(("win", "rows"), "cols", None),
        P(("win", "rows"), "cols", None),
        P(("win", "rows"), "cols", None),
        P(("win", "rows"), "cols", None),
        P(None, "cols"),
        P(None, "cols"),
        P(None, "cols"),
        P(None, "cols"),
        P(None, "cols"),
        P(None, "cols"),
        P(None, "cols"),
        P(None, "cols"),
        P(None, "cols"),
        P(None, "cols"),
        P(),
    )
    return jax.shard_map(
        on_device,
        mesh=mesh,
        in_specs=placed,
        out_specs=(
            P(("win", "rows"), "cols", None),
            P(("win", "rows"), "cols", None),
            P(("win", "rows"), "cols", None),
            P(("win", "rows"), "cols", None),
        ),
        check_vma=False,
    )
```

profile of v0, /device:TPU:0, one launch (start us, length us, event | category | flops | bytes accessed | tf_op | source)
XLA Modules:
  0.0 218.7 jit_solution(7337313120745537531)
XLA Ops:
  7.3 0.7 all-gather.14.cloned.1.call-update
  8.0 0.7 all-gather.10.cloned.1.call-update
  8.8 0.7 all-gather.12.cloned.1.call-update
  9.6 5.0 %collective-permute-start.8 = (bf16[2,8,192]{2,1,0:T(8,128)(2,1)S(1)}, bf16[2,8,192]{2,1,0:T(8,128)(2,1)S(1)}, u32[]{:S(2)}, u32[]{:S(2)}) collective-permute-start(bf16[2,8,192]{2,1,0:T(8,128)(2,1)S(1)} %get-tuple-element.80), channel_id=1, source_target_pairs={{0,4},{4,8},{8,12},{1,5},{5,9},{9,13},{2,6},{6,10},{10,14},{3,7},{... | collective-permute-start | bytes 18440 | tf_op jit(solution)/shard_map/ppermute | solution.py:14
  14.5 1.3 collective-permute-start.9
  15.8 4.5 %collective-permute-start.4 = (bf16[2,16,96]{2,1,0:T(8,128)(2,1)S(1)}, bf16[2,16,96]{2,1,0:T(8,128)(2,1)S(1)}, u32[]{:S(2)}, u32[]{:S(2)}) collective-permute-start(bf16[2,16,96]{2,1,0:T(8,128)(2,1)S(1)} %get-tuple-element.67), channel_id=1, source_target_pairs={{0,4},{4,8},{8,12},{1,5},{5,9},{9,13},{2,6},{6,10},{10,14},{3,7},{... | collective-permute-start | bytes 18440 | tf_op jit(solution)/shard_map/ppermute | solution.py:14
  20.4 1.3 collective-permute-start.5
  21.7 4.5 %collective-permute-start.12 = (bf16[2,4,384]{2,1,0:T(4,128)(2,1)S(1)}, bf16[2,4,384]{2,1,0:T(4,128)(2,1)S(1)}, u32[]{:S(2)}, u32[]{:S(2)}) collective-permute-start(bf16[2,4,384]{2,1,0:T(4,128)(2,1)S(1)} %get-tuple-element.99), channel_id=1, source_target_pairs={{0,4},{4,8},{8,12},{1,5},{5,9},{9,13},{2,6},{6,10},{10,14},{3,7},{... | collective-permute-start | bytes 18440 | tf_op jit(solution)/shard_map/ppermute | solution.py:14
  26.3 0.7 fusion.100
  29.0 6.6 %all_gather.31 = bf16[1728,96]{0,1:T(8,128)(2,1)} all-gather(bf16[1728,24]{0,1:T(8,128)(2,1)S(1)} %copy-done.14), channel_id=1, replica_groups=mesh['win'=2,'rows'=4,'cols'=4] {'cols'}, dimensions={1}, use_global_device_ids=true | all-gather | bytes 414720 | tf_op jit(solution)/shard_map/all_gather | solution.py:135
  35.6 5.9 %all-gather.3 = bf16[4,84,384]{2,1,0:T(8,128)(2,1)S(1)} all-gather(bf16[1,84,384]{2,1,0:T(8,128)(2,1)S(1)} %bitcast.146), channel_id=1, replica_groups=mesh['win'=2,'rows'=4,'cols'=4] {'cols'}, dimensions={0}, use_global_device_ids=true | all-gather | bytes 322560 | tf_op jit(solution)/shard_map/all_gather | solution.py:142
  41.5 6.7 %all-gather = bf16[4,12,864]{2,1,0:T(8,128)(2,1)S(1)} all-gather(bf16[1,12,864]{2,1,0:T(8,128)(2,1)S(1)} %bitcast.147), channel_id=1, replica_groups=mesh['win'=2,'rows'=4,'cols'=4] {'cols'}, dimensions={0}, use_global_device_ids=true | all-gather | bytes 103680 | tf_op jit(solution)/shard_map/all_gather | solution.py:134
  48.2 9.1 %all-gather.4 = bf16[4,204,432]{2,1,0:T(8,128)(2,1)S(1)} all-gather(bf16[1,204,432]{2,1,0:T(8,128)(2,1)S(1)} %bitcast.141), channel_id=1, replica_groups=mesh['win'=2,'rows'=4,'cols'=4] {'cols'}, dimensions={0}, use_global_device_ids=true | all-gather | bytes 881280 | tf_op jit(solution)/shard_map/all_gather | solution.py:137
  60.0 5.7 %all-gather.2 = bf16[4,36,192]{2,1,0:T(8,128)(2,1)S(1)} all-gather(bf16[1,36,192]{2,1,0:T(8,128)(2,1)S(1)} %bitcast.148), channel_id=1, replica_groups=mesh['win'=2,'rows'=4,'cols'=4] {'cols'}, dimensions={0}, use_global_device_ids=true | all-gather | bytes 69120 | tf_op jit(solution)/shard_map/all_gather | solution.py:141
  68.3 5.4 %all-gather.1 = bf16[4,12,96]{2,1,0:T(8,128)(2,1)S(1)} all-gather(bf16[1,12,96]{2,1,0:T(8,128)(2,1)S(1)} %bitcast.149), channel_id=1, replica_groups=mesh['win'=2,'rows'=4,'cols'=4] {'cols'}, dimensions={0}, use_global_device_ids=true | all-gather | bytes 11520 | tf_op jit(solution)/shard_map/all_gather | solution.py:140
  74.3 0.8 reshape.330
  75.4 1.3 collective-permute-start.13
  76.8 4.5 %collective-permute-start = (bf16[2,32,48]{2,1,0:T(8,128)(2,1)S(1)}, bf16[2,32,48]{2,1,0:T(8,128)(2,1)S(1)}, u32[]{:S(2)}, u32[]{:S(2)}) collective-permute-start(bf16[2,32,48]{2,1,0:T(8,128)(2,1)S(1)} %get-tuple-element.30), channel_id=1, source_target_pairs={{0,4},{4,8},{8,12},{1,5},{5,9},{9,13},{2,6},{6,10},{10,14},{3,7},{... | collective-permute-start | bytes 18440 | tf_op jit(solution)/shard_map/ppermute | solution.py:14
  82.0 1.3 collective-permute-start.1
  83.3 1.3 collective-permute-start.11
  85.3 3.6 %collective-permute-start.10 = (bf16[12,2,192]{2,1,0:T(2,128)(2,1)}, bf16[12,2,192]{2,1,0:T(2,128)(2,1)}, u32[]{:S(2)}, u32[]{:S(2)}) collective-permute-start(bf16[12,2,192]{2,1,0:T(2,128)(2,1)} %get-tuple-element.78), channel_id=1, source_target_pairs={{0,1},{1,2},{2,3},{4,5},{5,6},{6,7},{8,9},{9,10},{10,11},{12,13},{... | collective-permute-start | bytes 27656 | tf_op jit(solution)/shard_map/ppermute | solution.py:14
  88.9 1.3 collective-permute-start.7
  90.3 1.3 collective-permute-start.3
  91.6 3.9 %collective-permute-start.2 = (bf16[36,2,48]{2,1,0:T(2,128)(2,1)S(1)}, bf16[36,2,48]{2,1,0:T(2,128)(2,1)S(1)}, u32[]{:S(2)}, u32[]{:S(2)}) collective-permute-start(bf16[36,2,48]{2,1,0:T(2,128)(2,1)S(1)} %get-tuple-element.26), channel_id=1, source_target_pairs={{0,1},{1,2},{2,3},{4,5},{5,6},{6,7},{8,9},{9,10},{10,11},{12,13},{... | collective-permute-start | bytes 20744 | tf_op jit(solution)/shard_map/ppermute | solution.py:14
  96.2 4.2 %collective-permute-start.6 = (bf16[20,2,96]{2,1,0:T(2,128)(2,1)}, bf16[20,2,96]{2,1,0:T(2,128)(2,1)}, u32[]{:S(2)}, u32[]{:S(2)}) collective-permute-start(bf16[20,2,96]{2,1,0:T(2,128)(2,1)} %get-tuple-element.56), channel_id=1, source_target_pairs={{0,1},{1,2},{2,3},{4,5},{5,6},{6,7},{8,9},{9,10},{10,11},{12,13},{... | collective-permute-start | bytes 23048 | tf_op jit(solution)/shard_map/ppermute | solution.py:14
  100.4 2.4 %collective-permute-start.14 = (bf16[8,2,384]{2,1,0:T(2,128)(2,1)}, bf16[8,2,384]{2,1,0:T(2,128)(2,1)}, u32[]{:S(2)}, u32[]{:S(2)}) collective-permute-start(bf16[8,2,384]{2,1,0:T(2,128)(2,1)} %get-tuple-element.82), channel_id=1, source_target_pairs={{0,1},{1,2},{2,3},{4,5},{5,6},{6,7},{8,9},{9,10},{10,11},{12,13},{... | collective-permute-start | bytes 36872 | tf_op jit(solution)/shard_map/ppermute | solution.py:14
  103.0 1.4 pad_maximum_fusion.2
  104.3 4.5 %concatenate.155 = bf16[34,34,432]{2,1,0:T(8,128)(2,1)} concatenate(bf16[34,34,48]{2,1,0:T(8,128)(2,1)S(1)} %get-tuple-element.23, bf16[34,34,48]{2,1,0:T(8,128)(2,1)S(1)} %get-tuple-element.114, bf16[34,34,48]{2,1,0:T(8,128)(2,1)S(1)} %get-tuple-element.17, bf16[34,34,48]{2,1,0:T(8,128)(2,1)S(1)} %get-tuple-element.22, bf16[34,34,48]{2,1,0:T(8,128)(2,1)} %get-tuple-element.115, ...), dimensions={2} | concatenate | bytes 1997568 | tf_op jit(solution)/shard_map/concatenate | solution.py:62
  108.9 1.9 fusion.8
  110.8 1.1 fusion.86
  111.8 2.6 %concatenate.156 = bf16[32,32,432]{2,1,0:T(8,128)(2,1)S(1)} concatenate(bf16[32,32,48]{2,1,0:T(8,128)(2,1)} %get-tuple-element.15, bf16[32,32,48]{2,1,0:T(8,128)(2,1)} %get-tuple-element.14, bf16[32,32,48]{2,1,0:T(8,128)(2,1)} %get-tuple-element.13, bf16[32,32,48]{2,1,0:T(8,128)(2,1)S(1)} %get-tuple-element.12, bf16[32,32,48]{2,1,0:T(8,128)(2,1)S(1)} %get-tuple-element.11, ...), dimensions={2} | concatenate | bytes 1769472 | tf_op jit(solution)/shard_map/concatenate | solution.py:62
  114.4 1.3 collective-permute-start.15
  115.7 1.0 pad_maximum_fusion.4
  116.7 2.2 pad_maximum_fusion.5
  118.9 1.5 concatenate.161
  122.6 4.5 %collective-permute-start.20 = (bf16[1,16,96]{2,1,0:T(8,128)(2,1)}, bf16[1,16,96]{2,1,0:T(8,128)(2,1)S(1)}, u32[]{:S(2)}, u32[]{:S(2)}) collective-permute-start(bf16[1,16,96]{2,1,0:T(8,128)(2,1)} %slice.962), channel_id=1, source_target_pairs={{0,4},{4,8},{8,12},{1,5},{5,9},{9,13},{2,6},{6,10},{10,14},{3,7},{... | collective-permute-start | bytes 9224 | tf_op jit(solution)/shard_map/ppermute | solution.py:29
  128.4 0.8 pad_maximum_fusion.7
  129.2 1.0 pad_maximum_fusion.11
  131.1 2.7 %collective-permute-start.21 = (bf16[17,1,96]{2,1,0:T(2,128)(2,1)S(1)}, bf16[17,1,96]{2,1,0:T(2,128)(2,1)S(1)}, u32[]{:S(2)}, u32[]{:S(2)}) collective-permute-start(bf16[17,1,96]{2,1,0:T(2,128)(2,1)S(1)} %fusion.81), channel_id=1, source_target_pairs={{0,1},{1,2},{2,3},{4,5},{5,6},{6,7},{8,9},{9,10},{10,11},{12,13},{... | collective-permute-start | bytes 9800 | tf_op jit(solution)/shard_map/ppermute | solution.py:29
  133.8 0.7 constant_dynamic-update-slice_fusion.20
  134.6 0.8 pad_maximum_fusion.13
  135.4 0.7 constant_dynamic-update-slice_fusion.17
  136.2 0.7 constant_dynamic-update-slice_fusion.14
  137.9 1.3 convolution_add_fusion.7
  139.4 3.1 %collective-permute-start.26 = (bf16[1,8,96]{2,1,0:T(8,128)(2,1)S(1)}, bf16[1,8,96]{2,1,0:T(8,128)(2,1)S(1)}, u32[]{:S(2)}, u32[]{:S(2)}) collective-permute-start(bf16[1,8,96]{2,1,0:T(8,128)(2,1)S(1)} %slice.978), channel_id=1, source_target_pairs={{0,4},{4,8},{8,12},{1,5},{5,9},{9,13},{2,6},{6,10},{10,14},{3,7},{... | collective-permute-start | bytes 4616 | tf_op jit(solution)/shard_map/ppermute | solution.py:29
  143.8 2.1 collective-permute-start.27
  147.4 1.5 fusion.17
  149.1 1.5 fusion.29
  150.7 4.1 %collective-permute-start.28 = (bf16[1,8,192]{2,1,0:T(8,128)(2,1)S(1)}, bf16[1,8,192]{2,1,0:T(8,128)(2,1)S(1)}, u32[]{:S(2)}, u32[]{:S(2)}) collective-permute-start(bf16[1,8,192]{2,1,0:T(8,128)(2,1)S(1)} %slice.982), channel_id=1, source_target_pairs={{0,4},{4,8},{8,12},{1,5},{5,9},{9,13},{2,6},{6,10},{10,14},{3,7},{... | collective-permute-start | bytes 9224 | tf_op jit(solution)/shard_map/ppermute | solution.py:29
  156.4 2.3 %collective-permute-start.29 = (bf16[9,1,192]{2,1,0:T(2,128)(2,1)S(1)}, bf16[9,1,192]{2,1,0:T(2,128)(2,1)S(1)}, u32[]{:S(2)}, u32[]{:S(2)}) collective-permute-start(bf16[9,1,192]{2,1,0:T(2,128)(2,1)S(1)} %fusion.79), channel_id=1, source_target_pairs={{0,1},{1,2},{2,3},{4,5},{5,6},{6,7},{8,9},{9,10},{10,11},{12,13},{... | collective-permute-start | bytes 10376 | tf_op jit(solution)/shard_map/ppermute | solution.py:29
  158.7 2.7 %fusion.28 = bf16[6,6,384]{2,1,0:T(8,128)(2,1)S(1)} fusion(bf16[6,6,3456]{2,1,0:T(8,128)(2,1)S(1)} %constant_dynamic-update-slice_fusion.12, bf16[6912,384]{0,1:T(8,128)(2,1)} %all-gather.12.cloned.1.call-done, f32[384]{0:T(512)S(1)} %copy-done.37, pred[6,6]{1,0:T(8,128)(4,1)S(1)} %copy-done.40), kind=kOutput, calls=%fused_computation.41 | convolution fusion | flops 95606784 | bytes 2932260 | tf_op jit(solution)/shard_map/dot_general | solution.py:64
  161.7 2.6 %fusion.52 = bf16[4,4,384]{2,1,0:T(4,128)(2,1)S(1)} fusion(bf16[4,4,3456]{2,1,0:T(4,128)(2,1)S(1)} %constant_dynamic-update-slice_fusion.21, bf16[6912,384]{0,1:T(8,128)(2,1)} %all-gather.12.cloned.1.call-done, bf16[4,4,384]{2,1,0:T(4,128)(2,1)S(1)} %copy-done.20, f32[384]{0:T(512)S(1)} %copy-done.36), kind=kOutput, calls=%fused_computation.59 | convolution fusion | flops 42498048 | bytes 2790912 | tf_op jit(solution)/shard_map/dot_general | solution.py:64
  165.4 1.2 fusion.54
  166.6 3.7 %collective-permute-start.16 = (bf16[1,32,48]{2,1,0:T(8,128)(2,1)S(1)}, bf16[1,32,48]{2,1,0:T(8,128)(2,1)S(1)}, u32[]{:S(2)}, u32[]{:S(2)}) collective-permute-start(bf16[1,32,48]{2,1,0:T(8,128)(2,1)S(1)} %slice.950), channel_id=1, source_target_pairs={{0,4},{4,8},{8,12},{1,5},{5,9},{9,13},{2,6},{6,10},{10,14},{3,7},{... | collective-permute-start | bytes 9224 | tf_op jit(solution)/shard_map/ppermute | solution.py:29
  173.4 5.1 %collective-permute-start.17 = (bf16[33,1,48]{2,1,0:T(2,128)(2,1)S(1)}, bf16[33,1,48]{2,1,0:T(2,128)(2,1)S(1)}, u32[]{:S(2)}, u32[]{:S(2)}) collective-permute-start(bf16[33,1,48]{2,1,0:T(2,128)(2,1)S(1)} %fusion.78), channel_id=1, source_target_pairs={{0,1},{1,2},{2,3},{4,5},{5,6},{6,7},{8,9},{9,10},{10,11},{12,13},{... | collective-permute-start | bytes 9512 | tf_op jit(solution)/shard_map/ppermute | solution.py:29
  181.6 3.7 %collective-permute-start.18 = (bf16[1,16,48]{2,1,0:T(8,128)(2,1)S(1)}, bf16[1,16,48]{2,1,0:T(8,128)(2,1)S(1)}, u32[]{:S(2)}, u32[]{:S(2)}) collective-permute-start(bf16[1,16,48]{2,1,0:T(8,128)(2,1)S(1)} %slice.958), channel_id=1, source_target_pairs={{0,4},{4,8},{8,12},{1,5},{5,9},{9,13},{2,6},{6,10},{10,14},{3,7},{... | collective-permute-start | bytes 4616 | tf_op jit(solution)/shard_map/ppermute | solution.py:29
  188.2 2.2 %collective-permute-start.22 = (bf16[1,16,48]{2,1,0:T(8,128)(2,1)S(1)}, bf16[1,16,48]{2,1,0:T(8,128)(2,1)S(1)}, u32[]{:S(2)}, u32[]{:S(2)}) collective-permute-start(bf16[1,16,48]{2,1,0:T(8,128)(2,1)S(1)} %slice.969), channel_id=1, source_target_pairs={{0,4},{4,8},{8,12},{1,5},{5,9},{9,13},{2,6},{6,10},{10,14},{3,7},{... | collective-permute-start | bytes 4616 | tf_op jit(solution)/shard_map/ppermute | solution.py:29
  190.5 1.9 collective-permute-start.19
  193.3 4.7 %collective-permute-start.23 = (bf16[17,1,48]{2,1,0:T(2,128)(2,1)S(1)}, bf16[17,1,48]{2,1,0:T(2,128)(2,1)S(1)}, u32[]{:S(2)}, u32[]{:S(2)}) collective-permute-start(bf16[17,1,48]{2,1,0:T(2,128)(2,1)S(1)} %fusion.80), channel_id=1, source_target_pairs={{0,1},{1,2},{2,3},{4,5},{5,6},{6,7},{8,9},{9,10},{10,11},{12,13},{... | collective-permute-start | bytes 4904 | tf_op jit(solution)/shard_map/ppermute | solution.py:29
  200.0 2.2 %collective-permute-start.24 = (bf16[1,8,48]{2,1,0:T(8,128)(2,1)S(1)}, bf16[1,8,48]{2,1,0:T(8,128)(2,1)S(1)}, u32[]{:S(2)}, u32[]{:S(2)}) collective-permute-start(bf16[1,8,48]{2,1,0:T(8,128)(2,1)S(1)} %slice.973), channel_id=1, source_target_pairs={{0,4},{4,8},{8,12},{1,5},{5,9},{9,13},{2,6},{6,10},{10,14},{3,7},{... | collective-permute-start | bytes 2312 | tf_op jit(solution)/shard_map/ppermute | solution.py:29
  202.3 0.8 fusion.30
  203.8 2.9 %collective-permute-start.25 = (bf16[9,1,48]{2,1,0:T(2,128)(2,1)S(1)}, bf16[9,1,48]{2,1,0:T(2,128)(2,1)S(1)}, u32[]{:S(2)}, u32[]{:S(2)}) collective-permute-start(bf16[9,1,48]{2,1,0:T(2,128)(2,1)S(1)} %fusion.84), channel_id=1, source_target_pairs={{0,1},{1,2},{2,3},{4,5},{5,6},{6,7},{8,9},{9,10},{10,11},{12,13},{... | collective-permute-start | bytes 2600 | tf_op jit(solution)/shard_map/ppermute | solution.py:29
  208.3 1.4 fusion.48
  209.8 2.4 %fusion.49 = bf16[4,4,384]{2,1,0:T(4,128)(2,1)} fusion(f32[4,4,384]{2,1,0:T(4,128)S(1)} %fusion.48, bf16[4,4,1728]{2,1,0:T(4,128)(2,1)S(1)} %concatenate.195, bf16[1728,384]{0,1:T(8,128)(2,1)} %all-gather.16.cloned.1.call-done, bf16[4,4,384]{2,1,0:T(4,128)(2,1)S(1)} %fusion.52, f32[384]{0:T(512)S(1)} %get-tuple-element.83), kind=kOutput, calls=%fused_computation.58 | convolution fusion | flops 21270528 | bytes 1433088 | tf_op jit(solution)/shard_map/dot_general | solution.py:64
  (315 shorter events, 35.4 us)
Async XLA Ops:
  7.2 8.6 %copy-start.7 = (bf16[16,16,96]{2,1,0:T(8,128)(2,1)S(1)}, bf16[16,16,96]{2,1,0:T(8,128)(2,1)}, u32[]{:S(2)}) copy-start(bf16[16,16,96]{2,1,0:T(8,128)(2,1)} %param.16) | copy-start | bytes 147460
  7.2 14.5 %copy-start.19 = (bf16[4,4,384]{2,1,0:T(4,128)(2,1)S(1)}, bf16[4,4,384]{2,1,0:T(4,128)(2,1)}, u32[]{:S(2)}) copy-start(bf16[4,4,384]{2,1,0:T(4,128)(2,1)} %param.18) | copy-start | bytes 36868
  7.2 19.1 %copy-start.21 = (f32[3840]{0:T(1024)S(1)}, f32[3840]{0:T(1024)}, u32[]{:S(2)}) copy-start(f32[3840]{0:T(1024)} %param.29) | copy-start | bytes 46084
  7.2 21.8 %copy-start.14 = (bf16[1728,24]{0,1:T(8,128)(2,1)S(1)}, bf16[1728,24]{0,1:T(8,128)(2,1)}, u32[]{:S(2)}) copy-start(bf16[1728,24]{0,1:T(8,128)(2,1)} %param.20) | copy-start | bytes 248836
  7.2 130.7 %all-gather.14.cloned.1.call-start = ((), (), s32[]{:S(2)}) async-start(), calls=%async_computation.2 | async-start | bytes 1505280 | tf_op jit(solution)/shard_map/all_gather | solution.py:138
  8.0 27.7 %copy-start.17 = (bf16[384,84]{0,1:T(8,128)(2,1)S(1)}, bf16[384,84]{0,1:T(8,128)(2,1)}, u32[]{:S(2)}) copy-start(bf16[384,84]{0,1:T(8,128)(2,1)} %param.28) | copy-start | bytes 193540
  8.0 139.4 %all-gather.10.cloned.1.call-start = ((), (), s32[]{:S(2)}) async-start(), calls=%async_computation | async-start | bytes 1658880 | tf_op jit(solution)/shard_map/all_gather | solution.py:136
  8.7 32.8 %copy-start = (bf16[32,32,48]{2,1,0:T(8,128)(2,1)S(1)}, bf16[32,32,48]{2,1,0:T(8,128)(2,1)}, u32[]{:S(2)}) copy-start(bf16[32,32,48]{2,1,0:T(8,128)(2,1)} %param.15) | copy-start | bytes 294916
  8.7 32.8 %copy-start.22 = (bf16[864,12]{0,1:T(8,128)(2,1)S(1)}, bf16[864,12]{0,1:T(8,128)(2,1)}, u32[]{:S(2)}) copy-start(bf16[864,12]{0,1:T(8,128)(2,1)} %param.19) | copy-start | bytes 62212
  8.7 39.5 %copy-start.11 = (bf16[432,204]{0,1:T(8,128)(2,1)S(1)}, bf16[432,204]{0,1:T(8,128)(2,1)}, u32[]{:S(2)}) copy-start(bf16[432,204]{0,1:T(8,128)(2,1)} %param.23) | copy-start | bytes 528772
  8.7 149.9 %all-gather.12.cloned.1.call-start = ((), (), s32[]{:S(2)}) async-start(), calls=%async_computation.1 | async-start | bytes 6635520 | tf_op jit(solution)/shard_map/all_gather | solution.py:148
  9.5 50.5 %copy-start.23 = (bf16[192,36]{0,1:T(8,128)(2,1)S(1)}, bf16[192,36]{0,1:T(8,128)(2,1)}, u32[]{:S(2)}) copy-start(bf16[192,36]{0,1:T(8,128)(2,1)} %param.27) | copy-start | bytes 41476
  9.5 200.3 %all-gather.16.cloned.1.call-start = ((), (), s32[]{:S(2)}) async-start(), calls=%async_computation.3 | async-start | bytes 1720320 | tf_op jit(solution)/shard_map/all_gather | solution.py:139
  9.6 65.9 %collective-permute-start.8 = (bf16[2,8,192]{2,1,0:T(8,128)(2,1)S(1)}, bf16[2,8,192]{2,1,0:T(8,128)(2,1)S(1)}, u32[]{:S(2)}, u32[]{:S(2)}) collective-permute-start(bf16[2,8,192]{2,1,0:T(8,128)(2,1)S(1)} %get-tuple-element.80), channel_id=1, source_target_pairs={{0,4},{4,8},{8,12},{1,5},{5,9},{9,13},{2,6},{6,10},{10,14},{3,7},{... | collective-permute-start | bytes 18440 | tf_op jit(solution)/shard_map/ppermute | solution.py:14
  14.5 62.2 %collective-permute-start.9 = (bf16[2,8,192]{2,1,0:T(8,128)(2,1)S(1)}, bf16[2,8,192]{2,1,0:T(8,128)(2,1)S(1)}, u32[]{:S(2)}, u32[]{:S(2)}) collective-permute-start(bf16[2,8,192]{2,1,0:T(8,128)(2,1)S(1)} %get-tuple-element.79), channel_id=1, source_target_pairs={{4,0},{8,4},{12,8},{5,1},{9,5},{13,9},{6,2},{10,6},{14,10},{7,3},{... | collective-permute-start | bytes 18440 | tf_op jit(solution)/shard_map/ppermute | solution.py:17
  15.8 66.1 %collective-permute-start.4 = (bf16[2,16,96]{2,1,0:T(8,128)(2,1)S(1)}, bf16[2,16,96]{2,1,0:T(8,128)(2,1)S(1)}, u32[]{:S(2)}, u32[]{:S(2)}) collective-permute-start(bf16[2,16,96]{2,1,0:T(8,128)(2,1)S(1)} %get-tuple-element.67), channel_id=1, source_target_pairs={{0,4},{4,8},{8,12},{1,5},{5,9},{9,13},{2,6},{6,10},{10,14},{3,7},{... | collective-permute-start | bytes 18440 | tf_op jit(solution)/shard_map/ppermute | solution.py:14
  20.4 62.9 %collective-permute-start.5 = (bf16[2,16,96]{2,1,0:T(8,128)(2,1)S(1)}, bf16[2,16,96]{2,1,0:T(8,128)(2,1)S(1)}, u32[]{:S(2)}, u32[]{:S(2)}) collective-permute-start(bf16[2,16,96]{2,1,0:T(8,128)(2,1)S(1)} %get-tuple-element.66), channel_id=1, source_target_pairs={{4,0},{8,4},{12,8},{5,1},{9,5},{13,9},{6,2},{10,6},{14,10},{7,3},{... | collective-permute-start | bytes 18440 | tf_op jit(solution)/shard_map/ppermute | solution.py:17
  21.7 46.6 %copy-start.30 = (bf16[96,12]{0,1:T(8,128)(2,1)S(1)}, bf16[96,12]{0,1:T(8,128)(2,1)}, u32[]{:S(2)}) copy-start(bf16[96,12]{0,1:T(8,128)(2,1)} %param.26) | copy-start | bytes 6916
  21.7 68.6 %collective-permute-start.12 = (bf16[2,4,384]{2,1,0:T(4,128)(2,1)S(1)}, bf16[2,4,384]{2,1,0:T(4,128)(2,1)S(1)}, u32[]{:S(2)}, u32[]{:S(2)}) collective-permute-start(bf16[2,4,384]{2,1,0:T(4,128)(2,1)S(1)} %get-tuple-element.99), channel_id=1, source_target_pairs={{0,4},{4,8},{8,12},{1,5},{5,9},{9,13},{2,6},{6,10},{10,14},{3,7},{... | collective-permute-start | bytes 18440 | tf_op jit(solution)/shard_map/ppermute | solution.py:14
  75.1 33.8 %copy-start.12 = (bf16[48,864]{1,0:T(8,128)(2,1)}, bf16[48,864]{1,0:T(8,128)(2,1)S(1)}, u32[]{:S(2)}) copy-start(bf16[48,864]{1,0:T(8,128)(2,1)S(1)} %reshape.311) | copy-start | bytes 248836
  75.4 16.2 %collective-permute-start.13 = (bf16[2,4,384]{2,1,0:T(4,128)(2,1)S(1)}, bf16[2,4,384]{2,1,0:T(4,128)(2,1)S(1)}, u32[]{:S(2)}, u32[]{:S(2)}) collective-permute-start(bf16[2,4,384]{2,1,0:T(4,128)(2,1)S(1)} %get-tuple-element.98), channel_id=1, source_target_pairs={{4,0},{8,4},{12,8},{5,1},{9,5},{13,9},{6,2},{10,6},{14,10},{7,3},{... | collective-permute-start | bytes 18440 | tf_op jit(solution)/shard_map/ppermute | solution.py:17
  76.8 8.5 %collective-permute-start = (bf16[2,32,48]{2,1,0:T(8,128)(2,1)S(1)}, bf16[2,32,48]{2,1,0:T(8,128)(2,1)S(1)}, u32[]{:S(2)}, u32[]{:S(2)}) collective-permute-start(bf16[2,32,48]{2,1,0:T(8,128)(2,1)S(1)} %get-tuple-element.30), channel_id=1, source_target_pairs={{0,4},{4,8},{8,12},{1,5},{5,9},{9,13},{2,6},{6,10},{10,14},{3,7},{... | collective-permute-start | bytes 18440 | tf_op jit(solution)/shard_map/ppermute | solution.py:14
  82.0 6.9 %collective-permute-start.1 = (bf16[2,32,48]{2,1,0:T(8,128)(2,1)S(1)}, bf16[2,32,48]{2,1,0:T(8,128)(2,1)S(1)}, u32[]{:S(2)}, u32[]{:S(2)}) collective-permute-start(bf16[2,32,48]{2,1,0:T(8,128)(2,1)S(1)} %get-tuple-element.29), channel_id=1, source_target_pairs={{4,0},{8,4},{12,8},{5,1},{9,5},{13,9},{6,2},{10,6},{14,10},{7,3},{... | collective-permute-start | bytes 18440 | tf_op jit(solution)/shard_map/ppermute | solution.py:17
  83.3 45.1 %collective-permute-start.11 = (bf16[12,2,192]{2,1,0:T(2,128)(2,1)}, bf16[12,2,192]{2,1,0:T(2,128)(2,1)}, u32[]{:S(2)}, u32[]{:S(2)}) collective-permute-start(bf16[12,2,192]{2,1,0:T(2,128)(2,1)} %get-tuple-element.77), channel_id=1, source_target_pairs={{1,0},{2,1},{3,2},{5,4},{6,5},{7,6},{9,8},{10,9},{11,10},{13,12},{... | collective-permute-start | bytes 27656 | tf_op jit(solution)/shard_map/ppermute | solution.py:17
  84.6 15.8 %copy-start.4 = (bf16[20,16,96]{2,1,0:T(8,128)(2,1)}, bf16[20,16,96]{2,1,0:T(8,128)(2,1)S(1)}, u32[]{:S(2)}) copy-start(bf16[20,16,96]{2,1,0:T(8,128)(2,1)S(1)} %constant_dynamic-update-slice_fusion.3) | copy-start | bytes 184324
  85.3 43.2 %collective-permute-start.10 = (bf16[12,2,192]{2,1,0:T(2,128)(2,1)}, bf16[12,2,192]{2,1,0:T(2,128)(2,1)}, u32[]{:S(2)}, u32[]{:S(2)}) collective-permute-start(bf16[12,2,192]{2,1,0:T(2,128)(2,1)} %get-tuple-element.78), channel_id=1, source_target_pairs={{0,1},{1,2},{2,3},{4,5},{5,6},{6,7},{8,9},{9,10},{10,11},{12,13},{... | collective-permute-start | bytes 27656 | tf_op jit(solution)/shard_map/ppermute | solution.py:14
  88.9 25.5 %collective-permute-start.7 = (bf16[20,2,96]{2,1,0:T(2,128)(2,1)}, bf16[20,2,96]{2,1,0:T(2,128)(2,1)}, u32[]{:S(2)}, u32[]{:S(2)}) collective-permute-start(bf16[20,2,96]{2,1,0:T(2,128)(2,1)} %get-tuple-element.55), channel_id=1, source_target_pairs={{1,0},{2,1},{3,2},{5,4},{6,5},{7,6},{9,8},{10,9},{11,10},{13,12},{... | collective-permute-start | bytes 23048 | tf_op jit(solution)/shard_map/ppermute | solution.py:17
  90.3 5.8 %collective-permute-start.3 = (bf16[36,2,48]{2,1,0:T(2,128)(2,1)S(1)}, bf16[36,2,48]{2,1,0:T(2,128)(2,1)S(1)}, u32[]{:S(2)}, u32[]{:S(2)}) collective-permute-start(bf16[36,2,48]{2,1,0:T(2,128)(2,1)S(1)} %get-tuple-element.25), channel_id=1, source_target_pairs={{1,0},{2,1},{3,2},{5,4},{6,5},{7,6},{9,8},{10,9},{11,10},{13,12},{... | collective-permute-start | bytes 20744 | tf_op jit(solution)/shard_map/ppermute | solution.py:17
  91.6 8.7 %collective-permute-start.2 = (bf16[36,2,48]{2,1,0:T(2,128)(2,1)S(1)}, bf16[36,2,48]{2,1,0:T(2,128)(2,1)S(1)}, u32[]{:S(2)}, u32[]{:S(2)}) collective-permute-start(bf16[36,2,48]{2,1,0:T(2,128)(2,1)S(1)} %get-tuple-element.26), channel_id=1, source_target_pairs={{0,1},{1,2},{2,3},{4,5},{5,6},{6,7},{8,9},{9,10},{10,11},{12,13},{... | collective-permute-start | bytes 20744 | tf_op jit(solution)/shard_map/ppermute | solution.py:14
  96.2 19.6 %collective-permute-start.6 = (bf16[20,2,96]{2,1,0:T(2,128)(2,1)}, bf16[20,2,96]{2,1,0:T(2,128)(2,1)}, u32[]{:S(2)}, u32[]{:S(2)}) collective-permute-start(bf16[20,2,96]{2,1,0:T(2,128)(2,1)} %get-tuple-element.56), channel_id=1, source_target_pairs={{0,1},{1,2},{2,3},{4,5},{5,6},{6,7},{8,9},{9,10},{10,11},{12,13},{... | collective-permute-start | bytes 23048 | tf_op jit(solution)/shard_map/ppermute | solution.py:14
  100.4 33.4 %collective-permute-start.14 = (bf16[8,2,384]{2,1,0:T(2,128)(2,1)}, bf16[8,2,384]{2,1,0:T(2,128)(2,1)}, u32[]{:S(2)}, u32[]{:S(2)}) collective-permute-start(bf16[8,2,384]{2,1,0:T(2,128)(2,1)} %get-tuple-element.82), channel_id=1, source_target_pairs={{0,1},{1,2},{2,3},{4,5},{5,6},{6,7},{8,9},{9,10},{10,11},{12,13},{... | collective-permute-start | bytes 36872 | tf_op jit(solution)/shard_map/ppermute | solution.py:14
  104.3 4.5 %copy-start.26 = (pred[34,34]{1,0:T(8,128)(4,1)S(1)}, pred[34,34]{1,0:T(8,128)(4,1)}, u32[]{:S(2)}) copy-start(pred[34,34]{1,0:T(8,128)(4,1)} %broadcast_and_fusion) | copy-start | bytes 3472
  104.3 4.5 %copy-start.44 = (f32[48]{0:T(128)S(1)}, f32[48]{0:T(128)}, u32[]{:S(2)}) copy-start(f32[48]{0:T(128)} %get-tuple-element.91) | copy-start | bytes 580
  114.4 20.1 %collective-permute-start.15 = (bf16[8,2,384]{2,1,0:T(2,128)(2,1)}, bf16[8,2,384]{2,1,0:T(2,128)(2,1)S(1)}, u32[]{:S(2)}, u32[]{:S(2)}) collective-permute-start(bf16[8,2,384]{2,1,0:T(2,128)(2,1)} %get-tuple-element.81), channel_id=1, source_target_pairs={{1,0},{2,1},{3,2},{5,4},{6,5},{7,6},{9,8},{10,9},{11,10},{13,12},{... | collective-permute-start | bytes 36872 | tf_op jit(solution)/shard_map/ppermute | solution.py:17
  116.7 3.7 %copy-start.3 = (bf16[1728,96]{0,1:T(8,128)(2,1)S(1)}, bf16[1728,96]{0,1:T(8,128)(2,1)}, u32[]{:S(2)}) copy-start(bf16[1728,96]{0,1:T(8,128)(2,1)} %all_gather.31) | copy-start | bytes 995332
  120.8 6.3 %copy-start.18 = (bf16[48,96,1]{1,0,2:T(8,128)(2,1)S(1)}, bf16[48,96,1]{1,0,2:T(8,128)(2,1)}, u32[]{:S(2)}) copy-start(bf16[48,96,1]{1,0,2:T(8,128)(2,1)} %reshape.324) | copy-start | bytes 27652
  120.8 6.3 %copy-start.34 = (f32[48]{0:T(128)S(1)}, f32[48]{0:T(128)}, u32[]{:S(2)}) copy-start(f32[48]{0:T(128)} %get-tuple-element.89) | copy-start | bytes 580
  120.9 7.5 %copy-start.6 = (bf16[12,8,192]{2,1,0:T(8,128)(2,1)S(1)}, bf16[12,8,192]{2,1,0:T(8,128)(2,1)}, u32[]{:S(2)}) copy-start(bf16[12,8,192]{2,1,0:T(8,128)(2,1)} %copy-done.5) | copy-start | bytes 110596
  122.6 8.0 %collective-permute-start.20 = (bf16[1,16,96]{2,1,0:T(8,128)(2,1)}, bf16[1,16,96]{2,1,0:T(8,128)(2,1)S(1)}, u32[]{:S(2)}, u32[]{:S(2)}) collective-permute-start(bf16[1,16,96]{2,1,0:T(8,128)(2,1)} %slice.962), channel_id=1, source_target_pairs={{0,4},{4,8},{8,12},{1,5},{5,9},{9,13},{2,6},{6,10},{10,14},{3,7},{... | collective-permute-start | bytes 9224 | tf_op jit(solution)/shard_map/ppermute | solution.py:29
  130.6 7.3 %copy-start.25 = (f32[288]{0:T(512)S(1)}, f32[288]{0:T(512)}, u32[]{:S(2)}) copy-start(f32[288]{0:T(512)} %slice.796) | copy-start | bytes 3460
  130.6 16.7 %copy-start.38 = (pred[10,10]{1,0:T(8,128)(4,1)S(1)}, pred[10,10]{1,0:T(8,128)(4,1)}, u32[]{:S(2)}) copy-start(pred[10,10]{1,0:T(8,128)(4,1)} %broadcast_and_fusion.2) | copy-start | bytes 304
  130.6 16.7 %copy-start.42 = (f32[192]{0:T(256)S(1)}, f32[192]{0:T(256)}, u32[]{:S(2)}) copy-start(f32[192]{0:T(256)} %get-tuple-element.95) | copy-start | bytes 2308
  131.1 5.9 %collective-permute-start.21 = (bf16[17,1,96]{2,1,0:T(2,128)(2,1)S(1)}, bf16[17,1,96]{2,1,0:T(2,128)(2,1)S(1)}, u32[]{:S(2)}, u32[]{:S(2)}) collective-permute-start(bf16[17,1,96]{2,1,0:T(2,128)(2,1)S(1)} %fusion.81), channel_id=1, source_target_pairs={{0,1},{1,2},{2,3},{4,5},{5,6},{6,7},{8,9},{9,10},{10,11},{12,13},{... | collective-permute-start | bytes 9800 | tf_op jit(solution)/shard_map/ppermute | solution.py:29
  139.4 4.4 %collective-permute-start.26 = (bf16[1,8,96]{2,1,0:T(8,128)(2,1)S(1)}, bf16[1,8,96]{2,1,0:T(8,128)(2,1)S(1)}, u32[]{:S(2)}, u32[]{:S(2)}) collective-permute-start(bf16[1,8,96]{2,1,0:T(8,128)(2,1)S(1)} %slice.978), channel_id=1, source_target_pairs={{0,4},{4,8},{8,12},{1,5},{5,9},{9,13},{2,6},{6,10},{10,14},{3,7},{... | collective-permute-start | bytes 4616 | tf_op jit(solution)/shard_map/ppermute | solution.py:29
  143.8 2.9 %collective-permute-start.27 = (bf16[9,1,96]{2,1,0:T(2,128)(2,1)S(1)}, bf16[9,1,96]{2,1,0:T(2,128)(2,1)S(1)}, u32[]{:S(2)}, u32[]{:S(2)}) collective-permute-start(bf16[9,1,96]{2,1,0:T(2,128)(2,1)S(1)} %fusion.83), channel_id=1, source_target_pairs={{0,1},{1,2},{2,3},{4,5},{5,6},{6,7},{8,9},{9,10},{10,11},{12,13},{... | collective-permute-start | bytes 5192 | tf_op jit(solution)/shard_map/ppermute | solution.py:29
  148.9 5.9 %copy-start.9 = (bf16[144,192,1]{1,0,2:T(8,128)(2,1)S(1)}, bf16[144,192,1]{1,0,2:T(8,128)(2,1)}, u32[]{:S(2)}) copy-start(bf16[144,192,1]{1,0,2:T(8,128)(2,1)} %reshape.327) | copy-start | bytes 165892
  148.9 5.9 %copy-start.27 = (f32[144]{0:T(256)S(1)}, f32[144]{0:T(256)}, u32[]{:S(2)}) copy-start(f32[144]{0:T(256)} %slice.724) | copy-start | bytes 1732
  148.9 9.8 %copy-start.37 = (f32[384]{0:T(512)S(1)}, f32[384]{0:T(512)}, u32[]{:S(2)}) copy-start(f32[384]{0:T(512)} %get-tuple-element.86) | copy-start | bytes 4612
  148.9 9.8 %copy-start.40 = (pred[6,6]{1,0:T(8,128)(4,1)S(1)}, pred[6,6]{1,0:T(8,128)(4,1)}, u32[]{:S(2)}) copy-start(pred[6,6]{1,0:T(8,128)(4,1)} %broadcast_and_fusion.3) | copy-start | bytes 112
  150.7 5.4 %collective-permute-start.28 = (bf16[1,8,192]{2,1,0:T(8,128)(2,1)S(1)}, bf16[1,8,192]{2,1,0:T(8,128)(2,1)S(1)}, u32[]{:S(2)}, u32[]{:S(2)}) collective-permute-start(bf16[1,8,192]{2,1,0:T(8,128)(2,1)S(1)} %slice.982), channel_id=1, source_target_pairs={{0,4},{4,8},{8,12},{1,5},{5,9},{9,13},{2,6},{6,10},{10,14},{3,7},{... | collective-permute-start | bytes 9224 | tf_op jit(solution)/shard_map/ppermute | solution.py:29
  154.9 6.5 %copy-start.10 = (f32[8,8,144]{2,1,0:T(8,128)}, f32[8,8,144]{2,1,0:T(8,128)S(1)}, u32[]{:S(2)}) copy-start(f32[8,8,144]{2,1,0:T(8,128)S(1)} %convolution_add_fusion.9) | copy-start | bytes 110596
  156.4 13.9 %collective-permute-start.29 = (bf16[9,1,192]{2,1,0:T(2,128)(2,1)S(1)}, bf16[9,1,192]{2,1,0:T(2,128)(2,1)S(1)}, u32[]{:S(2)}, u32[]{:S(2)}) collective-permute-start(bf16[9,1,192]{2,1,0:T(2,128)(2,1)S(1)} %fusion.79), channel_id=1, source_target_pairs={{0,1},{1,2},{2,3},{4,5},{5,6},{6,7},{8,9},{9,10},{10,11},{12,13},{... | collective-permute-start | bytes 10376 | tf_op jit(solution)/shard_map/ppermute | solution.py:29
  166.6 6.7 %collective-permute-start.16 = (bf16[1,32,48]{2,1,0:T(8,128)(2,1)S(1)}, bf16[1,32,48]{2,1,0:T(8,128)(2,1)S(1)}, u32[]{:S(2)}, u32[]{:S(2)}) collective-permute-start(bf16[1,32,48]{2,1,0:T(8,128)(2,1)S(1)} %slice.950), channel_id=1, source_target_pairs={{0,4},{4,8},{8,12},{1,5},{5,9},{9,13},{2,6},{6,10},{10,14},{3,7},{... | collective-permute-start | bytes 9224 | tf_op jit(solution)/shard_map/ppermute | solution.py:29
  173.4 7.8 %copy-start.29 = (f32[192]{0:T(256)S(1)}, f32[192]{0:T(256)}, u32[]{:S(2)}) copy-start(f32[192]{0:T(256)} %get-tuple-element.93) | copy-start | bytes 2308
  173.4 6.0 %collective-permute-start.17 = (bf16[33,1,48]{2,1,0:T(2,128)(2,1)S(1)}, bf16[33,1,48]{2,1,0:T(2,128)(2,1)S(1)}, u32[]{:S(2)}, u32[]{:S(2)}) collective-permute-start(bf16[33,1,48]{2,1,0:T(2,128)(2,1)S(1)} %fusion.78), channel_id=1, source_target_pairs={{0,1},{1,2},{2,3},{4,5},{5,6},{6,7},{8,9},{9,10},{10,11},{12,13},{... | collective-permute-start | bytes 9512 | tf_op jit(solution)/shard_map/ppermute | solution.py:29
  181.6 18.2 %copy-start.32 = (f32[48]{0:T(128)S(1)}, f32[48]{0:T(128)}, u32[]{:S(2)}) copy-start(f32[48]{0:T(128)} %get-tuple-element.88) | copy-start | bytes 580
  181.6 8.9 %collective-permute-start.18 = (bf16[1,16,48]{2,1,0:T(8,128)(2,1)S(1)}, bf16[1,16,48]{2,1,0:T(8,128)(2,1)S(1)}, u32[]{:S(2)}, u32[]{:S(2)}) collective-permute-start(bf16[1,16,48]{2,1,0:T(8,128)(2,1)S(1)} %slice.958), channel_id=1, source_target_pairs={{0,4},{4,8},{8,12},{1,5},{5,9},{9,13},{2,6},{6,10},{10,14},{3,7},{... | collective-permute-start | bytes 4616 | tf_op jit(solution)/shard_map/ppermute | solution.py:29
  185.3 17.0 %copy-start.28 = (f32[192]{0:T(256)S(1)}, f32[192]{0:T(256)}, u32[]{:S(2)}) copy-start(f32[192]{0:T(256)} %get-tuple-element.92) | copy-start | bytes 2308
  188.2 4.2 %collective-permute-start.22 = (bf16[1,16,48]{2,1,0:T(8,128)(2,1)S(1)}, bf16[1,16,48]{2,1,0:T(8,128)(2,1)S(1)}, u32[]{:S(2)}, u32[]{:S(2)}) collective-permute-start(bf16[1,16,48]{2,1,0:T(8,128)(2,1)S(1)} %slice.969), channel_id=1, source_target_pairs={{0,4},{4,8},{8,12},{1,5},{5,9},{9,13},{2,6},{6,10},{10,14},{3,7},{... | collective-permute-start | bytes 4616 | tf_op jit(solution)/shard_map/ppermute | solution.py:29
  190.5 17.8 %copy-start.35 = (f32[384]{0:T(512)S(1)}, f32[384]{0:T(512)}, u32[]{:S(2)}) copy-start(f32[384]{0:T(512)} %get-tuple-element.87) | copy-start | bytes 4612
  190.5 7.5 %collective-permute-start.19 = (bf16[17,1,48]{2,1,0:T(2,128)(2,1)S(1)}, bf16[17,1,48]{2,1,0:T(2,128)(2,1)S(1)}, u32[]{:S(2)}, u32[]{:S(2)}) collective-permute-start(bf16[17,1,48]{2,1,0:T(2,128)(2,1)S(1)} %fusion.82), channel_id=1, source_target_pairs={{0,1},{1,2},{2,3},{4,5},{5,6},{6,7},{8,9},{9,10},{10,11},{12,13},{... | collective-permute-start | bytes 4904 | tf_op jit(solution)/shard_map/ppermute | solution.py:29
  193.3 5.5 %collective-permute-start.23 = (bf16[17,1,48]{2,1,0:T(2,128)(2,1)S(1)}, bf16[17,1,48]{2,1,0:T(2,128)(2,1)S(1)}, u32[]{:S(2)}, u32[]{:S(2)}) collective-permute-start(bf16[17,1,48]{2,1,0:T(2,128)(2,1)S(1)} %fusion.80), channel_id=1, source_target_pairs={{0,1},{1,2},{2,3},{4,5},{5,6},{6,7},{8,9},{9,10},{10,11},{12,13},{... | collective-permute-start | bytes 4904 | tf_op jit(solution)/shard_map/ppermute | solution.py:29
  200.0 3.8 %collective-permute-start.24 = (bf16[1,8,48]{2,1,0:T(8,128)(2,1)S(1)}, bf16[1,8,48]{2,1,0:T(8,128)(2,1)S(1)}, u32[]{:S(2)}, u32[]{:S(2)}) collective-permute-start(bf16[1,8,48]{2,1,0:T(8,128)(2,1)S(1)} %slice.973), channel_id=1, source_target_pairs={{0,4},{4,8},{8,12},{1,5},{5,9},{9,13},{2,6},{6,10},{10,14},{3,7},{... | collective-permute-start | bytes 2312 | tf_op jit(solution)/shard_map/ppermute | solution.py:29
  203.8 3.7 %collective-permute-start.25 = (bf16[9,1,48]{2,1,0:T(2,128)(2,1)S(1)}, bf16[9,1,48]{2,1,0:T(2,128)(2,1)S(1)}, u32[]{:S(2)}, u32[]{:S(2)}) collective-permute-start(bf16[9,1,48]{2,1,0:T(2,128)(2,1)S(1)} %fusion.84), channel_id=1, source_target_pairs={{0,1},{1,2},{2,3},{4,5},{5,6},{6,7},{8,9},{9,10},{10,11},{12,13},{... | collective-permute-start | bytes 2600 | tf_op jit(solution)/shard_map/ppermute | solution.py:29
  (16 other events, 32.5 us)
Sparse Core Ops, SparseCore 0:
  9.6 20.2 all-gather.13
  31.5 18.8 all-gather.9
  51.9 41.4 all-gather.11
  94.8 18.0 all-gather.15
where the time goes:
time: 223 us; the launch traced here: 219 us
  starting transfers between devices  88.5 us (40%)
  blocking collectives  39.4 us (18%)
  local copies, waits for them, and re-layouts  37.9 us (17%)
  matrix products  19.3 us (9%)
  between operations  15.8 us (7%)
  other arithmetic  13.5 us (6%)
  waiting for transfers between devices  4.3 us (2%)
    ppermute x14, starting transfers between devices, passed_along(): return lax.ppermute(block, axis, route)  45.3 us
    ppermute x8, starting transfers between devices, extended_2(): lax.ppermute(lax.slice_in_dim(block, block.shape[dim] - width, None, axis...  32.7 us
    dot_general x15, matrix products, patch_conv(): jnp.dot(flat, weight, preferred_element_type=jnp.float32)  18.8 us
    slice x66, local copies, waits for them, and re-layouts, patch_conv(): lax.slice(extended, (row_tap, col_tap, 0), (row_tap + stride * (height -...  15.9 us
    concatenate x14, local copies, waits for them, and re-layouts, patch_conv(): stacked = jnp.concatenate(taps, axis=2)  10.5 us
    ppermute x8, starting transfers between devices, extended_2(): lax.ppermute(lax.slice_in_dim(block, 0, width, axis=dim), axis, backward)  10.3 us
    all_gather x1, blocking collectives, on_device(): lax.all_gather(down_one, 'cols', axis=1, tiled=True)  9.12 us
    concatenate x7, other arithmetic, extended_2(): block = jnp.concatenate([low, block, high], axis=dim)  7.15 us
  transfers between devices with their start and end apart: 34, of which 4 were waited for; matrix products, arithmetic and copies ran while one was open for 31% of the time, Pallas kernels for 0%

commit v1 on v0

v1 whole, which is shorter than its diff:
```python
import functools

import jax
import jax.numpy as jnp
from jax import lax
from jax.experimental import pallas as pl
from jax.experimental.pallas import tpu as pltpu
from jax.sharding import PartitionSpec as P

F32 = jnp.float32
BF16 = jnp.bfloat16
LANES = 128
BEFORE = (9, 5, 3, 2)
AFTER = 2


def up_to(value, multiple):
    return -(-value // multiple) * multiple


def dot(a, b):
    return jnp.dot(a.astype(BF16), b.astype(BF16), preferred_element_type=F32)


def iota(shape, dim):
    return lax.broadcasted_iota(jnp.int32, shape, dim)


def onehot(condition):
    return jnp.where(condition, 1.0, 0.0).astype(F32).astype(BF16)


def taps(ref, height, breadth, stride, row, col, weight_of, lanes=None):
    total = None
    for r in range(3):
        for q in range(3):
            rows = pl.ds(row + r, height, stride=stride) if stride > 1 else pl.ds(row + r, height)
            cols = pl.ds(col + q, breadth, stride=stride) if stride > 1 else pl.ds(col + q, breadth)
            if stride > 1:
                block = wide_load(ref, rows, cols)[:, :, lanes[0] : lanes[1]]
            else:
                block = ref[rows, cols, :]
            flat = block.reshape(height * breadth, block.shape[2])
            part = dot(flat, weight_of(3 * r + q))
            total = part if total is None else total + part
    return total


def wide_load(refs, rows, cols):
    parts = [ref[rows, cols, :] for ref in refs]
    return parts[0] if len(parts) == 1 else jnp.concatenate(parts, axis=2)


def wide_store(refs, rows, cols, value):
    channels = value.shape[2]
    for i, ref in enumerate(refs):
        part = value[:, :, i * LANES : min((i + 1) * LANES, channels)]
        if part.shape[2] < LANES:
            rest = jnp.zeros(part.shape[:2] + (LANES - part.shape[2],), part.dtype)
            part = jnp.concatenate([part, rest], axis=2)
        ref[rows, cols, :] = part


def inside(shape, row_first, row_count, col_first, col_count):
    rows = iota(shape, 0) + row_first
    cols = iota(shape, 1) + col_first
    return (rows >= 0) & (rows < row_count) & (cols >= 0) & (cols < col_count)


def rounded(value):
    return value.astype(BF16).astype(F32)


def vmem(count):
    return [pl.BlockSpec(memory_space=pltpu.VMEM)] * count


PARAMS = pltpu.CompilerParams(vmem_limit_bytes=56 * 1024 * 1024)


class RowLayout:
    def __init__(self, shapes, counts):
        self.counts = counts
        self.half = shapes[0][1] // 2
        self.start = []
        at = 0
        for level, ((_, breadth, channels), count) in enumerate(zip(shapes, counts)):
            self.start.append(at)
            positions = count * (self.half if level == 0 else breadth)
            at += positions * (1 if level == 0 else -(-channels // LANES))
        self.total = up_to(at, 16)


def pack_rows(layout, refs, firsts, scratch):
    one, two, three, four = refs
    count = layout.counts
    half = layout.half
    for part in range(2):
        block = one[firsts[0] : firsts[0] + count[0], part * half : (part + 1) * half, :]
        size = count[0] * half
        scratch[0:size, part * 64 : part * 64 + one.shape[2]] = block.astype(F32).reshape(size, -1)
    at = layout.start[1]
    size = count[1] * two.shape[1]
    block = two[firsts[1] : firsts[1] + count[1], :, :].astype(F32).reshape(size, two.shape[2])
    scratch[at : at + size, 0 : two.shape[2]] = block
    at = layout.start[2]
    size = count[2] * three.shape[1]
    block = three[firsts[2] : firsts[2] + count[2], :, :].astype(F32).reshape(size, three.shape[2])
    for low in range(0, three.shape[2], LANES):
        high = min(low + LANES, three.shape[2])
        scratch[at : at + size, 0 : high - low] = block[:, low:high]
        at += size
    breadth = four.shape[1]
    size = count[3] * breadth
    for row in range(count[3]):
        block = four[firsts[3] + row].astype(F32)
        at = layout.start[3] + row * breadth
        for low in range(0, four.shape[2], LANES):
            scratch[at : at + breadth, 0:LANES] = block[:, low : low + LANES]
            at += size


def rows_kernel(layouts, one, two, three, four, down_ref, up_ref, scratch):
    refs = (one, two, three, four)
    low, high = layouts
    firsts = tuple(ref.shape[0] - count for ref, count in zip(refs, low.counts))
    scratch[...] = jnp.zeros_like(scratch)
    pack_rows(low, refs, firsts, scratch)
    down_ref[...] = scratch[0 : low.total, :].astype(BF16)
    pack_rows(high, refs, (0, 0, 0, 0), scratch)
    up_ref[...] = scratch[0 : high.total, :].astype(BF16)


def stretch_fine(level, layout_pair, feat, top, bottom, target, col):
    low, high = layout_pair
    height, breadth, channels = feat.shape
    before, after = low.counts[level], high.counts[level]
    for layout, message, row, count in (
        (low, top, 0, before),
        (high, bottom, before + height, after),
    ):
        at = layout.start[level]
        if level == 0:
            half = layout.half
            for part in range(2):
                block = message[at : at + count * half, part * 64 : part * 64 + channels]
                target[row : row + count, col + part * half : col + (part + 1) * half, :] = (
                    block.astype(F32).reshape(count, half, channels)
                )
        else:
            block = message[at : at + count * breadth, 0:channels]
            target[row : row + count, col : col + breadth, :] = block.astype(F32).reshape(
                count, breadth, channels
            )
    target[before : before + height, col : col + breadth, :] = feat[...].astype(F32)


def columns_kernel(layouts, one, two, three, four, top, bottom, gather_ref, right_ref, left_ref,
                   full_one, full_two, full_three, message, edge):
    low, high = layouts
    breadth, channels = three.shape[1], three.shape[2]
    own = three.shape[0] * breadth
    before, after = low.counts[2] * breadth, high.counts[2] * breadth
    for layout, source, row, size in ((low, top, 0, before), (high, bottom, before + own, after)):
        at = layout.start[2]
        for first in range(0, channels, LANES):
            last = min(first + LANES, channels)
            full_three[row : row + size, first:last] = source[at : at + size, 0 : last - first].astype(F32)
            at += size
    full_three[before : before + own, :] = three[...].astype(F32).reshape(own, channels)
    size_four = gather_four(four.shape)
    breadth, channels4 = four.shape[1], four.shape[2]
    before, after = low.counts[3] * breadth, high.counts[3] * breadth
    for layout, source, row, size in (
        (low, top, 0, before),
        (high, bottom, before + four.shape[0] * breadth, after),
    ):
        at = layout.start[3]
        for first in range(0, channels4, LANES):
            message[row : row + size, first : first + LANES] = source[at : at + size, :].astype(F32)
            at += size
    for row in range(four.shape[0]):
        at = before + row * breadth
        message[at : at + breadth, 0:channels4] = four[row].astype(F32)
    total, head = gather_three(three.shape)
    message[size_four : size_four + head, 0:channels] = full_three[0:head, :]
    message[size_four : size_four + total - head, channels : 2 * channels] = full_three[head:total, :]
    gather_ref[...] = message[...].astype(BF16)
    stretch_fine(0, layouts, one, top, bottom, full_one, 0)
    stretch_fine(1, layouts, two, top, bottom, full_two, 0)
    wide, wide_two = one.shape[1], two.shape[1]
    left, left_two = BEFORE[0], BEFORE[1]
    rows, rows_two = full_one.shape[0], full_two.shape[0]
    edge[:, 0:left, 0 : one.shape[2]] = full_one[:, wide - left : wide, :]
    edge[0:rows_two, left : left + left_two, 0 : two.shape[2]] = full_two[
        :, wide_two - left_two : wide_two, :
    ]
    right_ref[...] = edge[...].astype(BF16)
    edge[:, 0:AFTER, 0 : one.shape[2]] = full_one[:, 0:AFTER, :]
    edge[0:rows_two, AFTER : 2 * AFTER, 0 : two.shape[2]] = full_two[:, 0:AFTER, :]
    left_ref[...] = edge[:, 0:8, :].astype(BF16)


def gather_four(shape):
    return (shape[0] + BEFORE[3] + AFTER) * shape[1]


def gather_three(shape):
    total = (shape[0] + BEFORE[2] + AFTER) * shape[1]
    return total, up_to(-(-total // 2), 8)


def own_channels(me, channels, own):
    return onehot(iota((channels, own), 0) == iota((channels, own), 1) + me * own)


def own_bias(bias_ref, first, channels, me, own):
    row = jnp.broadcast_to(bias_ref[0:1, first : first + channels], (8, channels))
    pick = jnp.where(iota((channels, own), 0) == iota((channels, own), 1) + me * own, 1.0, 0.0)
    return jnp.dot(row, pick.astype(F32), precision=lax.Precision.HIGHEST, preferred_element_type=F32)[0:1]


def spread(target, blocks, me, rows, block_cols):
    shift = block_cols.bit_length() - 1
    width = target.shape[1]
    total = None
    for k, block in enumerate(blocks):
        size = block.shape[0]
        shape = (rows, width, size)
        source = iota(shape, 2)
        slot = (me ^ k) * block_cols + 1 + (source & (block_cols - 1))
        choose = ((source >> shift) == iota(shape, 0)) & (iota(shape, 1) == slot)
        part = dot(onehot(choose).reshape(rows * width, size), block)
        total = part if total is None else total + part
    target[...] = total.reshape(rows, width, total.shape[1])


def coarse_first_kernel(sizes, index, *refs):
    count, high3, wide3, chan3, high4, wide4, chan4, bias3, bias4 = sizes
    blocks = refs[:count]
    conv3, conv4, bias, out, res3, res4, full3, full4, message = refs[count:]
    row, me = index[0], index[1]
    size4 = gather_four((high4, wide4))
    total3, head = gather_three((high3, wide3))
    spread(full4, [b[0:size4, 0:chan4] for b in blocks], me, high4 + BEFORE[3] + AFTER, wide4)
    parts = []
    for b in blocks:
        parts.append(
            jnp.concatenate(
                [
                    b[size4 : size4 + head, 0:chan3].astype(F32),
                    b[size4 : size4 + total3 - head, chan3 : 2 * chan3].astype(F32),
                ],
                axis=0,
            )
        )
    spread(full3, parts, me, high3 + BEFORE[2] + AFTER, wide3)
    heights = []
    for full, conv, high, wide, chan, before, base in (
        (full3, conv3, high3, wide3, chan3, BEFORE[2], bias3),
        (full4, conv4, high4, wide4, chan4, BEFORE[3], bias4),
    ):
        own = chan // count
        out_high = high + before + AFTER - 2
        out_wide = wide * count
        mid = taps(full, out_high, out_wide, 1, 0, 0, lambda t: conv[t * chan : (t + 1) * chan, :])
        mid = jax.nn.relu(mid + own_bias(bias, base, chan, me, own)).reshape(out_high, out_wide, own)
        rows = iota(mid.shape, 0) + row * high - (before - 1)
        valid = (rows >= 0) & (rows < index[2] * high)
        heights.append(jnp.where(valid, mid, 0.0).reshape(out_high * out_wide, own))
    mid3, mid4 = heights
    half = mid3.shape[0] // 2
    own3, own4 = mid3.shape[1], mid4.shape[1]
    message[0:half, 0:own3] = mid3[0:half]
    message[0:half, 64 : 64 + own3] = mid3[half:]
    message[half : half + mid4.shape[0], 0:own4] = mid4
    out[...] = message[...].astype(BF16)
    skip3 = BEFORE[2] - 1
    keep = full3[skip3 : skip3 + high3 + 1, 1 : 1 + wide3 * count, :].reshape(-1, chan3)
    res3[...] = dot(keep, own_channels(me, chan3, own3)).astype(BF16)
    keep = full4[BEFORE[3] : BEFORE[3] + high4, 1 : 1 + wide4 * count, :].reshape(-1, chan4)
    res4[...] = dot(keep, own_channels(me, chan4, own4)).astype(BF16)


def natural(blocks, me, own, channels):
    total = None
    for k, block in enumerate(blocks):
        place = onehot(iota((own, channels), 1) == iota((own, channels), 0) + (me ^ k) * own)
        part = dot(block, place)
        total = part if total is None else total + part
    return total


def message_rows(sizes):
    count, high3, wide3, chan3, high4, wide4, chan4, _, _ = sizes
    half = (high3 + BEFORE[2] + AFTER - 2) * wide3 * count // 2
    return half, half + (high4 + BEFORE[3] + AFTER - 2) * wide4 * count


def coarse_second_kernel(sizes, index, *refs):
    count, high3, wide3, chan3, high4, wide4, chan4, bias3, bias4 = sizes
    blocks = refs[:count]
    res3, res4, conv3, conv4, bias = refs[count : count + 5]
    outs = refs[count + 5 : 2 * count + 5]
    full3, full4, message = refs[2 * count + 5 :]
    row, me = index[0], index[1]
    own3, own4 = chan3 // count, chan4 // count
    half, last = message_rows(sizes)
    mids3 = [
        jnp.concatenate([b[0:half, 0:own3].astype(F32), b[0:half, 64 : 64 + own3].astype(F32)], axis=0)
        for b in blocks
    ]
    mids4 = [b[half:last, 0:own4] for b in blocks]
    results = []
    for full, mids, conv, res, high, wide, chan, before, base, extra in (
        (full3, mids3, conv3, res3, high3, wide3, chan3, BEFORE[2], bias3, 1),
        (full4, mids4, conv4, res4, high4, wide4, chan4, BEFORE[3], bias4, 0),
    ):
        own = chan // count
        mid_high = high + before + AFTER - 2
        out_wide = wide * count
        full[...] = jnp.zeros_like(full)
        full[:, 1 : 1 + out_wide, :] = natural(mids, me, own, chan).reshape(mid_high, out_wide, chan)
        out_high = high + extra
        first = 9 * chan
        y = taps(
            full, out_high, out_wide, 1, 0, 0,
            lambda t: conv[first + t * chan : first + (t + 1) * chan, :],
        )
        y = y + own_bias(bias, base + chan, chan, me, own) + res[...].astype(F32)
        y = jax.nn.relu(y).reshape(out_high, out_wide, own)
        rows = iota(y.shape, 0) + row * high - extra
        y = jnp.where((rows >= 0) & (rows < index[2] * high), y, 0.0)
        results.append(y.reshape(out_high * out_wide, own))
    y3, y4 = results
    for k, out in enumerate(outs):
        target = me ^ k
        wide = wide3 * count
        shape = (high3 + 1, 16, y3.shape[0])
        source = iota(shape, 2)
        slot = iota(shape, 1)
        choose = (
            ((source >> (wide.bit_length() - 1)) == iota(shape, 0))
            & ((source & (wide - 1)) == target * wide3 - 1 + slot)
            & (slot < wide3 + 1)
        )
        part = dot(onehot(choose).reshape((high3 + 1) * 16, -1), y3)
        cut = part.shape[0] // 2
        message[0:cut, 0:own3] = part[0:cut]
        message[0:cut, 64 : 64 + own3] = part[cut:]
        wide = wide4 * count
        shape = (high4, 8, y4.shape[0])
        source = iota(shape, 2)
        slot = iota(shape, 1)
        choose = (
            ((source >> (wide.bit_length() - 1)) == iota(shape, 0))
            & ((source & (wide - 1)) == target * wide4 + slot)
            & (slot < wide4)
        )
        part = dot(onehot(choose).reshape(high4 * 8, -1), y4)
        message[cut : cut + high4 * 8, 0:own4] = part
        out[...] = message[...].astype(BF16)


class Packing:
    def __init__(self, shapes):
        items = []
        for name, (rows, width) in shapes.items():
            for low in range(0, width, LANES):
                items.append((rows, min(LANES, width - low), name, low))
        items.sort(key=lambda item: (-item[0], -item[1], item[2]))
        blocks = []
        self.pieces = []
        for rows, width, name, low in items:
            for block in blocks:
                if block[1] + width <= LANES:
                    break
            else:
                block = [rows, 0, sum(b[0] for b in blocks)]
                blocks.append(block)
            self.pieces.append((name, low, width, rows, block[2], block[1]))
            block[1] += width
        self.total = sum(b[0] for b in blocks)

    def ranges(self, names):
        spans = sorted({(p[4], p[4] + p[3]) for p in self.pieces if p[0] in names})
        merged = []
        for low, high in spans:
            if merged and low <= merged[-1][1]:
                merged[-1][1] = max(merged[-1][1], high)
            else:
                merged.append([low, high])
        return merged

    def assemble(self, name, stacked, width, groups, target):
        count = stacked.shape[0]
        starts = aligned(groups)
        for piece, low, size, rows, row, lane in self.pieces:
            if piece != name:
                continue
            for j in range(count):
                at = j * width + low
                end = at + size
                first = 0
                for group, start in zip(groups, starts):
                    a, b = max(at, first), min(end, first + group)
                    if a < b:
                        target[0:rows, start + a - first : start + b - first] = stacked[
                            j, row : row + rows, lane + a - at : lane + b - at
                        ]
                    first += group


def aligned(groups):
    starts, at = [], 0
    for group in groups:
        starts.append(at)
        at += up_to(group, LANES)
    return starts


def aligned_width(groups):
    return sum(up_to(group, LANES) for group in groups)


def pack_kernel(packing, names, *refs):
    sources = dict(zip(names, refs[:-1]))
    out = refs[-1]
    for name, low, size, rows, row, lane in packing.pieces:
        out[row : row + rows, lane : lane + size] = sources[name][:, low : low + size]


def fetch(packing, names, me, buffers, stacked, semaphores):
    copies = []
    for k, buffer in enumerate(buffers):
        for s, (low, high) in enumerate(packing.ranges(names)):
            copy = pltpu.make_async_copy(
                buffer.at[pl.ds(low, high - low)],
                stacked.at[me ^ k, pl.ds(low, high - low)],
                semaphores.at[k, s],
            )
            copy.start()
            copies.append(copy)
    return copies


def fine_kernel(plan, index, *refs):
    packing, layouts, count, unit, offs, widths = plan
    one, two, top, bottom, from_left, from_right, bias = refs[:7]
    buffers = refs[7 : 7 + count]
    y1_ref, y2_ref, d12_ref, d3_ref, d4_ref = refs[7 + count : 12 + count]
    (x1, m1, v1, t1, tb, s12, x2, m2, v2, t2, s3, k1, k2, g1, g2, stacked, semaphores) = refs[12 + count :]
    row, me, row_count, col_count = index[0], index[1], index[2], index[3]
    copies = fetch(packing, FINE, me, buffers, stacked, semaphores)
    high1, wide1, chan1 = one.shape
    high2, wide2, chan2 = two.shape
    stretch_fine(0, layouts, one, top, bottom, x1, 16)
    stretch_fine(1, layouts, two, top, bottom, x2, 16)
    b1, b2 = BEFORE[0], BEFORE[1]
    rows2 = high2 + b2 + AFTER
    x1[:, 16 - b1 : 16, :] = from_left[:, 0:b1, 0:chan1].astype(F32)
    x1[:, 16 + wide1 : 16 + wide1 + AFTER, :] = from_right[:, 0:AFTER, 0:chan1].astype(F32)
    x2[:, 16 - b2 : 16, :] = from_left[0:rows2, b1 : b1 + b2, 0:chan2].astype(F32)
    x2[:, 16 + wide2 : 16 + wide2 + AFTER, :] = from_right[
        0:rows2, AFTER : 2 * AFTER, 0:chan2
    ].astype(F32)
    for copy in copies:
        copy.wait()
    packing.assemble("conv_one", stacked, widths["conv_one"], (chan1,), k1)
    packing.assemble("conv_two", stacked, widths["conv_two"], (chan2,), k2)
    packing.assemble("down_one", stacked, widths["down_one"], groups_one(unit), g1)
    packing.assemble("down_two", stacked, widths["down_two"], groups_two(unit), g2)
    ys = []
    for x, m, v, k, before, high, wide, chan, base in (
        (x1, m1, v1, k1, b1, high1, wide1, chan1, 0),
        (x2, m2, v2, k2, b2, high2, wide2, chan2, 2 * unit),
    ):
        mid_high = high + before
        mid_wide = up_to(wide + before, 8)
        mid = taps(x, mid_high, mid_wide, 1, 0, 16 - before, lambda t: k[t * chan : (t + 1) * chan, 0:chan])
        mid = jax.nn.relu(mid + bias[0:1, base : base + chan]).reshape(mid_high, mid_wide, chan)
        ok = inside(
            mid.shape, row * high - before + 1, row_count * high, me * wide - before + 1, col_count * wide
        )
        m[:, 0:mid_wide, :] = rounded(jnp.where(ok, mid, 0.0))
        y_high = high + before - 2
        y_wide = up_to(wide + before - 2, 8)
        first = 9 * chan
        y = taps(
            m, y_high, y_wide, 1, 0, 0,
            lambda t: k[first + t * chan : first + (t + 1) * chan, 0:chan],
        )
        y = y + bias[0:1, base + chan : base + 2 * chan]
        y = y.reshape(y_high, y_wide, chan) + x[2 : 2 + y_high, 18 - before : 18 - before + y_wide, :]
        skip = before - 2
        ok = inside(y.shape, row * high - skip, row_count * high, me * wide - skip, col_count * wide)
        v[:, 0:y_wide, 0:chan] = rounded(jnp.where(ok, jax.nn.relu(y), 0.0))
        ys.append(v[skip : skip + high, skip : skip + wide, 0:chan].astype(BF16))
    y1_ref[...] = ys[0]
    y2_ref[...] = ys[1]
    s1 = aligned(groups_one(unit))
    off1, off2 = offs[0], offs[1]
    half_high, half_wide = high1 // 2, wide1 // 2
    out_high, out_wide = half_high + 3, up_to(half_wide + 3, 8)
    first = taps(
        (v1,), out_high, out_wide, 2, 0, 0, lambda t: g1[t * unit : (t + 1) * unit, 0 : 4 * unit], (0, unit)
    )
    first = first + bias[0:1, off1 : off1 + 4 * unit]
    s12[...] = first[:, 0 : 2 * unit].reshape(out_high, out_wide, 2 * unit)
    d12_ref[...] = s12[3 : 3 + half_high, 3 : 3 + half_wide, :]
    t = jax.nn.relu(first[:, 2 * unit : 4 * unit]).reshape(out_high, out_wide, 2 * unit)
    ok = inside(
        t.shape, row * half_high - 3, row_count * half_high, me * half_wide - 3, col_count * half_wide
    )
    t1[:, 0:out_wide, 0 : 2 * unit] = rounded(jnp.where(ok, t, 0.0))
    quarter_high, quarter_wide = half_high // 2, half_wide // 2
    d13 = taps(
        (t1,), quarter_high, quarter_wide, 2, 2, 2,
        lambda t: g1[t * unit : (t + 1) * unit, s1[1] : s1[1] + 4 * unit], (0, unit),
    )
    d13 = d13 + bias[0:1, off1 + 4 * unit : off1 + 8 * unit]
    q_high, q_wide = quarter_high + 1, up_to(quarter_wide + 1, 8)
    t14b = taps(
        (t1,), q_high, q_wide, 2, 0, 0,
        lambda t: g1[t * unit : (t + 1) * unit, s1[2] : s1[2] + unit], (unit, 2 * unit),
    )
    t14b = jax.nn.relu(t14b + bias[0:1, off1 + 8 * unit : off1 + 9 * unit]).reshape(q_high, q_wide, unit)
    q_args = (row * quarter_high - 1, row_count * quarter_high, me * quarter_wide - 1, col_count * quarter_wide)
    tb[:, 0:q_wide, 0:unit] = rounded(jnp.where(inside(t14b.shape, *q_args), t14b, 0.0))
    e_high, e_wide = quarter_high // 2, 8
    d14 = taps(
        (tb,), e_high, e_wide, 2, 0, 0,
        lambda t: g1[t * unit : (t + 1) * unit, s1[3] : s1[3] + 8 * unit], (0, unit),
    )
    d14 = d14 + bias[0:1, off1 + 9 * unit : off1 + 17 * unit]
    s2 = aligned(groups_two(unit))
    second = taps(
        (v2,), q_high, q_wide, 2, 0, 0,
        lambda t: g2[t * chan2 : (t + 1) * chan2, 0 : s2[1] + 2 * unit], (0, chan2),
    )
    d23 = second[:, 0 : 4 * unit] + bias[0:1, off2 : off2 + 4 * unit]
    s3[...] = d23.reshape(q_high, q_wide, 4 * unit)
    d3_ref[...] = d13.reshape(quarter_high, quarter_wide, 4 * unit) + s3[
        1 : 1 + quarter_high, 1 : 1 + quarter_wide, :
    ]
    t24 = jax.nn.relu(second[:, s2[1] : s2[1] + 2 * unit] + bias[0:1, off2 + 4 * unit : off2 + 6 * unit])
    t24 = t24.reshape(q_high, q_wide, 2 * unit)
    t2[:, 0:q_wide, 0 : 2 * unit] = rounded(jnp.where(inside(t24.shape, *q_args), t24, 0.0))
    d24 = taps(
        (t2,), e_high, e_wide, 2, 0, 0,
        lambda t: g2[t * chan2 : (t + 1) * chan2, s2[2] : s2[2] + 8 * unit], (0, chan2),
    )
    d24 = d24 + bias[0:1, off2 + 6 * unit : off2 + 14 * unit]
    d4_ref[...] = (d14 + d24).reshape(e_high, e_wide, 8 * unit)


FINE = ("conv_one", "conv_two", "down_one", "down_two")
LAST = ("down_three", "lift_two", "lift_three", "lift_four")


def groups_one(unit):
    return (4 * unit, 4 * unit, unit, 8 * unit)


def groups_two(unit):
    return (4 * unit, 2 * unit, 8 * unit)


def join_kernel(plan, index, *refs):
    packing, count, unit, offs, widths, shapes = plan
    blocks = refs[:count]
    y1_ref, y2_ref, d12_ref, d3_ref, d4_ref, bias = refs[count : count + 6]
    buffers = refs[count + 6 : 2 * count + 6]
    out1, out2, out3, out4 = refs[2 * count + 6 : 2 * count + 10]
    (v3a, v3b, a2, a3a, a3b, a1, p2, p1, c3, k3, l2, l3, l4, stacked, semaphores) = refs[2 * count + 10 :]
    me = index[1]
    copies = fetch(packing, LAST, me, buffers, stacked, semaphores)
    (high2, wide2, chan2), (high3, wide3, chan3), (high4, wide4, chan4) = shapes[1:]
    own3, own4 = chan3 // count, chan4 // count
    cut = (high3 + 1) * 8
    parts = [
        jnp.concatenate([b[0:cut, 0:own3].astype(F32), b[0:cut, 64 : 64 + own3].astype(F32)], axis=0)
        for b in blocks
    ]
    whole3 = natural(parts, me, own3, chan3).reshape(high3 + 1, 16, chan3)
    v3 = (v3a, v3b)
    wide_store(v3, slice(None), slice(0, 16), whole3)
    y4 = natural([b[cut : cut + high4 * 8, 0:own4] for b in blocks], me, own4, chan4)
    y3 = wide_load(v3, slice(1, 1 + high3), slice(1, 1 + wide3))[:, :, 0:chan3]
    for copy in copies:
        copy.wait()
    groups3, groups4 = (unit, 2 * unit), (unit, 2 * unit, 4 * unit)
    packing.assemble("down_three", stacked, widths["down_three"], (chan4,), k3)
    packing.assemble("lift_two", stacked, widths["lift_two"], (unit,), l2)
    packing.assemble("lift_three", stacked, widths["lift_three"], groups3, l3)
    packing.assemble("lift_four", stacked, widths["lift_four"], groups4, l4)
    off3, offl2, offl3, offl4 = offs[2:]

    def lifted(flat, kernel, groups, offset):
        values, first = [], 0
        for group, start in zip(groups, aligned(groups)):
            value = dot(flat, kernel[:, start : start + group])
            values.append(value + bias[0:1, offset + first : offset + first + group])
            first += group
        return values

    def double(scratch, value, keep):
        high, wide, channels = value.shape
        for r in range(2):
            for q in range(2):
                wide_store(scratch, pl.ds(r, high, stride=2), pl.ds(q, wide, stride=2), value)
        return wide_load(scratch, slice(0, 2 * high), slice(0, keep))[:, :, 0:channels]

    u4 = [u.reshape(high4, 8, -1) for u in lifted(y4, l4, groups4, offl4)]
    u3 = [u.reshape(high3, wide3, -1) for u in lifted(y3.reshape(high3 * wide3, chan3), l3, groups3, offl3)]
    y2 = y2_ref[...]
    (u2,) = lifted(y2.reshape(high2 * wide2, chan2), l2, (unit,), offl2)
    d34 = taps(v3, high4, 8, 2, 0, 0, lambda t: k3[t * chan3 : (t + 1) * chan3, 0:chan4], (0, chan3))
    d34 = d34 + bias[0:1, off3 : off3 + chan4]
    four = jax.nn.relu(d4_ref[...] + (d34 + y4).reshape(high4, 8, chan4))
    c3[...] = four
    out4[...] = c3[:, 0:wide4, :].astype(BF16)
    three = double((a3a, a3b), u4[2], wide3) + d3_ref[...] + y3
    out3[...] = jax.nn.relu(three).astype(BF16)
    two = double((a2,), u4[1], wide3) + u3[1]
    two = double((p2,), two, wide2) + d12_ref[...] + y2.astype(F32)
    out2[...] = jax.nn.relu(two).astype(BF16)
    fine = double((a1,), u4[0], wide3) + u3[0]
    fine = double((p1,), fine, wide2) + u2.reshape(high2, wide2, unit)
    fine = double((p1,), fine, shapes[0][1]) + y1_ref[...].astype(F32)
    out1[...] = jax.nn.relu(fine).astype(BF16)


def offsets(width):
    start = 30 * width
    return (
        start,
        start + 17 * width,
        start + 31 * width,
        start + 39 * width,
        start + 40 * width,
        start + 43 * width,
    )


def flipped(value, mask, count):
    return lax.ppermute(value, "cols", [(i, i ^ mask) for i in range(count)])


def shifted(value, axis, distance):
    count = lax.axis_size(axis)
    route = [(i, i + distance) for i in range(count) if 0 <= i + distance < count]
    return lax.ppermute(value, axis, route)


def exchanged(value, count):
    return [value] + [flipped(value, mask, count) for mask in range(1, count)]


def gathered(value, count):
    held = {0: value}
    bits = [1 << b for b in range(1, count.bit_length() - 1)] + ([1] if count > 1 else [])
    for bit in bits:
        for mask in list(held):
            held[mask | bit] = flipped(held[mask], bit, count)
    return [held[mask] for mask in range(count)]


def on_device(
    feat_one,
    feat_two,
    feat_three,
    feat_four,
    conv_one,
    conv_two,
    conv_three,
    conv_four,
    down_one,
    down_two,
    down_three,
    lift_two,
    lift_three,
    lift_four,
    biases,
):
    count = lax.axis_size("cols")
    row_total = lax.axis_size("rows")
    feats = (feat_one, feat_two, feat_three, feat_four)
    shapes = tuple(f.shape for f in feats)
    unit = feat_one.shape[2]
    offs = offsets(unit)
    bias = biases.reshape(1, -1)
    index = jnp.stack(
        [
            lax.axis_index("rows").astype(jnp.int32),
            lax.axis_index("cols").astype(jnp.int32),
            jnp.int32(row_total),
            jnp.int32(count),
        ]
    )
    smem = [pl.BlockSpec(memory_space=pltpu.SMEM)]
    anywhere = [pl.BlockSpec(memory_space=pl.ANY)]
    layouts = (RowLayout(shapes, BEFORE), RowLayout(shapes, (AFTER,) * 4))
    most = max(layouts[0].total, layouts[1].total)
    down, up = pl.pallas_call(
        functools.partial(rows_kernel, layouts),
        out_shape=[jax.ShapeDtypeStruct((l.total, LANES), BF16) for l in layouts],
        in_specs=vmem(4),
        out_specs=vmem(2),
        scratch_shapes=[pltpu.VMEM((most, LANES), F32)],
        compiler_params=PARAMS,
        name="rows_pack",
    )(*feats)
    top = shifted(down, "rows", 1)
    bottom = shifted(up, "rows", -1)

    weights = {
        "conv_one": conv_one,
        "conv_two": conv_two,
        "down_one": down_one,
        "down_two": down_two,
        "down_three": down_three,
        "lift_two": lift_two,
        "lift_three": lift_three,
        "lift_four": lift_four,
    }
    widths = {name: w.shape[1] for name, w in weights.items()}
    packing = Packing({name: w.shape for name, w in weights.items()})
    packed = pl.pallas_call(
        functools.partial(pack_kernel, packing, tuple(weights)),
        out_shape=jax.ShapeDtypeStruct((packing.total, LANES), BF16),
        in_specs=vmem(len(weights)),
        out_specs=pl.BlockSpec(memory_space=pltpu.VMEM),
        compiler_params=PARAMS,
        name="weights_pack",
    )(*weights.values())
    buffers = gathered(packed, count)

    (high1, wide1, chan1), (high2, wide2, chan2), (high3, wide3, chan3), (high4, wide4, chan4) = shapes
    size4 = gather_four(shapes[3])
    total3, head3 = gather_three(shapes[2])
    lanes = max(chan4, 2 * chan3)
    rows1 = high1 + BEFORE[0] + AFTER
    rows2 = high2 + BEFORE[1] + AFTER
    gather, to_right, to_left = pl.pallas_call(
        functools.partial(columns_kernel, layouts),
        out_shape=[
            jax.ShapeDtypeStruct((size4 + head3, lanes), BF16),
            jax.ShapeDtypeStruct((rows1, 16, LANES), BF16),
            jax.ShapeDtypeStruct((rows1, 8, LANES), BF16),
        ],
        in_specs=vmem(6),
        out_specs=vmem(3),
        scratch_shapes=[
            pltpu.VMEM((rows1, wide1, chan1), F32),
            pltpu.VMEM((rows2, wide2, chan2), F32),
            pltpu.VMEM((total3, chan3), F32),
            pltpu.VMEM((size4 + head3, lanes), F32),
            pltpu.VMEM((rows1, 16, LANES), F32),
        ],
        compiler_params=PARAMS,
        name="columns_pack",
    )(*feats, top, bottom)
    coarse = exchanged(gather, count)
    from_left = shifted(to_right, "cols", 1)
    from_right = shifted(to_left, "cols", -1)

    sizes = (count, high3, wide3, chan3, high4, wide4, chan4, 6 * unit, 14 * unit)
    own3, own4 = chan3 // count, chan4 // count
    half, last = message_rows(sizes)
    full_wide3, full_wide4 = up_to(wide3 * count + 2, 8), up_to(wide4 * count + 2, 8)
    mid, res3, res4 = pl.pallas_call(
        functools.partial(coarse_first_kernel, sizes),
        out_shape=[
            jax.ShapeDtypeStruct((last, LANES), BF16),
            jax.ShapeDtypeStruct(((high3 + 1) * wide3 * count, own3), BF16),
            jax.ShapeDtypeStruct((high4 * wide4 * count, own4), BF16),
        ],
        in_specs=smem + vmem(count + 3),
        out_specs=vmem(3),
        scratch_shapes=[
            pltpu.VMEM((high3 + BEFORE[2] + AFTER, full_wide3, chan3), F32),
            pltpu.VMEM((high4 + BEFORE[3] + AFTER, full_wide4, chan4), F32),
            pltpu.VMEM((last, LANES), F32),
        ],
        compiler_params=PARAMS,
        name="coarse_first",
    )(index, *coarse, conv_three, conv_four, bias)
    mids = exchanged(mid, count)
    message = (high3 + 1) * 8 + high4 * 8
    sent = pl.pallas_call(
        functools.partial(coarse_second_kernel, sizes),
        out_shape=[jax.ShapeDtypeStruct((message, LANES), BF16)] * count,
        in_specs=smem + vmem(count + 5),
        out_specs=vmem(count),
        scratch_shapes=[
            pltpu.VMEM((high3 + BEFORE[2] + AFTER - 2, full_wide3, chan3), F32),
            pltpu.VMEM((high4 + BEFORE[3] + AFTER - 2, full_wide4, chan4), F32),
            pltpu.VMEM((message, LANES), F32),
        ],
        compiler_params=PARAMS,
        name="coarse_second",
    )(index, *mids, res3, res4, conv_three, conv_four, bias)
    coarse_out = [sent[0]] + [flipped(sent[mask], mask, count) for mask in range(1, count)]

    plan = (packing, layouts, count, unit, offs, widths)
    mid_wide1, mid_wide2 = up_to(wide1 + BEFORE[0], 8), up_to(wide2 + BEFORE[1], 8)
    y_wide1, y_wide2 = up_to(wide1 + BEFORE[0] - 2, 8), up_to(wide2 + BEFORE[1] - 2, 8)
    half_wide = up_to(wide1 // 2 + 3, 8)
    quarter_wide = up_to(wide1 // 4 + 1, 8)
    fine = pl.pallas_call(
        functools.partial(fine_kernel, plan),
        out_shape=[
            jax.ShapeDtypeStruct(shapes[0], BF16),
            jax.ShapeDtypeStruct(shapes[1], BF16),
            jax.ShapeDtypeStruct((high1 // 2, wide1 // 2, 2 * unit), F32),
            jax.ShapeDtypeStruct((high1 // 4, wide1 // 4, 4 * unit), F32),
            jax.ShapeDtypeStruct((high1 // 8, 8, 8 * unit), F32),
        ],
        in_specs=smem + vmem(7) + anywhere * count,
        out_specs=vmem(5),
        scratch_shapes=[
            pltpu.VMEM((rows1, 24 + mid_wide1, chan1), F32),
            pltpu.VMEM((high1 + BEFORE[0], mid_wide1 + 8, chan1), F32),
            pltpu.VMEM((high1 + BEFORE[0] - 2, 2 * half_wide + 8, LANES), F32),
            pltpu.VMEM((high1 // 2 + 3, max(2 * quarter_wide, half_wide) + 8, LANES), F32),
            pltpu.VMEM((high1 // 4 + 1, max(16, quarter_wide) + 8, LANES), F32),
            pltpu.VMEM((high1 // 2 + 3, half_wide, 2 * unit), F32),
            pltpu.VMEM((rows2, 24 + mid_wide2, chan2), F32),
            pltpu.VMEM((high2 + BEFORE[1], mid_wide2 + 8, chan2), F32),
            pltpu.VMEM((high2 + BEFORE[1] - 2, max(2 * quarter_wide, y_wide2) + 8, LANES), F32),
            pltpu.VMEM((high1 // 4 + 1, max(16, quarter_wide) + 8, LANES), F32),
            pltpu.VMEM((high1 // 4 + 1, quarter_wide, 4 * unit), F32),
            pltpu.VMEM((conv_one.shape[0], LANES), BF16),
            pltpu.VMEM((conv_two.shape[0], LANES), BF16),
            pltpu.VMEM((down_one.shape[0], aligned_width(groups_one(unit))), BF16),
            pltpu.VMEM((down_two.shape[0], aligned_width(groups_two(unit))), BF16),
            pltpu.VMEM((count, packing.total, LANES), BF16),
            pltpu.SemaphoreType.DMA((count, len(packing.ranges(FINE)))),
        ],
        compiler_params=PARAMS,
        name="fine",
    )(index, feat_one, feat_two, top, bottom, from_left, from_right, bias, *buffers)

    plan = (packing, count, unit, offs, widths, shapes)
    return tuple(
        pl.pallas_call(
            functools.partial(join_kernel, plan),
            out_shape=[jax.ShapeDtypeStruct(shape, BF16) for shape in shapes],
            in_specs=smem + vmem(count + 6) + anywhere * count,
            out_specs=vmem(4),
            scratch_shapes=[
                pltpu.VMEM((high3 + 1, 24, LANES), F32),
                pltpu.VMEM((high3 + 1, 24, LANES), F32),
                pltpu.VMEM((2 * high4, 16, LANES), F32),
                pltpu.VMEM((2 * high4, 16, LANES), F32),
                pltpu.VMEM((2 * high4, 16, LANES), F32),
                pltpu.VMEM((2 * high4, 16, LANES), F32),
                pltpu.VMEM((high2, wide2, LANES), F32),
                pltpu.VMEM((high1, wide1, LANES), F32),
                pltpu.VMEM((high4, 8, chan4), F32),
                pltpu.VMEM((down_three.shape[0], up_to(chan4, LANES)), BF16),
                pltpu.VMEM((chan2, LANES), BF16),
                pltpu.VMEM((chan3, aligned_width((unit, 2 * unit))), BF16),
                pltpu.VMEM((chan4, aligned_width((unit, 2 * unit, 4 * unit))), BF16),
                pltpu.VMEM((count, packing.total, LANES), BF16),
                pltpu.SemaphoreType.DMA((count, len(packing.ranges(LAST)))),
            ],
            compiler_params=PARAMS,
            name="join",
        )(index, *coarse_out, *fine, bias, *buffers)
    )


def solution(mesh):
    spatial = P(("win", "rows"), "cols", None)
    placed = (spatial,) * 4 + (P(None, "cols"),) * 10 + (P(),)
    return jax.shard_map(
        on_device,
        mesh=mesh,
        in_specs=placed,
        out_specs=(spatial,) * 4,
        check_vma=False,
    )
```

time: 223 us -> 108 us (0.48); the launches traced: 219 us -> 108 us
  starting transfers between devices: 88.5 us -> 17.1 us
  blocking collectives: 39.4 us -> 0 us
  Pallas kernels: 0 us -> 32.9 us
  waiting for transfers between devices: 4.3 us -> 36.9 us
  matrix products: 19.3 us -> 0 us
  local copies, waits for them, and re-layouts: 37.9 us -> 19.3 us
  between operations: 15.8 us -> 0.97 us
  other arithmetic: 13.5 us -> 0.56 us
    ppermute x30 -> x16, starting transfers between devices: 88.3 us -> 17.1 us  [the longest x4 8.66 us: shifted(): return lax.ppermute(value, axis, route)]
    all_gather x6 -> x0, blocking collectives: 39.4 us -> none  [the longest x1 9.12 us: on_device(): lax.all_gather(down_one, 'cols', axis=1, tiled=True)]
    ppermute x30 -> x16, waiting for transfers between devices: 2.16 us -> 36.9 us  [the longest x12 32.2 us: flipped(): return lax.ppermute(value, 'cols', [(i, i ^ mask) for i in range(count)])]
    pallas_call x0 -> x7, Pallas kernels: none -> 32.9 us  [the longest x1 11.9 us: on_device(): pl.pallas_call(functools.partial(fine_kernel, plan), out_shape=[jax.Shape...]
    slice x94 -> x0, local copies, waits for them, and re-layouts: 23.3 us -> none  [the longest x66 15.9 us: patch_conv(): lax.slice(extended, (row_tap, col_tap, 0), (row_tap + stride * (height -...]
    dot_general x18 -> x0, matrix products: 19.3 us -> none  [the longest x15 18.8 us: patch_conv(): jnp.dot(flat, weight, preferred_element_type=jnp.float32)]
    unnamed x114 -> x54, local copies, waits for them, and re-layouts: 3.51 us -> 18.7 us
    concatenate x18 -> x0, local copies, waits for them, and re-layouts: 10.5 us -> none  [the longest x14 10.5 us: patch_conv(): stacked = jnp.concatenate(taps, axis=2)]
  transfers between devices with their start and end apart: 34 -> 16, of which waited for: 4 -> 5; matrix products, arithmetic and copies ran while one was open for 31% -> 6% of each run, Pallas kernels for 0% -> 23%
where the time goes in v1:
time: 108 us
  waiting for transfers between devices  36.9 us (34%)
  Pallas kernels  32.9 us (30%)
  local copies, waits for them, and re-layouts  19.3 us (18%)
  starting transfers between devices  17.1 us (16%)
    ppermute x12, waiting for transfers between devices, flipped(): return lax.ppermute(value, 'cols', [(i, i ^ mask) for i in range(count)])  32.2 us
    unnamed x54, local copies, waits for them, and re-layouts  18.7 us
    pallas_call x1, Pallas kernels, on_device(): pl.pallas_call(functools.partial(fine_kernel, plan), out_shape=[jax.Shape...  11.9 us
    ppermute x4, starting transfers between devices, shifted(): return lax.ppermute(value, axis, route)  8.66 us
    ppermute x12, starting transfers between devices, flipped(): return lax.ppermute(value, 'cols', [(i, i ^ mask) for i in range(count)])  8.46 us
    pallas_call x1, Pallas kernels, on_device(): pl.pallas_call(functools.partial(join_kernel, plan), out_shape=[jax.Shape...  5.11 us
    ppermute x4, waiting for transfers between devices, shifted(): return lax.ppermute(value, axis, route)  4.73 us
    pallas_call x1, Pallas kernels, on_device(): pl.pallas_call(functools.partial(coarse_second_kernel, sizes), out_shape=...  4.54 us
  transfers between devices with their start and end apart: 16, of which 5 were waited for; matrix products, arithmetic and copies ran while one was open for 6% of the time, Pallas kernels for 23%

profile of v1, /device:TPU:0, one launch (start us, length us, event | category | flops | bytes accessed | tf_op | source)
XLA Modules:
  0.0 107.8 jit_solution(17055990288135130722)
XLA Ops:
  0.7 1.9 %copy.24.refs_1_ = bf16[1728,24]{1,0:T(8,128)(2,1)} copy(bf16[1728,24]{0,1:T(8,128)(2,1)} %param.20) | data formatting | bytes 165888 | tf_op args[5]
  2.6 2.0 %copy.26.refs_3_ = bf16[864,168]{1,0:T(8,128)(2,1)} copy(bf16[864,168]{0,1:T(8,128)(2,1)} %param.24) | data formatting | bytes 580608 | tf_op args[9]
  4.6 0.0 copy-done.3
  4.6 1.0 copy.27.refs_4_
  5.6 0.8 copy.23.refs_0_
  6.4 0.8 copy.25.refs_2_
  7.2 0.8 copy.30.refs_7_
  8.0 0.7 copy.29.refs_6_
  8.7 0.7 copy.28.refs_5_
  9.5 3.0 %weights_pack.1.refs_7_.refs_10_ = bf16[4368,128]{1,0:T(8,128)(2,1)} custom-call(bf16[864,12]{1,0:T(8,128)(2,1)} %copy.23.refs_0_, bf16[1728,24]{1,0:T(8,128)(2,1)} %copy.24.refs_1_, bf16[432,204]{1,0:T(8,128)(2,1)} %copy.25.refs_2_, bf16[864,168]{1,0:T(8,128)(2,1)} %copy.26.refs_3_, bf16[1728,96]{1,0:T(8,128)(2,1)} %copy.27.refs_4_, ...), custom_call_target="tpu_custom_call" | custom-call | tf_op jit(solution)/shard_map/weights_pack/pallas_call | solution.py:729
  12.4 3.0 %collective-permute-start.14 = (bf16[4368,128]{1,0:T(8,128)(2,1)}, bf16[4368,128]{1,0:T(8,128)(2,1)S(1)}, u32[]{:S(2)}, u32[]{:S(2)}) collective-permute-start(bf16[4368,128]{1,0:T(8,128)(2,1)} %weights_pack.1.refs_7_.refs_10_), channel_id=1, source_target_pairs={{0,2},{1,3},{2,0},{3,1},{4,6},{5,7},{6,4},{7,5},{8,10},{9,11},{10,... | collective-permute-start | bytes 3354632 | tf_op jit(solution)/shard_map/ppermute | solution.py:647
  15.4 0.0 collective-permute-start.13
  15.4 24.9 %collective-permute-done.14.refs_9_.refs_12_ = bf16[4368,128]{1,0:T(8,128)(2,1)S(1)} collective-permute-done((bf16[4368,128]{1,0:T(8,128)(2,1)}, bf16[4368,128]{1,0:T(8,128)(2,1)S(1)}, u32[]{:S(2)}, u32[]{:S(2)}) %collective-permute-start.14) | collective-permute-done | bytes 1118240 | tf_op jit(solution)/shard_map/ppermute | solution.py:647
  40.3 0.0 collective-permute-start.15
  40.3 2.0 %rows_pack.1 = (bf16[304,128]{1,0:T(8,128)(2,1)}, bf16[128,128]{1,0:T(8,128)(2,1)}) custom-call(bf16[32,32,48]{2,1,0:T(8,128)(2,1)} %refs_0_.2, bf16[16,16,96]{2,1,0:T(8,128)(2,1)} %refs_1_.2, bf16[8,8,192]{2,1,0:T(8,128)(2,1)} %three.3, bf16[4,4,384]{2,1,0:T(4,128)(2,1)} %four.3), custom_call_target="tpu_custom_call" | custom-call | tf_op jit(solution)/shard_map/rows_pack/pallas_call | solution.py:705
  42.3 3.7 %collective-permute-start = (bf16[304,128]{1,0:T(8,128)(2,1)}, bf16[304,128]{1,0:T(8,128)(2,1)S(1)}, u32[]{:S(2)}, u32[]{:S(2)}) collective-permute-start(bf16[304,128]{1,0:T(8,128)(2,1)} %get-tuple-element.21), channel_id=1, source_target_pairs={{0,4},{4,8},{8,12},{1,5},{5,9},{9,13},{2,6},{6,10},{10,14},{3,7},{... | collective-permute-start | bytes 233480 | tf_op jit(solution)/shard_map/ppermute | solution.py:653
  46.0 1.3 %collective-permute-start.1 = (bf16[128,128]{1,0:T(8,128)(2,1)}, bf16[128,128]{1,0:T(8,128)(2,1)S(1)}, u32[]{:S(2)}, u32[]{:S(2)}) collective-permute-start(bf16[128,128]{1,0:T(8,128)(2,1)} %get-tuple-element.22), channel_id=1, source_target_pairs={{4,0},{8,4},{12,8},{5,1},{9,5},{13,9},{6,2},{10,6},{14,10},{7,3},{... | collective-permute-start | bytes 98312 | tf_op jit(solution)/shard_map/ppermute | solution.py:653
  47.3 4.7 %collective-permute-done.1.bottom.refs_3_ = bf16[128,128]{1,0:T(8,128)(2,1)S(1)} collective-permute-done((bf16[128,128]{1,0:T(8,128)(2,1)}, bf16[128,128]{1,0:T(8,128)(2,1)S(1)}, u32[]{:S(2)}, u32[]{:S(2)}) %collective-permute-start.1) | collective-permute-done | bytes 32800 | tf_op jit(solution)/shard_map/ppermute | solution.py:653
  52.0 0.0 collective-permute-done.top.refs_2_
  52.0 0.6 copy-done.7
  52.6 0.6 copy-done.4
  53.3 1.9 %columns_pack.1 = (bf16[88,384]{1,0:T(8,128)(2,1)}, bf16[43,16,128]{2,1,0:T(8,128)(2,1)}, bf16[43,8,128]{2,1,0:T(8,128)(2,1)}) custom-call(bf16[32,32,48]{2,1,0:T(8,128)(2,1)} %refs_0_.2, bf16[16,16,96]{2,1,0:T(8,128)(2,1)} %refs_1_.2, bf16[8,8,192]{2,1,0:T(8,128)(2,1)} %three.3, bf16[4,4,384]{2,1,0:T(4,128)(2,1)} %four.3, bf16[304,128]{1,0:T(8,128)(2,1)} %copy-done.4, ...), custom_call_target="tpu_custom_call" | custom-call | tf_op jit(solution)/shard_map/columns_pack/pallas_call | solution.py:745
  55.2 0.0 collective-permute-start.2
  55.2 1.5 %collective-permute-start.3 = (bf16[88,384]{1,0:T(8,128)(2,1)}, bf16[88,384]{1,0:T(8,128)(2,1)}, u32[]{:S(2)}, u32[]{:S(2)}) collective-permute-start(bf16[88,384]{1,0:T(8,128)(2,1)} %get-tuple-element.23.refs_0_), channel_id=1, source_target_pairs={{0,2},{1,3},{2,0},{3,1},{4,6},{5,7},{6,4},{7,5},{8,10},{9,11},{10,... | collective-permute-start | bytes 202760 | tf_op jit(solution)/shard_map/ppermute | solution.py:647
  56.7 0.4 collective-permute-start.4
  57.1 0.0 collective-permute-done.2.refs_1_
  57.1 0.6 copy-done.13
  57.7 2.2 %collective-permute-start.11 = (bf16[43,16,128]{2,1,0:T(8,128)(2,1)}, bf16[43,16,128]{2,1,0:T(8,128)(2,1)S(1)}, u32[]{:S(2)}, u32[]{:S(2)}) collective-permute-start(bf16[43,16,128]{2,1,0:T(8,128)(2,1)} %get-tuple-element.31), channel_id=1, source_target_pairs={{0,1},{1,2},{2,3},{4,5},{5,6},{6,7},{8,9},{9,10},{10,11},{12,13},{... | collective-permute-start | bytes 528392 | tf_op jit(solution)/shard_map/ppermute | solution.py:653
  59.9 0.6 pad_add_fusion.index
  60.4 0.0 copy-done.19
  60.4 0.6 reshape.11.refs_6_.refs_8_.refs_9_
  61.1 2.6 %copy.20.refs_5_.refs_7_ = bf16[6912,96]{1,0:T(8,128)(2,1)} copy(bf16[6912,96]{0,1:T(8,128)(2,1)} %param.22) | data formatting | bytes 2654208 | tf_op args[7]
  63.7 2.2 %copy.19.refs_4_.refs_6_ = bf16[3456,48]{1,0:T(8,128)(2,1)} copy(bf16[3456,48]{0,1:T(8,128)(2,1)} %param.21) | data formatting | bytes 663552 | tf_op args[6]
  65.9 0.0 collective-permute-done.3.refs_2_
  65.9 0.0 collective-permute-done.4.refs_3_
  65.9 4.5 %coarse_first.1 = (bf16[272,128]{1,0:T(8,128)(2,1)}, bf16[288,48]{1,0:T(8,128)(2,1)}, bf16[64,96]{1,0:T(8,128)(2,1)}) custom-call(s32[4]{0:T(128)} %pad_add_fusion.index, bf16[88,384]{1,0:T(8,128)(2,1)} %get-tuple-element.23.refs_0_, bf16[88,384]{1,0:T(8,128)(2,1)} %copy-done.13, bf16[88,384]{1,0:T(8,128)(2,1)} %collective-permute-done.3.refs_2_, ...), custom_call_target="tpu_custom_call" | custom-call | tf_op jit(solution)/shard_map/coarse_first/pallas_call | solution.py:772
  70.4 1.3 %collective-permute-start.5 = (bf16[272,128]{1,0:T(8,128)(2,1)}, bf16[272,128]{1,0:T(8,128)(2,1)S(1)}, u32[]{:S(2)}, u32[]{:S(2)}) collective-permute-start(bf16[272,128]{1,0:T(8,128)(2,1)} %get-tuple-element.24.refs_0_), channel_id=1, source_target_pairs={{0,1},{1,0},{2,3},{3,2},{4,5},{5,4},{6,7},{7,6},{8,9},{9,8},{10,11... | collective-permute-start | bytes 208904 | tf_op jit(solution)/shard_map/ppermute | solution.py:647
  71.7 0.2 collective-permute-start.6
  71.9 0.9 collective-permute-done.5.refs_1_
  72.8 0.0 copy-done.21
  72.8 1.5 %collective-permute-start.12 = (bf16[43,8,128]{2,1,0:T(8,128)(2,1)S(1)}, bf16[43,8,128]{2,1,0:T(8,128)(2,1)S(1)}, u32[]{:S(2)}, u32[]{:S(2)}) collective-permute-start(bf16[43,8,128]{2,1,0:T(8,128)(2,1)S(1)} %copy-done.21), channel_id=1, source_target_pairs={{1,0},{2,1},{3,2},{5,4},{6,5},{7,6},{9,8},{10,9},{11,10},{13,12},{... | collective-permute-start | bytes 264200 | tf_op jit(solution)/shard_map/ppermute | solution.py:653
  74.3 1.9 %collective-permute-done.6.refs_2_ = bf16[272,128]{1,0:T(8,128)(2,1)S(1)} collective-permute-done((bf16[272,128]{1,0:T(8,128)(2,1)}, bf16[272,128]{1,0:T(8,128)(2,1)S(1)}, u32[]{:S(2)}, u32[]{:S(2)}) %collective-permute-start.6) | collective-permute-done | bytes 69664 | tf_op jit(solution)/shard_map/ppermute | solution.py:647
  76.2 0.0 collective-permute-start.7
  76.2 4.4 %collective-permute-done.7.refs_3_ = bf16[272,128]{1,0:T(8,128)(2,1)S(1)} collective-permute-done((bf16[272,128]{1,0:T(8,128)(2,1)}, bf16[272,128]{1,0:T(8,128)(2,1)S(1)}, u32[]{:S(2)}, u32[]{:S(2)}) %collective-permute-start.7) | collective-permute-done | bytes 69664 | tf_op jit(solution)/shard_map/ppermute | solution.py:647
  80.7 0.0 copy-done.9
  80.7 0.6 copy-done.11
  81.3 4.5 %coarse_second.1 = (bf16[104,128]{1,0:T(8,128)(2,1)}, bf16[104,128]{1,0:T(8,128)(2,1)}, bf16[104,128]{1,0:T(8,128)(2,1)}, bf16[104,128]{1,0:T(8,128)(2,1)}) custom-call(s32[4]{0:T(128)} %pad_add_fusion.index, bf16[272,128]{1,0:T(8,128)(2,1)} %get-tuple-element.24.refs_0_, bf16[272,128]{1,0:T(8,128)(2,1)} %copy-done.9, bf16[272,128]{1,0:T(8,128)(2,1)} %copy-done.10, ...), custom_call_target="tpu_custom_call" | custom-call | tf_op jit(solution)/shard_map/coarse_second/pallas_call | solution.py:791
  85.8 0.4 collective-permute-start.10
  86.2 0.0 collective-permute-done.12.refs_5_
  86.2 0.6 collective-permute-start.8
  86.8 0.0 collective-permute-done.11.refs_4_
  86.8 1.2 %collective-permute-start.9 = (bf16[104,128]{1,0:T(8,128)(2,1)}, bf16[104,128]{1,0:T(8,128)(2,1)S(1)}, u32[]{:S(2)}, u32[]{:S(2)}) collective-permute-start(bf16[104,128]{1,0:T(8,128)(2,1)} %get-tuple-element.29), channel_id=1, source_target_pairs={{0,2},{1,3},{2,0},{3,1},{4,6},{5,7},{6,4},{7,5},{8,10},{9,11},{10,... | collective-permute-start | bytes 79880 | tf_op jit(solution)/shard_map/ppermute | solution.py:647
  88.0 0.0 collective-permute-done.13.refs_8_.refs_11_
  88.0 0.0 collective-permute-done.15.refs_10_.refs_13_
  88.0 1.0 copy-done.1
  89.0 1.0 copy-done.2
  90.0 11.9 %fine.1 = (bf16[32,32,48]{2,1,0:T(8,128)(2,1)}, bf16[16,16,96]{2,1,0:T(8,128)(2,1)}, f32[16,16,96]{2,1,0:T(8,128)}, f32[8,8,192]{2,1,0:T(8,128)}, f32[4,8,384]{2,1,0:T(8,128)}) custom-call(s32[4]{0:T(128)} %pad_add_fusion.index, bf16[32,32,48]{2,1,0:T(8,128)(2,1)} %refs_0_.2, bf16[16,16,96]{2,1,0:T(8,128)(2,1)} %refs_1_.2, bf16[304,128]{1,0:T(8,128)(2,1)} %copy-done.4, ...), custom_call_target="tpu_custom_call" | custom-call | tf_op jit(solution)/shard_map/fine/pallas_call | solution.py:811
  101.9 0.0 collective-permute-done.10.refs_3_
  101.9 0.0 collective-permute-done.8.refs_1_
  101.9 0.0 collective-permute-done.9.refs_2_
  102.0 0.6 copy-done.15
  102.5 0.0 copy-done.16
  102.5 0.0 copy-done.17
  102.6 5.1 %join.1 = (bf16[32,32,48]{2,1,0:T(8,128)(2,1)}, bf16[16,16,96]{2,1,0:T(8,128)(2,1)}, bf16[8,8,192]{2,1,0:T(8,128)(2,1)}, bf16[4,4,384]{2,1,0:T(4,128)(2,1)}) custom-call(s32[4]{0:T(128)} %pad_add_fusion.index, bf16[104,128]{1,0:T(8,128)(2,1)} %get-tuple-element.27.refs_0_, bf16[104,128]{1,0:T(8,128)(2,1)} %copy-done.16, bf16[104,128]{1,0:T(8,128)(2,1)} %copy-done.17, ...), custom_call_target="tpu_custom_call" | custom-call | tf_op jit(solution)/shard_map/join/pallas_call | solution.py:847
  (32 shorter events, 0.1 us)
Async XLA Ops:
  0.6 3.9 %copy-start.3 = (bf16[1728,96]{0,1:T(8,128)(2,1)S(1)}, bf16[1728,96]{0,1:T(8,128)(2,1)}, u32[]{:S(2)}) copy-start(bf16[1728,96]{0,1:T(8,128)(2,1)} %param.25) | copy-start | bytes 995332
  0.6 4.9 %copy-start.14 = (bf16[864,12]{0,1:T(8,128)(2,1)S(1)}, bf16[864,12]{0,1:T(8,128)(2,1)}, u32[]{:S(2)}) copy-start(bf16[864,12]{0,1:T(8,128)(2,1)} %param.19) | copy-start | bytes 62212
  0.7 5.8 %copy-start.5 = (bf16[432,204]{0,1:T(8,128)(2,1)S(1)}, bf16[432,204]{0,1:T(8,128)(2,1)}, u32[]{:S(2)}) copy-start(bf16[432,204]{0,1:T(8,128)(2,1)} %param.23) | copy-start | bytes 528772
  2.6 4.7 %copy-start.12 = (bf16[384,84]{0,1:T(8,128)(2,1)S(1)}, bf16[384,84]{0,1:T(8,128)(2,1)}, u32[]{:S(2)}) copy-start(bf16[384,84]{0,1:T(8,128)(2,1)} %param.28) | copy-start | bytes 193540
  2.6 5.4 %copy-start.18 = (bf16[192,36]{0,1:T(8,128)(2,1)S(1)}, bf16[192,36]{0,1:T(8,128)(2,1)}, u32[]{:S(2)}) copy-start(bf16[192,36]{0,1:T(8,128)(2,1)} %param.27) | copy-start | bytes 41476
  2.6 6.1 %copy-start.20 = (bf16[96,12]{0,1:T(8,128)(2,1)S(1)}, bf16[96,12]{0,1:T(8,128)(2,1)}, u32[]{:S(2)}) copy-start(bf16[96,12]{0,1:T(8,128)(2,1)} %param.26) | copy-start | bytes 6916
  9.5 51.0 %copy-start.19 = (f32[3840]{0:T(1024)S(1)}, f32[3840]{0:T(1024)}, u32[]{:S(2)}) copy-start(f32[3840]{0:T(1024)} %param.29) | copy-start | bytes 46084
  12.4 27.8 %collective-permute-start.14 = (bf16[4368,128]{1,0:T(8,128)(2,1)}, bf16[4368,128]{1,0:T(8,128)(2,1)S(1)}, u32[]{:S(2)}, u32[]{:S(2)}) collective-permute-start(bf16[4368,128]{1,0:T(8,128)(2,1)} %weights_pack.1.refs_7_.refs_10_), channel_id=1, source_target_pairs={{0,2},{1,3},{2,0},{3,1},{4,6},{5,7},{6,4},{7,5},{8,10},{9,11},{10,... | collective-permute-start | bytes 3354632 | tf_op jit(solution)/shard_map/ppermute | solution.py:647
  15.4 72.6 %collective-permute-start.13 = (bf16[4368,128]{1,0:T(8,128)(2,1)}, bf16[4368,128]{1,0:T(8,128)(2,1)S(1)}, u32[]{:S(2)}, u32[]{:S(2)}) collective-permute-start(bf16[4368,128]{1,0:T(8,128)(2,1)} %weights_pack.1.refs_7_.refs_10_), channel_id=1, source_target_pairs={{0,1},{1,0},{2,3},{3,2},{4,5},{5,4},{6,7},{7,6},{8,9},{9,8},{10,11... | collective-permute-start | bytes 3354632 | tf_op jit(solution)/shard_map/ppermute | solution.py:647
  40.3 23.4 %copy-start = (bf16[4368,128]{1,0:T(8,128)(2,1)}, bf16[4368,128]{1,0:T(8,128)(2,1)S(1)}, u32[]{:S(2)}) copy-start(bf16[4368,128]{1,0:T(8,128)(2,1)S(1)} %collective-permute-done.14.refs_9_.refs_12_) | copy-start | bytes 3354628
  40.3 47.7 %collective-permute-start.15 = (bf16[4368,128]{1,0:T(8,128)(2,1)S(1)}, bf16[4368,128]{1,0:T(8,128)(2,1)S(1)}, u32[]{:S(2)}, u32[]{:S(2)}) collective-permute-start(bf16[4368,128]{1,0:T(8,128)(2,1)S(1)} %collective-permute-done.14.refs_9_.refs_12_), channel_id=1, source_target_pairs={{0,1},{1,0},{2,3},{3,2},{4,5},{5,4},{6,7},{7,6},{8,9},{9,8},{10,11... | collective-permute-start | bytes 3354632 | tf_op jit(solution)/shard_map/ppermute | solution.py:647
  42.3 9.8 %collective-permute-start = (bf16[304,128]{1,0:T(8,128)(2,1)}, bf16[304,128]{1,0:T(8,128)(2,1)S(1)}, u32[]{:S(2)}, u32[]{:S(2)}) collective-permute-start(bf16[304,128]{1,0:T(8,128)(2,1)} %get-tuple-element.21), channel_id=1, source_target_pairs={{0,4},{4,8},{8,12},{1,5},{5,9},{9,13},{2,6},{6,10},{10,14},{3,7},{... | collective-permute-start | bytes 233480 | tf_op jit(solution)/shard_map/ppermute | solution.py:653
  46.0 6.0 %collective-permute-start.1 = (bf16[128,128]{1,0:T(8,128)(2,1)}, bf16[128,128]{1,0:T(8,128)(2,1)S(1)}, u32[]{:S(2)}, u32[]{:S(2)}) collective-permute-start(bf16[128,128]{1,0:T(8,128)(2,1)} %get-tuple-element.22), channel_id=1, source_target_pairs={{4,0},{8,4},{12,8},{5,1},{9,5},{13,9},{6,2},{10,6},{14,10},{7,3},{... | collective-permute-start | bytes 98312 | tf_op jit(solution)/shard_map/ppermute | solution.py:653
  52.0 0.6 copy-start.7
  52.6 0.6 copy-start.4
  55.2 1.9 %collective-permute-start.2 = (bf16[88,384]{1,0:T(8,128)(2,1)}, bf16[88,384]{1,0:T(8,128)(2,1)S(1)}, u32[]{:S(2)}, u32[]{:S(2)}) collective-permute-start(bf16[88,384]{1,0:T(8,128)(2,1)} %get-tuple-element.23.refs_0_), channel_id=1, source_target_pairs={{0,1},{1,0},{2,3},{3,2},{4,5},{5,4},{6,7},{7,6},{8,9},{9,8},{10,11... | collective-permute-start | bytes 202760 | tf_op jit(solution)/shard_map/ppermute | solution.py:647
  55.2 10.7 %collective-permute-start.3 = (bf16[88,384]{1,0:T(8,128)(2,1)}, bf16[88,384]{1,0:T(8,128)(2,1)}, u32[]{:S(2)}, u32[]{:S(2)}) collective-permute-start(bf16[88,384]{1,0:T(8,128)(2,1)} %get-tuple-element.23.refs_0_), channel_id=1, source_target_pairs={{0,2},{1,3},{2,0},{3,1},{4,6},{5,7},{6,4},{7,5},{8,10},{9,11},{10,... | collective-permute-start | bytes 202760 | tf_op jit(solution)/shard_map/ppermute | solution.py:647
  56.7 9.3 %collective-permute-start.4 = (bf16[88,384]{1,0:T(8,128)(2,1)}, bf16[88,384]{1,0:T(8,128)(2,1)}, u32[]{:S(2)}, u32[]{:S(2)}) collective-permute-start(bf16[88,384]{1,0:T(8,128)(2,1)} %get-tuple-element.23.refs_0_), channel_id=1, source_target_pairs={{0,3},{1,2},{2,1},{3,0},{4,7},{5,6},{6,5},{7,4},{8,11},{9,10},{10,... | collective-permute-start | bytes 202760 | tf_op jit(solution)/shard_map/ppermute | solution.py:647
  57.1 0.6 copy-start.13
  57.7 29.1 %collective-permute-start.11 = (bf16[43,16,128]{2,1,0:T(8,128)(2,1)}, bf16[43,16,128]{2,1,0:T(8,128)(2,1)S(1)}, u32[]{:S(2)}, u32[]{:S(2)}) collective-permute-start(bf16[43,16,128]{2,1,0:T(8,128)(2,1)} %get-tuple-element.31), channel_id=1, source_target_pairs={{0,1},{1,2},{2,3},{4,5},{5,6},{6,7},{8,9},{9,10},{10,11},{12,13},{... | collective-permute-start | bytes 528392 | tf_op jit(solution)/shard_map/ppermute | solution.py:653
  65.9 6.9 %copy-start.21 = (bf16[43,8,128]{2,1,0:T(8,128)(2,1)S(1)}, bf16[43,8,128]{2,1,0:T(8,128)(2,1)}, u32[]{:S(2)}) copy-start(bf16[43,8,128]{2,1,0:T(8,128)(2,1)} %get-tuple-element.32) | copy-start | bytes 264196
  70.4 2.4 %collective-permute-start.5 = (bf16[272,128]{1,0:T(8,128)(2,1)}, bf16[272,128]{1,0:T(8,128)(2,1)S(1)}, u32[]{:S(2)}, u32[]{:S(2)}) collective-permute-start(bf16[272,128]{1,0:T(8,128)(2,1)} %get-tuple-element.24.refs_0_), channel_id=1, source_target_pairs={{0,1},{1,0},{2,3},{3,2},{4,5},{5,4},{6,7},{7,6},{8,9},{9,8},{10,11... | collective-permute-start | bytes 208904 | tf_op jit(solution)/shard_map/ppermute | solution.py:647
  71.7 4.5 %collective-permute-start.6 = (bf16[272,128]{1,0:T(8,128)(2,1)}, bf16[272,128]{1,0:T(8,128)(2,1)S(1)}, u32[]{:S(2)}, u32[]{:S(2)}) collective-permute-start(bf16[272,128]{1,0:T(8,128)(2,1)} %get-tuple-element.24.refs_0_), channel_id=1, source_target_pairs={{0,2},{1,3},{2,0},{3,1},{4,6},{5,7},{6,4},{7,5},{8,10},{9,11},{10,... | collective-permute-start | bytes 208904 | tf_op jit(solution)/shard_map/ppermute | solution.py:647
  72.8 7.8 %copy-start.9 = (bf16[272,128]{1,0:T(8,128)(2,1)}, bf16[272,128]{1,0:T(8,128)(2,1)S(1)}, u32[]{:S(2)}) copy-start(bf16[272,128]{1,0:T(8,128)(2,1)S(1)} %collective-permute-done.5.refs_1_) | copy-start | bytes 208900
  72.8 13.4 %collective-permute-start.12 = (bf16[43,8,128]{2,1,0:T(8,128)(2,1)S(1)}, bf16[43,8,128]{2,1,0:T(8,128)(2,1)S(1)}, u32[]{:S(2)}, u32[]{:S(2)}) collective-permute-start(bf16[43,8,128]{2,1,0:T(8,128)(2,1)S(1)} %copy-done.21), channel_id=1, source_target_pairs={{1,0},{2,1},{3,2},{5,4},{6,5},{7,6},{9,8},{10,9},{11,10},{13,12},{... | collective-permute-start | bytes 264200 | tf_op jit(solution)/shard_map/ppermute | solution.py:653
  76.2 4.4 %copy-start.10 = (bf16[272,128]{1,0:T(8,128)(2,1)}, bf16[272,128]{1,0:T(8,128)(2,1)S(1)}, u32[]{:S(2)}) copy-start(bf16[272,128]{1,0:T(8,128)(2,1)S(1)} %collective-permute-done.6.refs_2_) | copy-start | bytes 208900
  76.2 4.4 %collective-permute-start.7 = (bf16[272,128]{1,0:T(8,128)(2,1)}, bf16[272,128]{1,0:T(8,128)(2,1)S(1)}, u32[]{:S(2)}, u32[]{:S(2)}) collective-permute-start(bf16[272,128]{1,0:T(8,128)(2,1)} %get-tuple-element.24.refs_0_), channel_id=1, source_target_pairs={{0,3},{1,2},{2,1},{3,0},{4,7},{5,6},{6,5},{7,4},{8,11},{9,10},{10,... | collective-permute-start | bytes 208904 | tf_op jit(solution)/shard_map/ppermute | solution.py:647
  80.7 0.6 copy-start.11
  85.8 16.1 %collective-permute-start.10 = (bf16[104,128]{1,0:T(8,128)(2,1)}, bf16[104,128]{1,0:T(8,128)(2,1)S(1)}, u32[]{:S(2)}, u32[]{:S(2)}) collective-permute-start(bf16[104,128]{1,0:T(8,128)(2,1)} %get-tuple-element.30), channel_id=1, source_target_pairs={{0,3},{1,2},{2,1},{3,0},{4,7},{5,6},{6,5},{7,4},{8,11},{9,10},{10,... | collective-permute-start | bytes 79880 | tf_op jit(solution)/shard_map/ppermute | solution.py:647
  86.2 1.8 %copy-start.8 = (bf16[43,8,128]{2,1,0:T(8,128)(2,1)}, bf16[43,8,128]{2,1,0:T(8,128)(2,1)S(1)}, u32[]{:S(2)}) copy-start(bf16[43,8,128]{2,1,0:T(8,128)(2,1)S(1)} %collective-permute-done.12.refs_5_) | copy-start | bytes 264196
  86.2 15.7 %collective-permute-start.8 = (bf16[104,128]{1,0:T(8,128)(2,1)}, bf16[104,128]{1,0:T(8,128)(2,1)S(1)}, u32[]{:S(2)}, u32[]{:S(2)}) collective-permute-start(bf16[104,128]{1,0:T(8,128)(2,1)} %get-tuple-element.28), channel_id=1, source_target_pairs={{0,1},{1,0},{2,3},{3,2},{4,5},{5,4},{6,7},{7,6},{8,9},{9,8},{10,11... | collective-permute-start | bytes 79880 | tf_op jit(solution)/shard_map/ppermute | solution.py:647
  86.8 1.2 %copy-start.6 = (bf16[43,16,128]{2,1,0:T(8,128)(2,1)}, bf16[43,16,128]{2,1,0:T(8,128)(2,1)S(1)}, u32[]{:S(2)}) copy-start(bf16[43,16,128]{2,1,0:T(8,128)(2,1)S(1)} %collective-permute-done.11.refs_4_) | copy-start | bytes 528388
  86.8 15.1 %collective-permute-start.9 = (bf16[104,128]{1,0:T(8,128)(2,1)}, bf16[104,128]{1,0:T(8,128)(2,1)S(1)}, u32[]{:S(2)}, u32[]{:S(2)}) collective-permute-start(bf16[104,128]{1,0:T(8,128)(2,1)} %get-tuple-element.29), channel_id=1, source_target_pairs={{0,2},{1,3},{2,0},{3,1},{4,6},{5,7},{6,4},{7,5},{8,10},{9,11},{10,... | collective-permute-start | bytes 79880 | tf_op jit(solution)/shard_map/ppermute | solution.py:647
  88.0 1.0 copy-start.1
  89.0 1.0 copy-start.2
  101.9 0.6 copy-start.15
  101.9 0.6 copy-start.16
  102.0 0.6 copy-start.17

commit v2 on v1

v2 whole, which is shorter than its diff:
```python
import functools

import jax
import jax.numpy as jnp
from jax import lax
from jax.experimental import pallas as pl
from jax.experimental.pallas import tpu as pltpu
from jax.sharding import PartitionSpec as P


F32 = jnp.float32
BF16 = jnp.bfloat16
LANES = 128
BEFORE = (9, 5, 3, 2)
AFTER = 2


def up_to(value, multiple):
    return -(-value // multiple) * multiple


def dot(a, b):
    return jnp.dot(a.astype(BF16), b.astype(BF16), preferred_element_type=F32)


def iota(shape, dim):
    return lax.broadcasted_iota(jnp.int32, shape, dim)


def onehot(condition):
    return jnp.where(condition, 1.0, 0.0).astype(F32).astype(BF16)


def dot_t(a, b):
    return lax.dot_general(
        a.astype(BF16), b.astype(BF16), (((1,), (1,)), ((), ())), preferred_element_type=F32
    )


def conv(ref, height, breadth, row, col, weight_of):
    moved = []
    for q in range(3):
        block = ref[row : row + height + 2, col + q : col + q + breadth, :]
        moved.append(block.reshape((height + 2) * breadth, block.shape[2]).astype(BF16))
    wide = jnp.concatenate(moved, axis=1)
    size = height * breadth
    total = None
    for r in range(3):
        part = dot_t(wide[r * breadth : r * breadth + size], weight_of(r))
        total = part if total is None else total + part
    return total


def conv_strided(refs, height, breadth, row, col, lanes, weight_of):
    total = None
    for r in range(3):
        moved = []
        for q in range(3):
            block = wide_load(
                refs, pl.ds(row + r, height, stride=2), pl.ds(col + q, breadth, stride=2)
            )[:, :, lanes[0] : lanes[1]]
            moved.append(block.reshape(height * breadth, block.shape[2]).astype(BF16))
        part = dot_t(jnp.concatenate(moved, axis=1), weight_of(r))
        total = part if total is None else total + part
    return total


def third(kernel, first, last, start, channels):
    step = 3 * channels
    return lambda r: kernel[first:last, start + r * step : start + (r + 1) * step].astype(BF16)


def position():
    return lax.axis_index("rows"), lax.axis_index("cols")


def bias_row(bias_ref, line):
    for r in range(bias_ref.shape[0]):
        line[0:1, r * LANES : (r + 1) * LANES] = bias_ref[r : r + 1, :]


def wide_load(refs, rows, cols):
    parts = [ref[rows, cols, :] for ref in refs]
    return parts[0] if len(parts) == 1 else jnp.concatenate(parts, axis=2)


def wide_store(refs, rows, cols, value):
    channels = value.shape[2]
    for i, ref in enumerate(refs):
        part = value[:, :, i * LANES : min((i + 1) * LANES, channels)]
        if part.shape[2] < LANES:
            rest = jnp.zeros(part.shape[:2] + (LANES - part.shape[2],), part.dtype)
            part = jnp.concatenate([part, rest], axis=2)
        ref[rows, cols, :] = part


def inside(shape, row_first, row_count, col_first, col_count):
    rows = iota(shape, 0) + row_first
    cols = iota(shape, 1) + col_first
    return (rows >= 0) & (rows < row_count) & (cols >= 0) & (cols < col_count)


def rounded(value):
    return value.astype(BF16).astype(F32)


def vmem(count):
    return [pl.BlockSpec(memory_space=pltpu.VMEM)] * count


PARAMS = pltpu.CompilerParams(vmem_limit_bytes=56 * 1024 * 1024)


class RowLayout:
    def __init__(self, shapes, counts):
        self.counts = counts
        self.half = shapes[0][1] // 2
        self.start = []
        at = 0
        for level, ((_, breadth, channels), count) in enumerate(zip(shapes, counts)):
            self.start.append(at)
            positions = count * (self.half if level == 0 else breadth)
            at += positions * (1 if level == 0 else -(-channels // LANES))
        self.total = up_to(at, 16)


def pack_rows(layout, refs, firsts, scratch):
    one, two, three, four = refs
    count = layout.counts
    half = layout.half
    for part in range(2):
        block = one[firsts[0] : firsts[0] + count[0], part * half : (part + 1) * half, :]
        size = count[0] * half
        scratch[0:size, part * 64 : part * 64 + one.shape[2]] = block.astype(F32).reshape(size, -1)
    at = layout.start[1]
    size = count[1] * two.shape[1]
    block = two[firsts[1] : firsts[1] + count[1], :, :].astype(F32).reshape(size, two.shape[2])
    scratch[at : at + size, 0 : two.shape[2]] = block
    at = layout.start[2]
    size = count[2] * three.shape[1]
    block = three[firsts[2] : firsts[2] + count[2], :, :].astype(F32).reshape(size, three.shape[2])
    for low in range(0, three.shape[2], LANES):
        high = min(low + LANES, three.shape[2])
        scratch[at : at + size, 0 : high - low] = block[:, low:high]
        at += size
    breadth = four.shape[1]
    size = count[3] * breadth
    for row in range(count[3]):
        block = four[firsts[3] + row].astype(F32)
        at = layout.start[3] + row * breadth
        for low in range(0, four.shape[2], LANES):
            scratch[at : at + breadth, 0:LANES] = block[:, low : low + LANES]
            at += size


def rows_kernel(layouts, one, two, three, four, down_ref, up_ref, scratch):
    refs = (one, two, three, four)
    low, high = layouts
    firsts = tuple(ref.shape[0] - count for ref, count in zip(refs, low.counts))
    scratch[...] = jnp.zeros_like(scratch)
    pack_rows(low, refs, firsts, scratch)
    down_ref[...] = scratch[0 : low.total, :].astype(BF16)
    pack_rows(high, refs, (0, 0, 0, 0), scratch)
    up_ref[...] = scratch[0 : high.total, :].astype(BF16)


def stretch_fine(level, layout_pair, feat, top, bottom, target, col):
    low, high = layout_pair
    height, breadth, channels = feat.shape
    before, after = low.counts[level], high.counts[level]
    for layout, message, row, count in (
        (low, top, 0, before),
        (high, bottom, before + height, after),
    ):
        at = layout.start[level]
        if level == 0:
            half = layout.half
            for part in range(2):
                block = message[at : at + count * half, part * 64 : part * 64 + channels]
                target[row : row + count, col + part * half : col + (part + 1) * half, :] = (
                    block.astype(F32).reshape(count, half, channels)
                )
        else:
            block = message[at : at + count * breadth, 0:channels]
            target[row : row + count, col : col + breadth, :] = block.astype(F32).reshape(
                count, breadth, channels
            )
    target[before : before + height, col : col + breadth, :] = feat[...].astype(F32)


def columns_kernel(layouts, three, four, top, bottom, after, gather_ref, full_three, message):
    low, high = layouts
    breadth, channels = three.shape[1], three.shape[2]
    own = three.shape[0] * breadth
    before, after = low.counts[2] * breadth, high.counts[2] * breadth
    for layout, source, row, size in ((low, top, 0, before), (high, bottom, before + own, after)):
        at = layout.start[2]
        for first in range(0, channels, LANES):
            last = min(first + LANES, channels)
            full_three[row : row + size, first:last] = source[at : at + size, 0 : last - first].astype(F32)
            at += size
    full_three[before : before + own, :] = three[...].astype(F32).reshape(own, channels)
    size_four = gather_four(four.shape)
    breadth, channels4 = four.shape[1], four.shape[2]
    before, after = low.counts[3] * breadth, high.counts[3] * breadth
    for layout, source, row, size in (
        (low, top, 0, before),
        (high, bottom, before + four.shape[0] * breadth, after),
    ):
        at = layout.start[3]
        for first in range(0, channels4, LANES):
            message[row : row + size, first : first + LANES] = source[at : at + size, :].astype(F32)
            at += size
    for row in range(four.shape[0]):
        at = before + row * breadth
        message[at : at + breadth, 0:channels4] = four[row].astype(F32)
    total, head = gather_three(three.shape)
    message[size_four : size_four + head, 0:channels] = full_three[0:head, :]
    message[size_four : size_four + total - head, channels : 2 * channels] = full_three[head:total, :]
    gather_ref[...] = message[...].astype(BF16)


def edges_kernel(layouts, one, two, top, bottom, after, right_ref, left_ref, full_one, full_two, edge):
    stretch_fine(0, layouts, one, top, bottom, full_one, 0)
    stretch_fine(1, layouts, two, top, bottom, full_two, 0)
    wide, wide_two = one.shape[1], two.shape[1]
    left, left_two = BEFORE[0], BEFORE[1]
    rows_two = full_two.shape[0]
    edge[:, 0:left, 0 : one.shape[2]] = full_one[:, wide - left : wide, :]
    edge[0:rows_two, left : left + left_two, 0 : two.shape[2]] = full_two[
        :, wide_two - left_two : wide_two, :
    ]
    right_ref[...] = edge[...].astype(BF16)
    edge[:, 0:AFTER, 0 : one.shape[2]] = full_one[:, 0:AFTER, :]
    edge[0:rows_two, AFTER : 2 * AFTER, 0 : two.shape[2]] = full_two[:, 0:AFTER, :]
    left_ref[...] = edge[:, 0:8, :].astype(BF16)


def gather_four(shape):
    return (shape[0] + BEFORE[3] + AFTER) * shape[1]


def gather_three(shape):
    total = (shape[0] + BEFORE[2] + AFTER) * shape[1]
    return total, up_to(-(-total // 2), 8)


def own_channels(me, channels, own):
    return onehot(iota((channels, own), 0) == iota((channels, own), 1) + me * own)


def own_bias(line, first, me, own, count):
    total = None
    for j in range(count):
        part = jnp.where(me == j, line[0:1, first + j * own : first + (j + 1) * own], 0.0)
        total = part if total is None else total + part
    return total


def spread(target, blocks, me, rows, block_cols):
    shift = block_cols.bit_length() - 1
    width = target.shape[1]
    total = None
    for k, block in enumerate(blocks):
        size = block.shape[0]
        shape = (rows, width, size)
        source = iota(shape, 2)
        slot = (me ^ k) * block_cols + 1 + (source & (block_cols - 1))
        choose = ((source >> shift) == iota(shape, 0)) & (iota(shape, 1) == slot)
        part = dot(onehot(choose).reshape(rows * width, size), block)
        total = part if total is None else total + part
    target[...] = total.reshape(rows, width, total.shape[1])


def coarse_first_kernel(sizes, *refs):
    count, rows_all, high3, wide3, chan3, high4, wide4, chan4, bias3, bias4 = sizes
    blocks = refs[:count]
    conv3, conv4, bias_ref, _, out, res3, res4, full3, full4, message, line = refs[count:]
    row, me = position()
    bias_row(bias_ref, line)
    size4 = gather_four((high4, wide4))
    total3, head = gather_three((high3, wide3))
    spread(full4, [b[0:size4, 0:chan4] for b in blocks], me, high4 + BEFORE[3] + AFTER, wide4)
    parts = []
    for b in blocks:
        parts.append(
            jnp.concatenate(
                [
                    b[size4 : size4 + head, 0:chan3].astype(F32),
                    b[size4 : size4 + total3 - head, chan3 : 2 * chan3].astype(F32),
                ],
                axis=0,
            )
        )
    spread(full3, parts, me, high3 + BEFORE[2] + AFTER, wide3)
    heights = []
    for full, kernel, high, wide, chan, before, base in (
        (full3, conv3, high3, wide3, chan3, BEFORE[2], bias3),
        (full4, conv4, high4, wide4, chan4, BEFORE[3], bias4),
    ):
        own = chan // count
        out_high = high + before + AFTER - 2
        out_wide = wide * count
        mid = conv(full, out_high, out_wide, 0, 0, third(kernel, 0, own, 0, chan))
        mid = jax.nn.relu(mid + own_bias(line, base, me, own, count)).reshape(out_high, out_wide, own)
        rows = iota(mid.shape, 0) + row * high - (before - 1)
        valid = (rows >= 0) & (rows < rows_all * high)
        heights.append(jnp.where(valid, mid, 0.0).reshape(out_high * out_wide, own))
    mid3, mid4 = heights
    half = mid3.shape[0] // 2
    own3, own4 = mid3.shape[1], mid4.shape[1]
    message[0:half, 0:own3] = mid3[0:half]
    message[0:half, 64 : 64 + own3] = mid3[half:]
    message[half : half + mid4.shape[0], 0:own4] = mid4
    out[...] = message[...].astype(BF16)
    skip3 = BEFORE[2] - 1
    keep = full3[skip3 : skip3 + high3 + 1, 1 : 1 + wide3 * count, :].reshape(-1, chan3)
    res3[...] = dot(keep, own_channels(me, chan3, own3)).astype(BF16)
    keep = full4[BEFORE[3] : BEFORE[3] + high4, 1 : 1 + wide4 * count, :].reshape(-1, chan4)
    res4[...] = dot(keep, own_channels(me, chan4, own4)).astype(BF16)


def natural(blocks, me, own, channels):
    total = None
    for k, block in enumerate(blocks):
        place = onehot(iota((own, channels), 1) == iota((own, channels), 0) + (me ^ k) * own)
        part = dot(block, place)
        total = part if total is None else total + part
    return total


def message_rows(sizes):
    count, _, high3, wide3, _, high4, wide4, _, _, _ = sizes
    half = (high3 + BEFORE[2] + AFTER - 2) * wide3 * count // 2
    return half, half + (high4 + BEFORE[3] + AFTER - 2) * wide4 * count


def coarse_second_kernel(sizes, *refs):
    count, rows_all, high3, wide3, chan3, high4, wide4, chan4, bias3, bias4 = sizes
    blocks = refs[:count]
    res3, res4, conv3, conv4, bias_ref, _ = refs[count : count + 6]
    outs = refs[count + 6 : 2 * count + 6]
    full3, full4, message, line = refs[2 * count + 6 :]
    row, me = position()
    bias_row(bias_ref, line)
    own3, own4 = chan3 // count, chan4 // count
    half, last = message_rows(sizes)
    mids3 = [
        jnp.concatenate([b[0:half, 0:own3].astype(F32), b[0:half, 64 : 64 + own3].astype(F32)], axis=0)
        for b in blocks
    ]
    mids4 = [b[half:last, 0:own4] for b in blocks]
    results = []
    for full, mids, kernel, res, high, wide, chan, before, base, extra in (
        (full3, mids3, conv3, res3, high3, wide3, chan3, BEFORE[2], bias3, 1),
        (full4, mids4, conv4, res4, high4, wide4, chan4, BEFORE[3], bias4, 0),
    ):
        own = chan // count
        mid_high = high + before + AFTER - 2
        out_wide = wide * count
        full[...] = jnp.zeros_like(full)
        full[:, 1 : 1 + out_wide, :] = natural(mids, me, own, chan).reshape(mid_high, out_wide, chan)
        out_high = high + extra
        first = 9 * chan
        y = conv(full, out_high, out_wide, 0, 0, third(kernel, 0, own, first, chan))
        y = y + own_bias(line, base + chan, me, own, count) + res[...].astype(F32)
        y = jax.nn.relu(y).reshape(out_high, out_wide, own)
        rows = iota(y.shape, 0) + row * high - extra
        y = jnp.where((rows >= 0) & (rows < rows_all * high), y, 0.0)
        results.append(y.reshape(out_high * out_wide, own))
    y3, y4 = results
    for k, out in enumerate(outs):
        target = me ^ k
        wide = wide3 * count
        shape = (high3 + 1, 16, y3.shape[0])
        source = iota(shape, 2)
        slot = iota(shape, 1)
        choose = (
            ((source >> (wide.bit_length() - 1)) == iota(shape, 0))
            & ((source & (wide - 1)) == target * wide3 - 1 + slot)
            & (slot < wide3 + 1)
        )
        part = dot(onehot(choose).reshape((high3 + 1) * 16, -1), y3)
        cut = part.shape[0] // 2
        message[0:cut, 0:own3] = part[0:cut]
        message[0:cut, 64 : 64 + own3] = part[cut:]
        wide = wide4 * count
        shape = (high4, 8, y4.shape[0])
        source = iota(shape, 2)
        slot = iota(shape, 1)
        choose = (
            ((source >> (wide.bit_length() - 1)) == iota(shape, 0))
            & ((source & (wide - 1)) == target * wide4 + slot)
            & (slot < wide4)
        )
        part = dot(onehot(choose).reshape(high4 * 8, -1), y4)
        message[cut : cut + high4 * 8, 0:own4] = part
        out[...] = message[...].astype(BF16)


class Packing:
    def __init__(self, shapes):
        self.place = {}
        at = 0
        for name, (rows, width) in shapes.items():
            pad = up_to(width, 16)
            self.place[name] = (at, pad, width, rows)
            at += pad * -(-rows // LANES)
        self.total = at

    def tiles(self, name):
        at, pad, width, rows = self.place[name]
        for low in range(0, rows, LANES):
            yield at + low // LANES * pad, width, low, min(LANES, rows - low)

    def span(self, names):
        ends = [(self.place[n][0], self.place[n][0] + self.place[n][1] * -(-self.place[n][3] // LANES)) for n in names]
        return min(e[0] for e in ends), max(e[1] for e in ends)

    def scratch(self, name, count):
        _, _, width, rows = self.place[name]
        return pltpu.VMEM((width * count, rows), BF16 if width % 16 == 0 else F32)

    def unpack(self, name, stacked, base, target):
        for j in range(stacked.shape[0]):
            for at, width, low, size in self.tiles(name):
                target[j * width : (j + 1) * width, low : low + size] = stacked[
                    j, at - base : at - base + width, 0:size
                ].astype(target.dtype)


def pack_kernel(packings, *refs):
    inputs = sum(len(p.place) for p in packings)
    sources, outs = iter(refs[:inputs]), refs[inputs + 1 :]
    for packing, out in zip(packings, outs):
        for name in packing.place:
            source = next(sources)
            for at, width, low, size in packing.tiles(name):
                out[at : at + width, 0:size] = source[:, low : low + size]


def fetch(span, me, buffers, stacked, semaphores):
    copies = []
    for k, buffer in enumerate(buffers):
        copy = pltpu.make_async_copy(
            buffer.at[pl.ds(span[0], span[1] - span[0])], stacked.at[me ^ k], semaphores.at[k]
        )
        copy.start()
        copies.append(copy)
    return copies


def fine_kernel(plan, *refs):
    packing, layouts, count, rows_all, unit = plan
    one, two, top, bottom, from_left, from_right, bias_ref, _ = refs[:8]
    buffers = refs[8 : 8 + count]
    y1_ref, y2_ref, v1, v2 = refs[8 + count : 12 + count]
    x1, m1, x2, m2, k1, k2, stacked, line, semaphores = refs[12 + count :]
    row, me = position()
    copies = fetch((0, packing.total), me, buffers, stacked, semaphores)
    bias_row(bias_ref, line)
    high1, wide1, chan1 = one.shape
    high2, wide2, chan2 = two.shape
    stretch_fine(0, layouts, one, top, bottom, x1, 16)
    stretch_fine(1, layouts, two, top, bottom, x2, 16)
    b1, b2 = BEFORE[0], BEFORE[1]
    rows2 = high2 + b2 + AFTER
    x1[:, 16 - b1 : 16, :] = from_left[:, 0:b1, 0:chan1].astype(F32)
    x1[:, 16 + wide1 : 16 + wide1 + AFTER, :] = from_right[:, 0:AFTER, 0:chan1].astype(F32)
    x2[:, 16 - b2 : 16, :] = from_left[0:rows2, b1 : b1 + b2, 0:chan2].astype(F32)
    x2[:, 16 + wide2 : 16 + wide2 + AFTER, :] = from_right[
        0:rows2, AFTER : 2 * AFTER, 0:chan2
    ].astype(F32)
    for copy in copies:
        copy.wait()
    packing.unpack("conv_one", stacked, 0, k1)
    packing.unpack("conv_two", stacked, 0, k2)
    ys = []
    for x, m, v, k, before, high, wide, chan, base in (
        (x1, m1, v1, k1, b1, high1, wide1, chan1, 0),
        (x2, m2, v2, k2, b2, high2, wide2, chan2, 2 * unit),
    ):
        mid_high = high + before
        mid_wide = up_to(wide + before, 16)
        mid = conv(x, mid_high, mid_wide, 0, 16 - before, third(k, 0, chan, 0, chan))
        mid = jax.nn.relu(mid + line[0:1, base : base + chan]).reshape(mid_high, mid_wide, chan)
        ok = inside(
            mid.shape, row * high - before + 1, rows_all * high, me * wide - before + 1, count * wide
        )
        m[:, 0:mid_wide, :] = rounded(jnp.where(ok, mid, 0.0))
        y_high = high + before - 2
        y_wide = up_to(wide + before - 2, 16)
        y = conv(m, y_high, y_wide, 0, 0, third(k, 0, chan, 9 * chan, chan))
        y = y + line[0:1, base + chan : base + 2 * chan]
        y = y.reshape(y_high, y_wide, chan) + x[2 : 2 + y_high, 18 - before : 18 - before + y_wide, :]
        skip = before - 2
        ok = inside(y.shape, row * high - skip, rows_all * high, me * wide - skip, count * wide)
        v[:, 0:y_wide, 0:chan] = rounded(jnp.where(ok, jax.nn.relu(y), 0.0))
        ys.append(v[skip : skip + high, skip : skip + wide, 0:chan].astype(BF16))
    y1_ref[...] = ys[0]
    y2_ref[...] = ys[1]


def down_kernel(plan, *refs):
    packing, count, rows_all, unit, offs, shapes = plan
    v1, v2, bias_ref, _ = refs[:4]
    buffers = refs[4 : 4 + count]
    d12_ref, d3_ref, d4_ref = refs[4 + count : 7 + count]
    t1, tb, s12, t2, s3, g1, g2, stacked, line, semaphores = refs[7 + count :]
    row, me = position()
    span = packing.span(("down_one", "down_two"))
    copies = fetch(span, me, buffers, stacked, semaphores)
    bias_row(bias_ref, line)
    for copy in copies:
        copy.wait()
    packing.unpack("down_one", stacked, span[0], g1)
    packing.unpack("down_two", stacked, span[0], g2)
    (high1, wide1, _), (_, _, chan2) = shapes[:2]
    off1, off2 = offs[0], offs[1]
    half_high, half_wide = high1 // 2, wide1 // 2
    out_high, out_wide = half_high + 3, up_to(half_wide + 3, 8)
    first = conv_strided((v1,), out_high, out_wide, 0, 0, (0, unit), third(g1, 0, 4 * unit, 0, unit))
    first = first + line[0:1, off1 : off1 + 4 * unit]
    s12[...] = first[:, 0 : 2 * unit].reshape(out_high, out_wide, 2 * unit)
    d12_ref[...] = s12[3 : 3 + half_high, 3 : 3 + half_wide, :]
    t = jax.nn.relu(first[:, 2 * unit : 4 * unit]).reshape(out_high, out_wide, 2 * unit)
    ok = inside(t.shape, row * half_high - 3, rows_all * half_high, me * half_wide - 3, count * half_wide)
    t1[:, 0:out_wide, 0 : 2 * unit] = rounded(jnp.where(ok, t, 0.0))
    quarter_high, quarter_wide = half_high // 2, half_wide // 2
    d13 = conv_strided(
        (t1,), quarter_high, quarter_wide, 2, 2, (0, unit), third(g1, 4 * unit, 8 * unit, 0, unit)
    )
    d13 = d13 + line[0:1, off1 + 4 * unit : off1 + 8 * unit]
    q_high, q_wide = quarter_high + 1, up_to(quarter_wide + 1, 8)
    t14b = conv_strided((t1,), q_high, q_wide, 0, 0, (unit, 2 * unit), third(g1, 8 * unit, 9 * unit, 0, unit))
    t14b = jax.nn.relu(t14b + line[0:1, off1 + 8 * unit : off1 + 9 * unit]).reshape(q_high, q_wide, unit)
    q_args = (row * quarter_high - 1, rows_all * quarter_high, me * quarter_wide - 1, count * quarter_wide)
    tb[:, 0:q_wide, 0:unit] = rounded(jnp.where(inside(t14b.shape, *q_args), t14b, 0.0))
    e_high, e_wide = quarter_high // 2, 8
    d14 = conv_strided((tb,), e_high, e_wide, 0, 0, (0, unit), third(g1, 9 * unit, 17 * unit, 0, unit))
    d14 = d14 + line[0:1, off1 + 9 * unit : off1 + 17 * unit]
    second = conv_strided((v2,), q_high, q_wide, 0, 0, (0, chan2), third(g2, 0, 6 * unit, 0, chan2))
    second = second + line[0:1, off2 : off2 + 6 * unit]
    s3[...] = second[:, 0 : 4 * unit].reshape(q_high, q_wide, 4 * unit)
    d3_ref[...] = d13.reshape(quarter_high, quarter_wide, 4 * unit) + s3[
        1 : 1 + quarter_high, 1 : 1 + quarter_wide, :
    ]
    t24 = jax.nn.relu(second[:, 4 * unit : 6 * unit]).reshape(q_high, q_wide, 2 * unit)
    t2[:, 0:q_wide, 0 : 2 * unit] = rounded(jnp.where(inside(t24.shape, *q_args), t24, 0.0))
    d24 = conv_strided((t2,), e_high, e_wide, 0, 0, (0, 2 * unit), third(g2, 6 * unit, 14 * unit, 0, chan2))
    d24 = d24 + line[0:1, off2 + 6 * unit : off2 + 14 * unit]
    d4_ref[...] = (d14 + d24).reshape(e_high, e_wide, 8 * unit)


LAST = ("down_three", "lift_two", "lift_three", "lift_four")


def join_kernel(plan, *refs):
    packing, count, unit, offs, shapes = plan
    blocks = refs[:count]
    y1_ref, y2_ref, d12_ref, d3_ref, d4_ref, bias_ref = refs[count : count + 6]
    buffers = refs[count + 6 : 2 * count + 6]
    out1, out2, out3, out4 = refs[2 * count + 6 : 2 * count + 10]
    (v3a, v3b, a2, a3a, a3b, a1, p2, p1, c3, k3, l2, l3, l4, stacked, line, semaphores) = refs[2 * count + 10 :]
    _, me = position()
    span = packing.span(LAST)
    copies = fetch(span, me, buffers, stacked, semaphores)
    bias_row(bias_ref, line)
    (high2, wide2, chan2), (high3, wide3, chan3), (high4, wide4, chan4) = shapes[1:]
    own3, own4 = chan3 // count, chan4 // count
    cut = (high3 + 1) * 8
    parts = [
        jnp.concatenate([b[0:cut, 0:own3].astype(F32), b[0:cut, 64 : 64 + own3].astype(F32)], axis=0)
        for b in blocks
    ]
    whole3 = natural(parts, me, own3, chan3).reshape(high3 + 1, 16, chan3)
    v3 = (v3a, v3b)
    wide_store(v3, slice(None), slice(0, 16), whole3)
    y4 = natural([b[cut : cut + high4 * 8, 0:own4] for b in blocks], me, own4, chan4)
    y3 = wide_load(v3, slice(1, 1 + high3), slice(1, 1 + wide3))[:, :, 0:chan3]
    for copy in copies:
        copy.wait()
    groups3, groups4 = (unit, 2 * unit), (unit, 2 * unit, 4 * unit)
    for name, target in zip(LAST, (k3, l2, l3, l4)):
        packing.unpack(name, stacked, span[0], target)
    off3, offl2, offl3, offl4 = offs[2:]

    def lifted(flat, kernel, groups, offset):
        values, first = [], 0
        for group in groups:
            value = dot_t(flat, kernel[first : first + group, :])
            values.append(value + line[0:1, offset + first : offset + first + group])
            first += group
        return values

    def double(scratch, value, keep):
        high, wide, channels = value.shape
        for r in range(2):
            for q in range(2):
                wide_store(scratch, pl.ds(r, high, stride=2), pl.ds(q, wide, stride=2), value)
        return wide_load(scratch, slice(0, 2 * high), slice(0, keep))[:, :, 0:channels]

    u4 = [u.reshape(high4, 8, -1) for u in lifted(y4, l4, groups4, offl4)]
    u3 = [u.reshape(high3, wide3, -1) for u in lifted(y3.reshape(high3 * wide3, chan3), l3, groups3, offl3)]
    y2 = y2_ref[...]
    (u2,) = lifted(y2.reshape(high2 * wide2, chan2), l2, (unit,), offl2)
    d34 = conv_strided(v3, high4, 8, 0, 0, (0, chan3), third(k3, 0, chan4, 0, chan3))
    d34 = d34 + line[0:1, off3 : off3 + chan4]
    four = jax.nn.relu(d4_ref[...] + (d34 + y4).reshape(high4, 8, chan4))
    c3[...] = four
    out4[...] = c3[:, 0:wide4, :].astype(BF16)
    three = double((a3a, a3b), u4[2], wide3) + d3_ref[...] + y3
    out3[...] = jax.nn.relu(three).astype(BF16)
    two = double((a2,), u4[1], wide3) + u3[1]
    two = double((p2,), two, wide2) + d12_ref[...] + y2.astype(F32)
    out2[...] = jax.nn.relu(two).astype(BF16)
    fine = double((a1,), u4[0], wide3) + u3[0]
    fine = double((p1,), fine, wide2) + u2.reshape(high2, wide2, unit)
    fine = double((p1,), fine, shapes[0][1]) + y1_ref[...].astype(F32)
    out1[...] = jax.nn.relu(fine).astype(BF16)


def offsets(width):
    start = 30 * width
    return (
        start,
        start + 17 * width,
        start + 31 * width,
        start + 39 * width,
        start + 40 * width,
        start + 43 * width,
    )


def flipped(value, mask, count):
    return lax.ppermute(value, "cols", [(i, i ^ mask) for i in range(count)])


def shifted(value, axis, distance):
    count = lax.axis_size(axis)
    route = [(i, i + distance) for i in range(count) if 0 <= i + distance < count]
    return lax.ppermute(value, axis, route)


def exchanged(value, count):
    return [value] + [flipped(value, mask, count) for mask in range(1, count)]


def gathered(value, count):
    held = {0: value}
    for b in range(1, count.bit_length() - 1):
        for mask in list(held):
            held[mask | 1 << b] = flipped(held[mask], 1 << b, count)
    if count > 1:
        for mask in list(held):
            held[mask | 1] = flipped(held[mask], 1, count)
    return [held[mask] for mask in range(count)]


def local(kernel, cost, outs, scratch, operands, anywhere=()):
    return pl.pallas_call(
        kernel,
        out_shape=list(outs),
        in_specs=vmem(len(operands)) + [pl.BlockSpec(memory_space=pl.ANY)] * len(anywhere),
        out_specs=vmem(len(outs)),
        scratch_shapes=scratch,
        compiler_params=PARAMS,
        cost_estimate=pl.CostEstimate(flops=int(cost * 1.15e9), bytes_accessed=0, transcendentals=0),
    )(*operands, *anywhere)


def on_device(
    feat_one,
    feat_two,
    feat_three,
    feat_four,
    conv_one,
    conv_two,
    conv_three,
    conv_four,
    down_one,
    down_two,
    down_three,
    lift_two,
    lift_three,
    lift_four,
    biases,
):
    count = lax.axis_size("cols")
    row_total = lax.axis_size("rows")
    feats = (feat_one, feat_two, feat_three, feat_four)
    shapes = tuple(f.shape for f in feats)
    unit = feat_one.shape[2]
    offs = offsets(unit)
    lines = biases.shape[0] // LANES
    bias = biases.reshape(lines, LANES)
    line = pltpu.VMEM((8, lines * LANES), F32)
    layouts = (RowLayout(shapes, BEFORE), RowLayout(shapes, (AFTER,) * 4))
    most = max(layouts[0].total, layouts[1].total)
    down, up = local(
        functools.partial(rows_kernel, layouts),
        1.5,
        [jax.ShapeDtypeStruct((l.total, LANES), BF16) for l in layouts],
        [pltpu.VMEM((most, LANES), F32)],
        feats,
    )
    top = shifted(down, "rows", 1)
    bottom = shifted(up, "rows", -1)

    early = {"conv_one": conv_one, "conv_two": conv_two}
    late = {
        "down_one": down_one,
        "down_two": down_two,
        "down_three": down_three,
        "lift_two": lift_two,
        "lift_three": lift_three,
        "lift_four": lift_four,
    }
    packings = [Packing({name: w.shape for name, w in group.items()}) for group in (early, late)]
    packed = local(
        functools.partial(pack_kernel, packings),
        1.5,
        [jax.ShapeDtypeStruct((p.total, LANES), BF16) for p in packings],
        [],
        [w.T for group in (early, late) for w in group.values()],
        [down],
    )
    early_buffers = gathered(packed[0], count)

    (high1, wide1, chan1), (high2, wide2, chan2), (high3, wide3, chan3), (high4, wide4, chan4) = shapes
    size4 = gather_four(shapes[3])
    total3, head3 = gather_three(shapes[2])
    lanes = max(chan4, 2 * chan3)
    rows1 = high1 + BEFORE[0] + AFTER
    rows2 = high2 + BEFORE[1] + AFTER
    (gather,) = local(
        functools.partial(columns_kernel, layouts),
        1.0,
        [jax.ShapeDtypeStruct((size4 + head3, lanes), BF16)],
        [pltpu.VMEM((total3, chan3), F32), pltpu.VMEM((size4 + head3, lanes), F32)],
        (feat_three, feat_four, top, bottom),
        [packed[1]],
    )
    coarse = exchanged(gather, count)
    to_right, to_left = local(
        functools.partial(edges_kernel, layouts),
        1.5,
        [jax.ShapeDtypeStruct((rows1, 16, LANES), BF16), jax.ShapeDtypeStruct((rows1, 8, LANES), BF16)],
        [
            pltpu.VMEM((rows1, wide1, chan1), F32),
            pltpu.VMEM((rows2, wide2, chan2), F32),
            pltpu.VMEM((rows1, 16, LANES), F32),
        ],
        (feat_one, feat_two, top, bottom),
        [gather],
    )
    from_left = shifted(to_right, "cols", 1)
    from_right = shifted(to_left, "cols", -1)

    sizes = (count, row_total, high3, wide3, chan3, high4, wide4, chan4, 6 * unit, 14 * unit)
    own3, own4 = chan3 // count, chan4 // count
    _, last = message_rows(sizes)
    full_wide3, full_wide4 = up_to(wide3 * count + 2, 8), up_to(wide4 * count + 2, 8)
    three_t, four_t = conv_three.T, conv_four.T
    mid, res3, res4 = local(
        functools.partial(coarse_first_kernel, sizes),
        3.0,
        [
            jax.ShapeDtypeStruct((last, LANES), BF16),
            jax.ShapeDtypeStruct(((high3 + 1) * wide3 * count, own3), BF16),
            jax.ShapeDtypeStruct((high4 * wide4 * count, own4), BF16),
        ],
        [
            pltpu.VMEM((high3 + BEFORE[2] + AFTER, full_wide3, chan3), F32),
            pltpu.VMEM((high4 + BEFORE[3] + AFTER, full_wide4, chan4), F32),
            pltpu.VMEM((last, LANES), F32),
            line,
        ],
        (*coarse, three_t, four_t, bias),
        [to_right],
    )
    mids = exchanged(mid, count)

    mid_wide1, mid_wide2 = up_to(wide1 + BEFORE[0], 16), up_to(wide2 + BEFORE[1], 16)
    y_wide1, y_wide2 = up_to(wide1 + BEFORE[0] - 2, 16), up_to(wide2 + BEFORE[1] - 2, 16)
    half_wide = up_to(wide1 // 2 + 3, 8)
    quarter_wide = up_to(wide1 // 4 + 1, 8)
    y1, y2, v1, v2 = local(
        functools.partial(fine_kernel, (packings[0], layouts, count, row_total, unit)),
        5.0,
        [
            jax.ShapeDtypeStruct(shapes[0], BF16),
            jax.ShapeDtypeStruct(shapes[1], BF16),
            jax.ShapeDtypeStruct((high1 + BEFORE[0] - 2, max(2 * half_wide, y_wide1) + 8, LANES), F32),
            jax.ShapeDtypeStruct((high2 + BEFORE[1] - 2, max(2 * quarter_wide, y_wide2) + 8, LANES), F32),
        ],
        [
            pltpu.VMEM((rows1, 24 + mid_wide1, chan1), F32),
            pltpu.VMEM((high1 + BEFORE[0], max(mid_wide1, y_wide1) + 8, chan1), F32),
            pltpu.VMEM((rows2, 24 + mid_wide2, chan2), F32),
            pltpu.VMEM((high2 + BEFORE[1], max(mid_wide2, y_wide2) + 8, chan2), F32),
            packings[0].scratch("conv_one", count),
            packings[0].scratch("conv_two", count),
            pltpu.VMEM((count, packings[0].total, LANES), BF16),
            line,
            pltpu.SemaphoreType.DMA((count,)),
        ],
        (feat_one, feat_two, top, bottom, from_left, from_right, bias),
        [mid, *early_buffers],
    )

    message = (high3 + 1) * 8 + high4 * 8
    sent = local(
        functools.partial(coarse_second_kernel, sizes),
        3.0,
        [jax.ShapeDtypeStruct((message, LANES), BF16)] * count,
        [
            pltpu.VMEM((high3 + BEFORE[2] + AFTER - 2, full_wide3, chan3), F32),
            pltpu.VMEM((high4 + BEFORE[3] + AFTER - 2, full_wide4, chan4), F32),
            pltpu.VMEM((message, LANES), F32),
            line,
        ],
        (*mids, res3, res4, three_t, four_t, bias),
        [y1],
    )
    coarse_out = [sent[0]] + [flipped(sent[mask], mask, count) for mask in range(1, count)]
    late_buffers = gathered(packed[1], count)

    span = packings[1].span(("down_one", "down_two"))
    downs = local(
        functools.partial(down_kernel, (packings[1], count, row_total, unit, offs, shapes)),
        5.0,
        [
            jax.ShapeDtypeStruct((high1 // 2, wide1 // 2, 2 * unit), F32),
            jax.ShapeDtypeStruct((high1 // 4, wide1 // 4, 4 * unit), F32),
            jax.ShapeDtypeStruct((high1 // 8, 8, 8 * unit), F32),
        ],
        [
            pltpu.VMEM((high1 // 2 + 3, max(2 * quarter_wide, half_wide) + 8, LANES), F32),
            pltpu.VMEM((high1 // 4 + 1, max(16, quarter_wide) + 8, LANES), F32),
            pltpu.VMEM((high1 // 2 + 3, half_wide, 2 * unit), F32),
            pltpu.VMEM((high1 // 4 + 1, max(16, quarter_wide) + 8, LANES), F32),
            pltpu.VMEM((high1 // 4 + 1, quarter_wide, 4 * unit), F32),
            packings[1].scratch("down_one", count),
            packings[1].scratch("down_two", count),
            pltpu.VMEM((count, span[1] - span[0], LANES), BF16),
            line,
            pltpu.SemaphoreType.DMA((count,)),
        ],
        (v1, v2, bias),
        [sent[0], *late_buffers],
    )

    span = packings[1].span(LAST)
    return tuple(
        local(
            functools.partial(join_kernel, (packings[1], count, unit, offs, shapes)),
            4.0,
            [jax.ShapeDtypeStruct(shape, BF16) for shape in shapes],
            [
                pltpu.VMEM((high3 + 1, 24, LANES), F32),
                pltpu.VMEM((high3 + 1, 24, LANES), F32),
                pltpu.VMEM((2 * high4, 16, LANES), F32),
                pltpu.VMEM((2 * high4, 16, LANES), F32),
                pltpu.VMEM((2 * high4, 16, LANES), F32),
                pltpu.VMEM((2 * high4, 16, LANES), F32),
                pltpu.VMEM((high2, wide2, LANES), F32),
                pltpu.VMEM((high1, wide1, LANES), F32),
                pltpu.VMEM((high4, 8, chan4), F32),
                *[packings[1].scratch(name, count) for name in LAST],
                pltpu.VMEM((count, span[1] - span[0], LANES), BF16),
                line,
                pltpu.SemaphoreType.DMA((count,)),
            ],
            (*coarse_out, y1, y2, *downs, bias),
            late_buffers,
        )
    )


def solution(mesh):
    spatial = P(("win", "rows"), "cols", None)
    placed = (spatial,) * 4 + (P(None, "cols"),) * 10 + (P(),)
    return jax.shard_map(
        on_device,
        mesh=mesh,
        in_specs=placed,
        out_specs=(spatial,) * 4,
        check_vma=False,
    )
```

time: 108 us -> 74.9 us (0.69)
  waiting for transfers between devices: 36.9 us -> 15.9 us
  local copies, waits for them, and re-layouts: 19.3 us -> 4.4 us
  starting transfers between devices: 17.1 us -> 20.3 us
    ppermute x12 -> x15, waiting for transfers between devices: 32.2 us -> 11.5 us  [flipped(): return lax.ppermute(value, 'cols', [(i, i ^ mask) for i in range(count)])]
    unnamed x54 -> x44, local copies, waits for them, and re-layouts: 18.7 us -> 4.4 us
    ppermute x12 -> x15, starting transfers between devices: 8.46 us -> 11.2 us  [flipped(): return lax.ppermute(value, 'cols', [(i, i ^ mask) for i in range(count)])]
    pallas_call x7 -> x9, Pallas kernels: 32.9 us -> 32.9 us  [local(): pl.pallas_call(kernel, out_shape=list(outs), in_specs=vmem(len(operands))...]
  transfers between devices with their start and end apart: 16 -> 19, of which waited for: 5 -> 2; matrix products, arithmetic and copies ran while one was open for 6% -> 0% of each run, Pallas kernels for 23% -> 33%
where the time goes in v2:
time: 74.9 us; the launch traced here: 74.4 us
  Pallas kernels  32.9 us (44%)
  starting transfers between devices  20.3 us (27%)
  waiting for transfers between devices  15.9 us (21%)
  local copies, waits for them, and re-layouts  4.4 us (6%)
  between operations  0.88 us (1%)
    pallas_call x9, Pallas kernels, local(): pl.pallas_call(kernel, out_shape=list(outs), in_specs=vmem(len(operands))...  32.9 us
    ppermute x15, waiting for transfers between devices, flipped(): return lax.ppermute(value, 'cols', [(i, i ^ mask) for i in range(count)])  11.5 us
    ppermute x15, starting transfers between devices, flipped(): return lax.ppermute(value, 'cols', [(i, i ^ mask) for i in range(count)])  11.2 us
    ppermute x4, starting transfers between devices, shifted(): return lax.ppermute(value, axis, route)  9.07 us
    ppermute x4, waiting for transfers between devices, shifted(): return lax.ppermute(value, axis, route)  4.44 us
    unnamed x44, local copies, waits for them, and re-layouts  4.4 us
  transfers between devices with their start and end apart: 19, of which 2 were waited for; matrix products, arithmetic and copies ran while one was open for 0% of the time, Pallas kernels for 33%

profile of v2, /device:TPU:0, one launch (start us, length us, event | category | flops | bytes accessed | tf_op | source)
XLA Modules:
  0.0 74.4 jit_solution(5663059293793857608)
XLA Ops:
  0.6 1.7 %shard_map.174 = (bf16[304,128]{1,0:T(8,128)(2,1)}, bf16[128,128]{1,0:T(8,128)(2,1)}) custom-call(bf16[32,32,48]{2,1,0:T(8,128)(2,1)} %refs_0_.1, bf16[16,16,96]{2,1,0:T(8,128)(2,1)} %refs_1_.1, bf16[8,8,192]{2,1,0:T(8,128)(2,1)} %three.3, bf16[4,4,384]{2,1,0:T(4,128)(2,1)} %four.3), custom_call_target="tpu_custom_call" | custom-call | flops 1724999936 | tf_op jit(solution)/shard_map/pallas_call | solution.py:661
  2.4 2.5 %shard_map.175 = (bf16[560,128]{1,0:T(8,128)(2,1)}, bf16[3808,128]{1,0:T(8,128)(2,1)}) custom-call(bf16[12,864]{1,0:T(8,128)(2,1)} %bitcast.20, bf16[24,1728]{1,0:T(8,128)(2,1)} %bitcast.18, bf16[204,432]{1,0:T(8,128)(2,1)} %bitcast.17, bf16[168,864]{1,0:T(8,128)(2,1)} %bitcast.16, bf16[96,1728]{1,0:T(8,128)(2,1)} %bitcast.13, bf16[12,96]{1,0:T(8,128)(2,1)} %bitcast.27, ...), custom_call_target="tpu_custom_call" | custom-call | flops 1724999936 | tf_op jit(solution)/shard_map/pallas_call | solution.py:661
  4.9 3.0 %collective-permute-start.17 = (bf16[3808,128]{1,0:T(8,128)(2,1)}, bf16[3808,128]{1,0:T(8,128)(2,1)S(1)}, u32[]{:S(2)}, u32[]{:S(2)}) collective-permute-start(bf16[3808,128]{1,0:T(8,128)(2,1)} %get-tuple-element.26.after.refs_4_.refs_10_), channel_id=1, source_target_pairs={{0,2},{1,3},{2,0},{3,1},{4,6},{5,7},{6,4},{7,5},{8,10},{9,11},{10,... | collective-permute-start | bytes 2924552 | tf_op jit(solution)/shard_map/ppermute | solution.py:636
  7.8 0.0 copy-done.10
  7.8 3.5 %collective-permute-start = (bf16[304,128]{1,0:T(8,128)(2,1)S(1)}, bf16[304,128]{1,0:T(8,128)(2,1)S(1)}, u32[]{:S(2)}, u32[]{:S(2)}) collective-permute-start(bf16[304,128]{1,0:T(8,128)(2,1)S(1)} %copy-done.10), channel_id=1, source_target_pairs={{0,4},{4,8},{8,12},{1,5},{5,9},{9,13},{2,6},{6,10},{10,14},{3,7},{... | collective-permute-start | bytes 233480 | tf_op jit(solution)/shard_map/ppermute | solution.py:642
  11.3 0.6 collective-permute-start.11
  11.9 1.3 %collective-permute-start.1 = (bf16[128,128]{1,0:T(8,128)(2,1)S(1)}, bf16[128,128]{1,0:T(8,128)(2,1)S(1)}, u32[]{:S(2)}, u32[]{:S(2)}) collective-permute-start(bf16[128,128]{1,0:T(8,128)(2,1)S(1)} %copy-done.18), channel_id=1, source_target_pairs={{4,0},{8,4},{12,8},{5,1},{9,5},{13,9},{6,2},{10,6},{14,10},{7,3},{... | collective-permute-start | bytes 98312 | tf_op jit(solution)/shard_map/ppermute | solution.py:642
  13.2 0.1 collective-permute-start.10
  13.3 4.4 %collective-permute-done.1.bottom.refs_3_ = bf16[128,128]{1,0:T(8,128)(2,1)S(1)} collective-permute-done((bf16[128,128]{1,0:T(8,128)(2,1)S(1)}, bf16[128,128]{1,0:T(8,128)(2,1)S(1)}, u32[]{:S(2)}, u32[]{:S(2)}) %collective-permute-start.1) | collective-permute-done | bytes 32800 | tf_op jit(solution)/shard_map/ppermute | solution.py:642
  17.7 0.0 collective-permute-done.top.refs_2_
  17.7 0.6 copy-done.17
  18.3 0.6 copy-done.9
  19.0 1.6 %shard_map.176.after.refs_0_ = bf16[88,384]{1,0:T(8,128)(2,1)} custom-call(bf16[8,8,192]{2,1,0:T(8,128)(2,1)} %three.3, bf16[4,4,384]{2,1,0:T(4,128)(2,1)} %four.3, bf16[304,128]{1,0:T(8,128)(2,1)} %copy-done.9, bf16[128,128]{1,0:T(8,128)(2,1)} %copy-done.17, bf16[3808,128]{1,0:T(8,128)(2,1)} %get-tuple-element.26.after.refs_4_.refs_10_), custom_call_target="tpu_custom_call" | custom-call | flops 1150000000 | tf_op jit(solution)/shard_map/pallas_call | solution.py:661
  20.6 0.0 collective-permute-start.4
  20.6 1.5 %collective-permute-start.3 = (bf16[88,384]{1,0:T(8,128)(2,1)}, bf16[88,384]{1,0:T(8,128)(2,1)S(1)}, u32[]{:S(2)}, u32[]{:S(2)}) collective-permute-start(bf16[88,384]{1,0:T(8,128)(2,1)} %shard_map.176.after.refs_0_), channel_id=1, source_target_pairs={{0,2},{1,3},{2,0},{3,1},{4,6},{5,7},{6,4},{7,5},{8,10},{9,11},{10,... | collective-permute-start | bytes 202760 | tf_op jit(solution)/shard_map/ppermute | solution.py:636
  22.1 11.4 %collective-permute-done.11.refs_10_ = bf16[560,128]{1,0:T(8,128)(2,1)S(1)} collective-permute-done((bf16[560,128]{1,0:T(8,128)(2,1)}, bf16[560,128]{1,0:T(8,128)(2,1)S(1)}, u32[]{:S(2)}, u32[]{:S(2)}) %collective-permute-start.11) | collective-permute-done | bytes 143392 | tf_op jit(solution)/shard_map/ppermute | solution.py:636
  33.5 0.0 collective-permute-start.2
  33.5 1.9 %shard_map.177 = (bf16[43,16,128]{2,1,0:T(8,128)(2,1)}, bf16[43,8,128]{2,1,0:T(8,128)(2,1)}) custom-call(bf16[32,32,48]{2,1,0:T(8,128)(2,1)} %refs_0_.1, bf16[16,16,96]{2,1,0:T(8,128)(2,1)} %refs_1_.1, bf16[304,128]{1,0:T(8,128)(2,1)} %copy-done.9, bf16[128,128]{1,0:T(8,128)(2,1)} %copy-done.17, bf16[88,384]{1,0:T(8,128)(2,1)} %shard_map.176.after.refs_0_), custom_call_target="tpu_custom_call" | custom-call | flops 1724999936 | tf_op jit(solution)/shard_map/pallas_call | solution.py:661
  35.5 0.0 collective-permute-done.10.refs_9_
  35.5 0.0 copy-done
  35.5 0.5 collective-permute-start.16
  36.0 0.0 collective-permute-done.4.refs_3_
  36.0 1.3 %collective-permute-start.9 = (bf16[43,8,128]{2,1,0:T(8,128)(2,1)}, bf16[43,8,128]{2,1,0:T(8,128)(2,1)S(1)}, u32[]{:S(2)}, u32[]{:S(2)}) collective-permute-start(bf16[43,8,128]{2,1,0:T(8,128)(2,1)} %get-tuple-element.31), channel_id=1, source_target_pairs={{1,0},{2,1},{3,2},{5,4},{6,5},{7,6},{9,8},{10,9},{11,10},{13,12},{... | collective-permute-start | bytes 264200 | tf_op jit(solution)/shard_map/ppermute | solution.py:642
  37.3 0.0 collective-permute-done.3.refs_2_
  37.3 3.0 %collective-permute-start.8 = (bf16[43,16,128]{2,1,0:T(8,128)(2,1)}, bf16[43,16,128]{2,1,0:T(8,128)(2,1)S(1)}, u32[]{:S(2)}, u32[]{:S(2)}) collective-permute-start(bf16[43,16,128]{2,1,0:T(8,128)(2,1)} %get-tuple-element.27.refs_7_), channel_id=1, source_target_pairs={{0,1},{1,2},{2,3},{4,5},{5,6},{6,7},{8,9},{9,10},{10,11},{12,13},{... | collective-permute-start | bytes 528392 | tf_op jit(solution)/shard_map/ppermute | solution.py:642
  40.4 0.0 collective-permute-done.2.refs_1_
  40.4 1.7 %collective-permute-start.12 = (bf16[560,128]{1,0:T(8,128)(2,1)S(1)}, bf16[560,128]{1,0:T(8,128)(2,1)S(1)}, u32[]{:S(2)}, u32[]{:S(2)}) collective-permute-start(bf16[560,128]{1,0:T(8,128)(2,1)S(1)} %collective-permute-done.11.refs_10_), channel_id=1, source_target_pairs={{0,1},{1,0},{2,3},{3,2},{4,5},{5,4},{6,7},{7,6},{8,9},{9,8},{10,11... | collective-permute-start | bytes 430088 | tf_op jit(solution)/shard_map/ppermute | solution.py:636
  42.1 0.0 collective-permute-done.17.refs_6_.refs_12_
  42.1 0.1 collective-permute-start.18
  42.2 4.1 %shard_map.178 = (bf16[272,128]{1,0:T(8,128)(2,1)}, bf16[288,48]{1,0:T(8,128)(2,1)}, bf16[64,96]{1,0:T(8,128)(2,1)}) custom-call(bf16[88,384]{1,0:T(8,128)(2,1)} %shard_map.176.after.refs_0_, bf16[88,384]{1,0:T(8,128)(2,1)} %copy-done.16, bf16[88,384]{1,0:T(8,128)(2,1)} %copy-done.15, bf16[88,384]{1,0:T(8,128)(2,1)} %copy-done.14, ...), custom_call_target="tpu_custom_call" | custom-call | flops 3449999872 | tf_op jit(solution)/shard_map/pallas_call | solution.py:661
  46.3 0.0 collective-permute-done.9.refs_5_
  46.4 0.6 collective-permute-start.7
  46.9 0.0 collective-permute-done.8.refs_4_
  46.9 1.3 %collective-permute-start.6 = (bf16[272,128]{1,0:T(8,128)(2,1)}, bf16[272,128]{1,0:T(8,128)(2,1)S(1)}, u32[]{:S(2)}, u32[]{:S(2)}) collective-permute-start(bf16[272,128]{1,0:T(8,128)(2,1)} %get-tuple-element.28.refs_7_.refs_0_), channel_id=1, source_target_pairs={{0,2},{1,3},{2,0},{3,1},{4,6},{5,7},{6,4},{7,5},{8,10},{9,11},{10,... | collective-permute-start | bytes 208904 | tf_op jit(solution)/shard_map/ppermute | solution.py:636
  48.2 0.0 collective-permute-done.12.refs_11_
  48.3 0.0 collective-permute-start.5
  48.3 0.0 copy-done.8
  48.3 0.6 copy-done.7
  48.9 7.0 %shard_map.179 = (bf16[32,32,48]{2,1,0:T(8,128)(2,1)}, bf16[16,16,96]{2,1,0:T(8,128)(2,1)}, f32[39,56,128]{2,1,0:T(8,128)}, f32[19,40,128]{2,1,0:T(8,128)}) custom-call(bf16[32,32,48]{2,1,0:T(8,128)(2,1)} %refs_0_.1, bf16[16,16,96]{2,1,0:T(8,128)(2,1)} %refs_1_.1, bf16[304,128]{1,0:T(8,128)(2,1)} %copy-done.9, bf16[128,128]{1,0:T(8,128)(2,1)} %copy-done.17, ...), custom_call_target="tpu_custom_call" | custom-call | flops 5750000128 | tf_op jit(solution)/shard_map/pallas_call | solution.py:661
  55.9 0.0 collective-permute-done.7.refs_3_
  55.9 0.0 copy-start.11
  55.9 0.0 collective-permute-done.6.refs_2_
  55.9 0.0 collective-permute-done.5.refs_1_
  55.9 0.0 copy-start.13
  55.9 0.6 copy-done.11
  56.5 0.0 copy-done.12
  56.5 0.0 copy-done.13
  56.5 4.1 %shard_map.180 = (bf16[104,128]{1,0:T(8,128)(2,1)}, bf16[104,128]{1,0:T(8,128)(2,1)}, bf16[104,128]{1,0:T(8,128)(2,1)}, bf16[104,128]{1,0:T(8,128)(2,1)}) custom-call(bf16[272,128]{1,0:T(8,128)(2,1)} %get-tuple-element.28.refs_7_.refs_0_, bf16[272,128]{1,0:T(8,128)(2,1)} %copy-done.13, bf16[272,128]{1,0:T(8,128)(2,1)} %copy-done.12, ...), custom_call_target="tpu_custom_call" | custom-call | flops 3449999872 | tf_op jit(solution)/shard_map/pallas_call | solution.py:661
  60.6 0.0 collective-permute-start.13
  60.7 0.7 collective-permute-start.14
  61.4 1.1 %collective-permute-start.15 = (bf16[104,128]{1,0:T(8,128)(2,1)}, bf16[104,128]{1,0:T(8,128)(2,1)S(1)}, u32[]{:S(2)}, u32[]{:S(2)}) collective-permute-start(bf16[104,128]{1,0:T(8,128)(2,1)} %get-tuple-element.37), channel_id=1, source_target_pairs={{0,3},{1,2},{2,1},{3,0},{4,7},{5,6},{6,5},{7,4},{8,11},{9,10},{10,... | collective-permute-start | bytes 79880 | tf_op jit(solution)/shard_map/ppermute | solution.py:636
  62.5 0.0 collective-permute-done.16.refs_5_.refs_11_
  62.5 0.0 collective-permute-done.18.refs_7_.refs_13_
  62.5 1.0 %copy-done.2 = bf16[3808,128]{1,0:T(8,128)(2,1)} copy-done((bf16[3808,128]{1,0:T(8,128)(2,1)}, bf16[3808,128]{1,0:T(8,128)(2,1)S(1)}, u32[]{:S(2)}) %copy-start.2) | copy-done | bytes 974872
  63.5 0.3 copy-done.3
  63.8 5.8 %shard_map.181 = (f32[16,16,96]{2,1,0:T(8,128)}, f32[8,8,192]{2,1,0:T(8,128)}, f32[4,8,384]{2,1,0:T(8,128)}) custom-call(f32[39,56,128]{2,1,0:T(8,128)} %get-tuple-element.39.refs_0_, f32[19,40,128]{2,1,0:T(8,128)} %get-tuple-element.40.refs_1_, f32[30,128]{1,0:T(8,128)} %bitcast.25, bf16[104,128]{1,0:T(8,128)(2,1)} %get-tuple-element.34.refs_3_.refs_0_, ...), custom_call_target="tpu_custom_call" | custom-call | flops 5750000128 | tf_op jit(solution)/shard_map/pallas_call | solution.py:661
  69.6 0.0 collective-permute-done.13.refs_1_
  69.6 0.0 copy-start.19
  69.6 0.0 collective-permute-done.14.refs_2_
  69.6 0.0 collective-permute-done.15.refs_3_
  69.6 0.6 copy-done.19
  70.2 0.0 copy-done.20
  70.2 0.0 copy-done.21
  70.2 4.1 %shard_map.182 = (bf16[32,32,48]{2,1,0:T(8,128)(2,1)}, bf16[16,16,96]{2,1,0:T(8,128)(2,1)}, bf16[8,8,192]{2,1,0:T(8,128)(2,1)}, bf16[4,4,384]{2,1,0:T(4,128)(2,1)}) custom-call(bf16[104,128]{1,0:T(8,128)(2,1)} %get-tuple-element.34.refs_3_.refs_0_, bf16[104,128]{1,0:T(8,128)(2,1)} %copy-done.19, bf16[104,128]{1,0:T(8,128)(2,1)} %copy-done.20, ...), custom_call_target="tpu_custom_call" | custom-call | flops 4600000000 | tf_op jit(solution)/shard_map/pallas_call | solution.py:661
  (27 shorter events, 0.1 us)
Async XLA Ops:
  2.4 5.5 %copy-start.10 = (bf16[304,128]{1,0:T(8,128)(2,1)S(1)}, bf16[304,128]{1,0:T(8,128)(2,1)}, u32[]{:S(2)}) copy-start(bf16[304,128]{1,0:T(8,128)(2,1)} %get-tuple-element.24.refs_8_) | copy-start | bytes 233476
  2.4 9.6 %copy-start.18 = (bf16[128,128]{1,0:T(8,128)(2,1)S(1)}, bf16[128,128]{1,0:T(8,128)(2,1)}, u32[]{:S(2)}) copy-start(bf16[128,128]{1,0:T(8,128)(2,1)} %get-tuple-element.25) | copy-start | bytes 98308
  4.9 37.2 %collective-permute-start.17 = (bf16[3808,128]{1,0:T(8,128)(2,1)}, bf16[3808,128]{1,0:T(8,128)(2,1)S(1)}, u32[]{:S(2)}, u32[]{:S(2)}) collective-permute-start(bf16[3808,128]{1,0:T(8,128)(2,1)} %get-tuple-element.26.after.refs_4_.refs_10_), channel_id=1, source_target_pairs={{0,2},{1,3},{2,0},{3,1},{4,6},{5,7},{6,4},{7,5},{8,10},{9,11},{10,... | collective-permute-start | bytes 2924552 | tf_op jit(solution)/shard_map/ppermute | solution.py:636
  7.8 9.9 %collective-permute-start = (bf16[304,128]{1,0:T(8,128)(2,1)S(1)}, bf16[304,128]{1,0:T(8,128)(2,1)S(1)}, u32[]{:S(2)}, u32[]{:S(2)}) collective-permute-start(bf16[304,128]{1,0:T(8,128)(2,1)S(1)} %copy-done.10), channel_id=1, source_target_pairs={{0,4},{4,8},{8,12},{1,5},{5,9},{9,13},{2,6},{6,10},{10,14},{3,7},{... | collective-permute-start | bytes 233480 | tf_op jit(solution)/shard_map/ppermute | solution.py:642
  11.3 22.2 %collective-permute-start.11 = (bf16[560,128]{1,0:T(8,128)(2,1)}, bf16[560,128]{1,0:T(8,128)(2,1)S(1)}, u32[]{:S(2)}, u32[]{:S(2)}) collective-permute-start(bf16[560,128]{1,0:T(8,128)(2,1)} %get-tuple-element.32.refs_8_), channel_id=1, source_target_pairs={{0,2},{1,3},{2,0},{3,1},{4,6},{5,7},{6,4},{7,5},{8,10},{9,11},{10,... | collective-permute-start | bytes 430088 | tf_op jit(solution)/shard_map/ppermute | solution.py:636
  11.9 5.8 %collective-permute-start.1 = (bf16[128,128]{1,0:T(8,128)(2,1)S(1)}, bf16[128,128]{1,0:T(8,128)(2,1)S(1)}, u32[]{:S(2)}, u32[]{:S(2)}) collective-permute-start(bf16[128,128]{1,0:T(8,128)(2,1)S(1)} %copy-done.18), channel_id=1, source_target_pairs={{4,0},{8,4},{12,8},{5,1},{9,5},{13,9},{6,2},{10,6},{14,10},{7,3},{... | collective-permute-start | bytes 98312 | tf_op jit(solution)/shard_map/ppermute | solution.py:642
  13.2 22.2 %collective-permute-start.10 = (bf16[560,128]{1,0:T(8,128)(2,1)}, bf16[560,128]{1,0:T(8,128)(2,1)S(1)}, u32[]{:S(2)}, u32[]{:S(2)}) collective-permute-start(bf16[560,128]{1,0:T(8,128)(2,1)} %get-tuple-element.32.refs_8_), channel_id=1, source_target_pairs={{0,1},{1,0},{2,3},{3,2},{4,5},{5,4},{6,7},{7,6},{8,9},{9,8},{10,11... | collective-permute-start | bytes 430088 | tf_op jit(solution)/shard_map/ppermute | solution.py:636
  17.7 0.6 copy-start.17
  18.3 0.6 copy-start.9
  20.6 14.9 %copy-start = (bf16[3808,128]{1,0:T(8,128)(2,1)S(1)}, bf16[3808,128]{1,0:T(8,128)(2,1)}, u32[]{:S(2)}) copy-start(bf16[3808,128]{1,0:T(8,128)(2,1)} %get-tuple-element.26.after.refs_4_.refs_10_) | copy-start | bytes 2924548
  20.6 15.4 %collective-permute-start.4 = (bf16[88,384]{1,0:T(8,128)(2,1)}, bf16[88,384]{1,0:T(8,128)(2,1)S(1)}, u32[]{:S(2)}, u32[]{:S(2)}) collective-permute-start(bf16[88,384]{1,0:T(8,128)(2,1)} %shard_map.176.after.refs_0_), channel_id=1, source_target_pairs={{0,3},{1,2},{2,1},{3,0},{4,7},{5,6},{6,5},{7,4},{8,11},{9,10},{10,... | collective-permute-start | bytes 202760 | tf_op jit(solution)/shard_map/ppermute | solution.py:636
  20.6 16.7 %collective-permute-start.3 = (bf16[88,384]{1,0:T(8,128)(2,1)}, bf16[88,384]{1,0:T(8,128)(2,1)S(1)}, u32[]{:S(2)}, u32[]{:S(2)}) collective-permute-start(bf16[88,384]{1,0:T(8,128)(2,1)} %shard_map.176.after.refs_0_), channel_id=1, source_target_pairs={{0,2},{1,3},{2,0},{3,1},{4,6},{5,7},{6,4},{7,5},{8,10},{9,11},{10,... | collective-permute-start | bytes 202760 | tf_op jit(solution)/shard_map/ppermute | solution.py:636
  33.5 6.8 %copy-start.5 = (bf16[560,128]{1,0:T(8,128)(2,1)}, bf16[560,128]{1,0:T(8,128)(2,1)S(1)}, u32[]{:S(2)}) copy-start(bf16[560,128]{1,0:T(8,128)(2,1)S(1)} %collective-permute-done.11.refs_10_) | copy-start | bytes 430084
  33.5 6.8 %collective-permute-start.2 = (bf16[88,384]{1,0:T(8,128)(2,1)}, bf16[88,384]{1,0:T(8,128)(2,1)S(1)}, u32[]{:S(2)}, u32[]{:S(2)}) collective-permute-start(bf16[88,384]{1,0:T(8,128)(2,1)} %shard_map.176.after.refs_0_), channel_id=1, source_target_pairs={{0,1},{1,0},{2,3},{3,2},{4,5},{5,4},{6,7},{7,6},{8,9},{9,8},{10,11... | collective-permute-start | bytes 202760 | tf_op jit(solution)/shard_map/ppermute | solution.py:636
  35.5 10.9 %copy-start.6 = (bf16[560,128]{1,0:T(8,128)(2,1)}, bf16[560,128]{1,0:T(8,128)(2,1)S(1)}, u32[]{:S(2)}) copy-start(bf16[560,128]{1,0:T(8,128)(2,1)S(1)} %collective-permute-done.10.refs_9_) | copy-start | bytes 430084
  35.5 27.0 %collective-permute-start.16 = (bf16[3808,128]{1,0:T(8,128)(2,1)S(1)}, bf16[3808,128]{1,0:T(8,128)(2,1)S(1)}, u32[]{:S(2)}, u32[]{:S(2)}) collective-permute-start(bf16[3808,128]{1,0:T(8,128)(2,1)S(1)} %copy-done), channel_id=1, source_target_pairs={{0,1},{1,0},{2,3},{3,2},{4,5},{5,4},{6,7},{7,6},{8,9},{9,8},{10,11... | collective-permute-start | bytes 2924552 | tf_op jit(solution)/shard_map/ppermute | solution.py:636
  36.0 6.2 %copy-start.14 = (bf16[88,384]{1,0:T(8,128)(2,1)}, bf16[88,384]{1,0:T(8,128)(2,1)S(1)}, u32[]{:S(2)}) copy-start(bf16[88,384]{1,0:T(8,128)(2,1)S(1)} %collective-permute-done.4.refs_3_) | copy-start | bytes 202756
  36.0 10.4 %collective-permute-start.9 = (bf16[43,8,128]{2,1,0:T(8,128)(2,1)}, bf16[43,8,128]{2,1,0:T(8,128)(2,1)S(1)}, u32[]{:S(2)}, u32[]{:S(2)}) collective-permute-start(bf16[43,8,128]{2,1,0:T(8,128)(2,1)} %get-tuple-element.31), channel_id=1, source_target_pairs={{1,0},{2,1},{3,2},{5,4},{6,5},{7,6},{9,8},{10,9},{11,10},{13,12},{... | collective-permute-start | bytes 264200 | tf_op jit(solution)/shard_map/ppermute | solution.py:642
  37.3 4.9 %copy-start.15 = (bf16[88,384]{1,0:T(8,128)(2,1)}, bf16[88,384]{1,0:T(8,128)(2,1)S(1)}, u32[]{:S(2)}) copy-start(bf16[88,384]{1,0:T(8,128)(2,1)S(1)} %collective-permute-done.3.refs_2_) | copy-start | bytes 202756
  37.3 9.6 %collective-permute-start.8 = (bf16[43,16,128]{2,1,0:T(8,128)(2,1)}, bf16[43,16,128]{2,1,0:T(8,128)(2,1)S(1)}, u32[]{:S(2)}, u32[]{:S(2)}) collective-permute-start(bf16[43,16,128]{2,1,0:T(8,128)(2,1)} %get-tuple-element.27.refs_7_), channel_id=1, source_target_pairs={{0,1},{1,2},{2,3},{4,5},{5,6},{6,7},{8,9},{9,10},{10,11},{12,13},{... | collective-permute-start | bytes 528392 | tf_op jit(solution)/shard_map/ppermute | solution.py:642
  40.4 1.8 %copy-start.16 = (bf16[88,384]{1,0:T(8,128)(2,1)}, bf16[88,384]{1,0:T(8,128)(2,1)S(1)}, u32[]{:S(2)}) copy-start(bf16[88,384]{1,0:T(8,128)(2,1)S(1)} %collective-permute-done.2.refs_1_) | copy-start | bytes 202756
  40.4 7.9 %collective-permute-start.12 = (bf16[560,128]{1,0:T(8,128)(2,1)S(1)}, bf16[560,128]{1,0:T(8,128)(2,1)S(1)}, u32[]{:S(2)}, u32[]{:S(2)}) collective-permute-start(bf16[560,128]{1,0:T(8,128)(2,1)S(1)} %collective-permute-done.11.refs_10_), channel_id=1, source_target_pairs={{0,1},{1,0},{2,3},{3,2},{4,5},{5,4},{6,7},{7,6},{8,9},{9,8},{10,11... | collective-permute-start | bytes 430088 | tf_op jit(solution)/shard_map/ppermute | solution.py:636
  42.1 4.3 %copy-start.1 = (bf16[3808,128]{1,0:T(8,128)(2,1)}, bf16[3808,128]{1,0:T(8,128)(2,1)S(1)}, u32[]{:S(2)}) copy-start(bf16[3808,128]{1,0:T(8,128)(2,1)S(1)} %collective-permute-done.17.refs_6_.refs_12_) | copy-start | bytes 2924548
  42.1 20.4 %collective-permute-start.18 = (bf16[3808,128]{1,0:T(8,128)(2,1)S(1)}, bf16[3808,128]{1,0:T(8,128)(2,1)S(1)}, u32[]{:S(2)}, u32[]{:S(2)}) collective-permute-start(bf16[3808,128]{1,0:T(8,128)(2,1)S(1)} %collective-permute-done.17.refs_6_.refs_12_), channel_id=1, source_target_pairs={{0,1},{1,0},{2,3},{3,2},{4,5},{5,4},{6,7},{7,6},{8,9},{9,8},{10,11... | collective-permute-start | bytes 2924552 | tf_op jit(solution)/shard_map/ppermute | solution.py:636
  46.4 2.0 %copy-start.8 = (bf16[43,8,128]{2,1,0:T(8,128)(2,1)}, bf16[43,8,128]{2,1,0:T(8,128)(2,1)S(1)}, u32[]{:S(2)}) copy-start(bf16[43,8,128]{2,1,0:T(8,128)(2,1)S(1)} %collective-permute-done.9.refs_5_) | copy-start | bytes 264196
  46.4 9.5 %collective-permute-start.7 = (bf16[272,128]{1,0:T(8,128)(2,1)}, bf16[272,128]{1,0:T(8,128)(2,1)S(1)}, u32[]{:S(2)}, u32[]{:S(2)}) collective-permute-start(bf16[272,128]{1,0:T(8,128)(2,1)} %get-tuple-element.28.refs_7_.refs_0_), channel_id=1, source_target_pairs={{0,3},{1,2},{2,1},{3,0},{4,7},{5,6},{6,5},{7,4},{8,11},{9,10},{10,... | collective-permute-start | bytes 208904 | tf_op jit(solution)/shard_map/ppermute | solution.py:636
  46.9 1.4 %copy-start.4 = (bf16[43,16,128]{2,1,0:T(8,128)(2,1)}, bf16[43,16,128]{2,1,0:T(8,128)(2,1)S(1)}, u32[]{:S(2)}) copy-start(bf16[43,16,128]{2,1,0:T(8,128)(2,1)S(1)} %collective-permute-done.8.refs_4_) | copy-start | bytes 528388
  46.9 9.0 %collective-permute-start.6 = (bf16[272,128]{1,0:T(8,128)(2,1)}, bf16[272,128]{1,0:T(8,128)(2,1)S(1)}, u32[]{:S(2)}, u32[]{:S(2)}) collective-permute-start(bf16[272,128]{1,0:T(8,128)(2,1)} %get-tuple-element.28.refs_7_.refs_0_), channel_id=1, source_target_pairs={{0,2},{1,3},{2,0},{3,1},{4,6},{5,7},{6,4},{7,5},{8,10},{9,11},{10,... | collective-permute-start | bytes 208904 | tf_op jit(solution)/shard_map/ppermute | solution.py:636
  48.2 0.6 copy-start.7
  48.3 7.7 %collective-permute-start.5 = (bf16[272,128]{1,0:T(8,128)(2,1)}, bf16[272,128]{1,0:T(8,128)(2,1)S(1)}, u32[]{:S(2)}, u32[]{:S(2)}) collective-permute-start(bf16[272,128]{1,0:T(8,128)(2,1)} %get-tuple-element.28.refs_7_.refs_0_), channel_id=1, source_target_pairs={{0,1},{1,0},{2,3},{3,2},{4,5},{5,4},{6,7},{7,6},{8,9},{9,8},{10,11... | collective-permute-start | bytes 208904 | tf_op jit(solution)/shard_map/ppermute | solution.py:636
  55.9 0.6 copy-start.11
  55.9 0.6 copy-start.12
  55.9 0.6 copy-start.13
  60.6 9.0 %collective-permute-start.13 = (bf16[104,128]{1,0:T(8,128)(2,1)}, bf16[104,128]{1,0:T(8,128)(2,1)S(1)}, u32[]{:S(2)}, u32[]{:S(2)}) collective-permute-start(bf16[104,128]{1,0:T(8,128)(2,1)} %get-tuple-element.35), channel_id=1, source_target_pairs={{0,1},{1,0},{2,3},{3,2},{4,5},{5,4},{6,7},{7,6},{8,9},{9,8},{10,11... | collective-permute-start | bytes 79880 | tf_op jit(solution)/shard_map/ppermute | solution.py:636
  60.7 8.9 %collective-permute-start.14 = (bf16[104,128]{1,0:T(8,128)(2,1)}, bf16[104,128]{1,0:T(8,128)(2,1)S(1)}, u32[]{:S(2)}, u32[]{:S(2)}) collective-permute-start(bf16[104,128]{1,0:T(8,128)(2,1)} %get-tuple-element.36), channel_id=1, source_target_pairs={{0,2},{1,3},{2,0},{3,1},{4,6},{5,7},{6,4},{7,5},{8,10},{9,11},{10,... | collective-permute-start | bytes 79880 | tf_op jit(solution)/shard_map/ppermute | solution.py:636
  61.4 8.3 %collective-permute-start.15 = (bf16[104,128]{1,0:T(8,128)(2,1)}, bf16[104,128]{1,0:T(8,128)(2,1)S(1)}, u32[]{:S(2)}, u32[]{:S(2)}) collective-permute-start(bf16[104,128]{1,0:T(8,128)(2,1)} %get-tuple-element.37), channel_id=1, source_target_pairs={{0,3},{1,2},{2,1},{3,0},{4,7},{5,6},{6,5},{7,4},{8,11},{9,10},{10,... | collective-permute-start | bytes 79880 | tf_op jit(solution)/shard_map/ppermute | solution.py:636
  62.5 1.0 %copy-start.2 = (bf16[3808,128]{1,0:T(8,128)(2,1)}, bf16[3808,128]{1,0:T(8,128)(2,1)S(1)}, u32[]{:S(2)}) copy-start(bf16[3808,128]{1,0:T(8,128)(2,1)S(1)} %collective-permute-done.16.refs_5_.refs_11_) | copy-start | bytes 2924548
  62.5 1.3 %copy-start.3 = (bf16[3808,128]{1,0:T(8,128)(2,1)}, bf16[3808,128]{1,0:T(8,128)(2,1)S(1)}, u32[]{:S(2)}) copy-start(bf16[3808,128]{1,0:T(8,128)(2,1)S(1)} %collective-permute-done.18.refs_7_.refs_13_) | copy-start | bytes 2924548
  69.6 0.6 copy-start.19
  69.6 0.6 copy-start.20
  69.6 0.6 copy-start.21

commit v3 on v2

--- a/solution.py
+++ b/solution.py
@@ -153,63 +153,79 @@
             at += size
 
 
-def rows_kernel(layouts, one, two, three, four, down_ref, up_ref, scratch):
+def rows_kernel(layouts, one, two, three, four, even_ref, odd_ref, scratch):
     refs = (one, two, three, four)
     low, high = layouts
     firsts = tuple(ref.shape[0] - count for ref, count in zip(refs, low.counts))
+    row, _ = position()
     scratch[...] = jnp.zeros_like(scratch)
     pack_rows(low, refs, firsts, scratch)
-    down_ref[...] = scratch[0 : low.total, :].astype(BF16)
+    last_rows = scratch[...].astype(BF16)
     pack_rows(high, refs, (0, 0, 0, 0), scratch)
-    up_ref[...] = scratch[0 : high.total, :].astype(BF16)
-
-
-def stretch_fine(level, layout_pair, feat, top, bottom, target, col):
+    first_rows = scratch[...].astype(BF16)
+    even_ref[...] = jnp.where((row & 1) == 0, last_rows, first_rows)
+    odd_ref[...] = jnp.where((row & 1) == 0, first_rows, last_rows)
+
+
+class Border:
+    def __init__(self, even, odd, index):
+        self.even, self.odd, self.is_odd = even, odd, (index & 1) == 1
+
+    def prev(self, *at):
+        return jnp.where(self.is_odd, self.even[at], self.odd[at]).astype(F32)
+
+    def next(self, *at):
+        return jnp.where(self.is_odd, self.odd[at], self.even[at]).astype(F32)
+
+
+def stretch_fine(level, layout_pair, feat, border, target, col):
     low, high = layout_pair
     height, breadth, channels = feat.shape
     before, after = low.counts[level], high.counts[level]
     for layout, message, row, count in (
-        (low, top, 0, before),
-        (high, bottom, before + height, after),
+        (low, border.prev, 0, before),
+        (high, border.next, before + height, after),
     ):
         at = layout.start[level]
         if level == 0:
             half = layout.half
             for part in range(2):
-                block = message[at : at + count * half, part * 64 : part * 64 + channels]
+                block = message(slice(at, at + count * half), slice(part * 64, part * 64 + channels))
                 target[row : row + count, col + part * half : col + (part + 1) * half, :] = (
-                    block.astype(F32).reshape(count, half, channels)
+                    block.reshape(count, half, channels)
                 )
         else:
-            block = message[at : at + count * breadth, 0:channels]
-            target[row : row + count, col : col + breadth, :] = block.astype(F32).reshape(
-                count, breadth, channels
-            )
+            block = message(slice(at, at + count * breadth), slice(0, channels))
+            target[row : row + count, col : col + breadth, :] = block.reshape(count, breadth, channels)
     target[before : before + height, col : col + breadth, :] = feat[...].astype(F32)
 
 
-def columns_kernel(layouts, three, four, top, bottom, after, gather_ref, full_three, message):
+def columns_kernel(layouts, three, four, even, odd, after, gather_ref, full_three, message):
     low, high = layouts
+    border = Border(even, odd, position()[0])
     breadth, channels = three.shape[1], three.shape[2]
     own = three.shape[0] * breadth
     before, after = low.counts[2] * breadth, high.counts[2] * breadth
-    for layout, source, row, size in ((low, top, 0, before), (high, bottom, before + own, after)):
+    for layout, source, row, size in (
+        (low, border.prev, 0, before),
+        (high, border.next, before + own, after),
+    ):
         at = layout.start[2]
         for first in range(0, channels, LANES):
             last = min(first + LANES, channels)
-            full_three[row : row + size, first:last] = source[at : at + size, 0 : last - first].astype(F32)
+            full_three[row : row + size, first:last] = source(slice(at, at + size), slice(0, last - first))
             at += size
     full_three[before : before + own, :] = three[...].astype(F32).reshape(own, channels)
     size_four = gather_four(four.shape)
     breadth, channels4 = four.shape[1], four.shape[2]
     before, after = low.counts[3] * breadth, high.counts[3] * breadth
     for layout, source, row, size in (
-        (low, top, 0, before),
-        (high, bottom, before + four.shape[0] * breadth, after),
+        (low, border.prev, 0, before),
+        (high, border.next, before + four.shape[0] * breadth, after),
     ):
         at = layout.start[3]
         for first in range(0, channels4, LANES):
-            message[row : row + size, first : first + LANES] = source[at : at + size, :].astype(F32)
+            message[row : row + size, first : first + LANES] = source(slice(at, at + size), slice(0, LANES))
             at += size
     for row in range(four.shape[0]):
         at = before + row * breadth
@@ -220,20 +236,25 @@
     gather_ref[...] = message[...].astype(BF16)
 
 
-def edges_kernel(layouts, one, two, top, bottom, after, right_ref, left_ref, full_one, full_two, edge):
-    stretch_fine(0, layouts, one, top, bottom, full_one, 0)
-    stretch_fine(1, layouts, two, top, bottom, full_two, 0)
+def edges_kernel(layouts, one, two, even, odd, after, even_ref, odd_ref, full_one, full_two, edge):
+    row, me = position()
+    border = Border(even, odd, row)
+    stretch_fine(0, layouts, one, border, full_one, 0)
+    stretch_fine(1, layouts, two, border, full_two, 0)
     wide, wide_two = one.shape[1], two.shape[1]
     left, left_two = BEFORE[0], BEFORE[1]
     rows_two = full_two.shape[0]
+    edge[...] = jnp.zeros_like(edge)
     edge[:, 0:left, 0 : one.shape[2]] = full_one[:, wide - left : wide, :]
     edge[0:rows_two, left : left + left_two, 0 : two.shape[2]] = full_two[
         :, wide_two - left_two : wide_two, :
     ]
-    right_ref[...] = edge[...].astype(BF16)
+    last_columns = edge[...].astype(BF16)
     edge[:, 0:AFTER, 0 : one.shape[2]] = full_one[:, 0:AFTER, :]
     edge[0:rows_two, AFTER : 2 * AFTER, 0 : two.shape[2]] = full_two[:, 0:AFTER, :]
-    left_ref[...] = edge[:, 0:8, :].astype(BF16)
+    first_columns = edge[...].astype(BF16)
+    even_ref[...] = jnp.where((me & 1) == 0, last_columns, first_columns)
+    odd_ref[...] = jnp.where((me & 1) == 0, first_columns, last_columns)
 
 
 def gather_four(shape):
@@ -452,25 +473,28 @@
 
 def fine_kernel(plan, *refs):
     packing, layouts, count, rows_all, unit = plan
-    one, two, top, bottom, from_left, from_right, bias_ref, _ = refs[:8]
+    one, two, rows_even, rows_odd, cols_even, cols_odd, bias_ref, _ = refs[:8]
     buffers = refs[8 : 8 + count]
     y1_ref, y2_ref, v1, v2 = refs[8 + count : 12 + count]
     x1, m1, x2, m2, k1, k2, stacked, line, semaphores = refs[12 + count :]
     row, me = position()
-    copies = fetch((0, packing.total), me, buffers, stacked, semaphores)
+    span = packing.span(("conv_one", "conv_two"))
+    copies = fetch(span, me, buffers, stacked, semaphores)
+    rows_border, cols_border = Border(rows_even, rows_odd, row), Border(cols_even, cols_odd, me)
     bias_row(bias_ref, line)
     high1, wide1, chan1 = one.shape
     high2, wide2, chan2 = two.shape
-    stretch_fine(0, layouts, one, top, bottom, x1, 16)
-    stretch_fine(1, layouts, two, top, bottom, x2, 16)
+    stretch_fine(0, layouts, one, rows_border, x1, 16)
+    stretch_fine(1, layouts, two, rows_border, x2, 16)
     b1, b2 = BEFORE[0], BEFORE[1]
     rows2 = high2 + b2 + AFTER
-    x1[:, 16 - b1 : 16, :] = from_left[:, 0:b1, 0:chan1].astype(F32)
-    x1[:, 16 + wide1 : 16 + wide1 + AFTER, :] = from_right[:, 0:AFTER, 0:chan1].astype(F32)
-    x2[:, 16 - b2 : 16, :] = from_left[0:rows2, b1 : b1 + b2, 0:chan2].astype(F32)
-    x2[:, 16 + wide2 : 16 + wide2 + AFTER, :] = from_right[
-        0:rows2, AFTER : 2 * AFTER, 0:chan2
-    ].astype(F32)
+    every = slice(None)
+    x1[:, 16 - b1 : 16, :] = cols_border.prev(every, slice(0, b1), slice(0, chan1))
+    x1[:, 16 + wide1 : 16 + wide1 + AFTER, :] = cols_border.next(every, slice(0, AFTER), slice(0, chan1))
+    x2[:, 16 - b2 : 16, :] = cols_border.prev(slice(0, rows2), slice(b1, b1 + b2), slice(0, chan2))
+    x2[:, 16 + wide2 : 16 + wide2 + AFTER, :] = cols_border.next(
+        slice(0, rows2), slice(AFTER, 2 * AFTER), slice(0, chan2)
+    )
     for copy in copies:
         copy.wait()
     packing.unpack("conv_one", stacked, 0, k1)
@@ -502,19 +526,20 @@
 
 
 def down_kernel(plan, *refs):
-    packing, count, rows_all, unit, offs, shapes = plan
+    packings, count, rows_all, unit, offs, shapes = plan
     v1, v2, bias_ref, _ = refs[:4]
-    buffers = refs[4 : 4 + count]
-    d12_ref, d3_ref, d4_ref = refs[4 + count : 7 + count]
-    t1, tb, s12, t2, s3, g1, g2, stacked, line, semaphores = refs[7 + count :]
+    buffers = (refs[4 : 4 + count], refs[4 + count : 4 + 2 * count])
+    d12_ref, d3_ref, d4_ref = refs[4 + 2 * count : 7 + 2 * count]
+    t1, tb, s12, t2, s3, g1, g2, stacked1, stacked2, line, semaphores1, semaphores2 = refs[7 + 2 * count :]
     row, me = position()
-    span = packing.span(("down_one", "down_two"))
-    copies = fetch(span, me, buffers, stacked, semaphores)
+    spans = packings[0].span(("down_one",)), packings[1].span(("down_two",))
+    copies = fetch(spans[0], me, buffers[0], stacked1, semaphores1)
+    copies += fetch(spans[1], me, buffers[1], stacked2, semaphores2)
     bias_row(bias_ref, line)
     for copy in copies:
         copy.wait()
-    packing.unpack("down_one", stacked, span[0], g1)
-    packing.unpack("down_two", stacked, span[0], g2)
+    packings[0].unpack("down_one", stacked1, spans[0][0], g1)
+    packings[1].unpack("down_two", stacked2, spans[1][0], g2)
     (high1, wide1, _), (_, _, chan2) = shapes[:2]
     off1, off2 = offs[0], offs[1]
     half_high, half_wide = high1 // 2, wide1 // 2
@@ -552,19 +577,20 @@
     d4_ref[...] = (d14 + d24).reshape(e_high, e_wide, 8 * unit)
 
 
-LAST = ("down_three", "lift_two", "lift_three", "lift_four")
+LIFTS = ("lift_two", "lift_three", "lift_four")
 
 
 def join_kernel(plan, *refs):
-    packing, count, unit, offs, shapes = plan
+    packings, count, unit, offs, shapes = plan
     blocks = refs[:count]
     y1_ref, y2_ref, d12_ref, d3_ref, d4_ref, bias_ref = refs[count : count + 6]
-    buffers = refs[count + 6 : 2 * count + 6]
-    out1, out2, out3, out4 = refs[2 * count + 6 : 2 * count + 10]
-    (v3a, v3b, a2, a3a, a3b, a1, p2, p1, c3, k3, l2, l3, l4, stacked, line, semaphores) = refs[2 * count + 10 :]
+    buffers = refs[count + 6 : 2 * count + 6], refs[2 * count + 6 : 3 * count + 6]
+    out1, out2, out3, out4 = refs[3 * count + 6 : 3 * count + 10]
+    (v3a, v3b, a2, a3a, a3b, a1, p2, p1, c3, l2, l3, l4, k3, stacked1, stacked2, line, semaphores1, semaphores2) = refs[3 * count + 10 :]
     _, me = position()
-    span = packing.span(LAST)
-    copies = fetch(span, me, buffers, stacked, semaphores)
+    spans = packings[0].span(LIFTS), packings[1].span(("down_three",))
+    copies = fetch(spans[0], me, buffers[0], stacked1, semaphores1)
+    copies += fetch(spans[1], me, buffers[1], stacked2, semaphores2)
     bias_row(bias_ref, line)
     (high2, wide2, chan2), (high3, wide3, chan3), (high4, wide4, chan4) = shapes[1:]
     own3, own4 = chan3 // count, chan4 // count
@@ -581,8 +607,9 @@
     for copy in copies:
         copy.wait()
     groups3, groups4 = (unit, 2 * unit), (unit, 2 * unit, 4 * unit)
-    for name, target in zip(LAST, (k3, l2, l3, l4)):
-        packing.unpack(name, stacked, span[0], target)
+    for name, target in zip(LIFTS, (l2, l3, l4)):
+        packings[0].unpack(name, stacked1, spans[0][0], target)
+    packings[1].unpack("down_three", stacked2, spans[1][0], k3)
     off3, offl2, offl3, offl4 = offs[2:]
 
     def lifted(flat, kernel, groups, offset):
@@ -636,10 +663,13 @@
     return lax.ppermute(value, "cols", [(i, i ^ mask) for i in range(count)])
 
 
-def shifted(value, axis, distance):
+def paired(even, odd, axis):
     count = lax.axis_size(axis)
-    route = [(i, i + distance) for i in range(count) if 0 <= i + distance < count]
-    return lax.ppermute(value, axis, route)
+    results = []
+    for value, start in ((even, 0), (odd, 1)):
+        ups = [(i, i + 1) for i in range(start, count - 1, 2)]
+        results.append(lax.ppermute(value, axis, ups + [(b, a) for a, b in ups]))
+    return results
 
 
 def exchanged(value, count):
@@ -655,6 +685,11 @@
         for mask in list(held):
             held[mask | 1] = flipped(held[mask], 1, count)
     return [held[mask] for mask in range(count)]
+
+
+def stack(packing, names, count):
+    low, high = packing.span(names)
+    return pltpu.VMEM((count, high - low, LANES), BF16)
 
 
 def local(kernel, cost, outs, scratch, operands, anywhere=()):
@@ -697,35 +732,32 @@
     line = pltpu.VMEM((8, lines * LANES), F32)
     layouts = (RowLayout(shapes, BEFORE), RowLayout(shapes, (AFTER,) * 4))
     most = max(layouts[0].total, layouts[1].total)
-    down, up = local(
+    rows_pair = local(
         functools.partial(rows_kernel, layouts),
         1.5,
-        [jax.ShapeDtypeStruct((l.total, LANES), BF16) for l in layouts],
+        [jax.ShapeDtypeStruct((most, LANES), BF16)] * 2,
         [pltpu.VMEM((most, LANES), F32)],
         feats,
     )
-    top = shifted(down, "rows", 1)
-    bottom = shifted(up, "rows", -1)
-
-    early = {"conv_one": conv_one, "conv_two": conv_two}
-    late = {
-        "down_one": down_one,
-        "down_two": down_two,
-        "down_three": down_three,
-        "lift_two": lift_two,
-        "lift_three": lift_three,
-        "lift_four": lift_four,
-    }
-    packings = [Packing({name: w.shape for name, w in group.items()}) for group in (early, late)]
+    rows_border = paired(*rows_pair, "rows")
+
+    groups = (
+        {"conv_one": conv_one, "conv_two": conv_two, "down_one": down_one},
+        {"down_two": down_two, "lift_two": lift_two, "lift_three": lift_three, "lift_four": lift_four},
+        {"down_three": down_three},
+    )
+    packings = [Packing({name: w.shape for name, w in group.items()}) for group in groups]
     packed = local(
         functools.partial(pack_kernel, packings),
         1.5,
         [jax.ShapeDtypeStruct((p.total, LANES), BF16) for p in packings],
         [],
-        [w.T for group in (early, late) for w in group.values()],
-        [down],
+        [w.T for group in groups for w in group.values()],
+        [rows_pair[0]],
     )
     early_buffers = gathered(packed[0], count)
+    middle_buffers = gathered(packed[1], count)
+    late_buffers = gathered(packed[2], count)
 
     (high1, wide1, chan1), (high2, wide2, chan2), (high3, wide3, chan3), (high4, wide4, chan4) = shapes
     size4 = gather_four(shapes[3])
@@ -738,24 +770,23 @@
         1.0,
         [jax.ShapeDtypeStruct((size4 + head3, lanes), BF16)],
         [pltpu.VMEM((total3, chan3), F32), pltpu.VMEM((size4 + head3, lanes), F32)],
-        (feat_three, feat_four, top, bottom),
+        (feat_three, feat_four, *rows_border),
         [packed[1]],
     )
     coarse = exchanged(gather, count)
-    to_right, to_left = local(
+    cols_pair = local(
         functools.partial(edges_kernel, layouts),
         1.5,
-        [jax.ShapeDtypeStruct((rows1, 16, LANES), BF16), jax.ShapeDtypeStruct((rows1, 8, LANES), BF16)],
+        [jax.ShapeDtypeStruct((rows1, 16, LANES), BF16)] * 2,
         [
             pltpu.VMEM((rows1, wide1, chan1), F32),
             pltpu.VMEM((rows2, wide2, chan2), F32),
             pltpu.VMEM((rows1, 16, LANES), F32),
         ],
-        (feat_one, feat_two, top, bottom),
+        (feat_one, feat_two, *rows_border),
         [gather],
     )
-    from_left = shifted(to_right, "cols", 1)
-    from_right = shifted(to_left, "cols", -1)
+    cols_border = paired(*cols_pair, "cols")
 
     sizes = (count, row_total, high3, wide3, chan3, high4, wide4, chan4, 6 * unit, 14 * unit)
     own3, own4 = chan3 // count, chan4 // count
@@ -777,7 +808,7 @@
             line,
         ],
         (*coarse, three_t, four_t, bias),
-        [to_right],
+        [cols_pair[0]],
     )
     mids = exchanged(mid, count)
 
@@ -801,11 +832,11 @@
             pltpu.VMEM((high2 + BEFORE[1], max(mid_wide2, y_wide2) + 8, chan2), F32),
             packings[0].scratch("conv_one", count),
             packings[0].scratch("conv_two", count),
-            pltpu.VMEM((count, packings[0].total, LANES), BF16),
+            stack(packings[0], ("conv_one", "conv_two"), count),
             line,
             pltpu.SemaphoreType.DMA((count,)),
         ],
-        (feat_one, feat_two, top, bottom, from_left, from_right, bias),
+        (feat_one, feat_two, *rows_border, *cols_border, bias),
         [mid, *early_buffers],
     )
 
@@ -824,11 +855,9 @@
         [y1],
     )
     coarse_out = [sent[0]] + [flipped(sent[mask], mask, count) for mask in range(1, count)]
-    late_buffers = gathered(packed[1], count)
-
-    span = packings[1].span(("down_one", "down_two"))
+
     downs = local(
-        functools.partial(down_kernel, (packings[1], count, row_total, unit, offs, shapes)),
+        functools.partial(down_kernel, (packings[:2], count, row_total, unit, offs, shapes)),
         5.0,
         [
             jax.ShapeDtypeStruct((high1 // 2, wide1 // 2, 2 * unit), F32),
@@ -841,20 +870,21 @@
             pltpu.VMEM((high1 // 2 + 3, half_wide, 2 * unit), F32),
             pltpu.VMEM((high1 // 4 + 1, max(16, quarter_wide) + 8, LANES), F32),
             pltpu.VMEM((high1 // 4 + 1, quarter_wide, 4 * unit), F32),
-            packings[1].scratch("down_one", count),
+            packings[0].scratch("down_one", count),
             packings[1].scratch("down_two", count),
-            pltpu.VMEM((count, span[1] - span[0], LANES), BF16),
+            stack(packings[0], ("down_one",), count),
+            stack(packings[1], ("down_two",), count),
             line,
+            pltpu.SemaphoreType.DMA((count,)),
             pltpu.SemaphoreType.DMA((count,)),
         ],
         (v1, v2, bias),
-        [sent[0], *late_buffers],
-    )
-
-    span = packings[1].span(LAST)
+        [sent[0], *early_buffers, *middle_buffers],
+    )
+
     return tuple(
         local(
-            functools.partial(join_kernel, (packings[1], count, unit, offs, shapes)),
+            functools.partial(join_kernel, (packings[1:], count, unit, offs, shapes)),
             4.0,
             [jax.ShapeDtypeStruct(shape, BF16) for shape in shapes],
             [
@@ -867,13 +897,16 @@
                 pltpu.VMEM((high2, wide2, LANES), F32),
                 pltpu.VMEM((high1, wide1, LANES), F32),
                 pltpu.VMEM((high4, 8, chan4), F32),
-                *[packings[1].scratch(name, count) for name in LAST],
-                pltpu.VMEM((count, span[1] - span[0], LANES), BF16),
+                *[packings[1].scratch(name, count) for name in LIFTS],
+                packings[2].scratch("down_three", count),
+                stack(packings[1], LIFTS, count),
+                stack(packings[2], ("down_three",), count),
                 line,
+                pltpu.SemaphoreType.DMA((count,)),
                 pltpu.SemaphoreType.DMA((count,)),
             ],
             (*coarse_out, y1, y2, *downs, bias),
-            late_buffers,
+            [*middle_buffers, *late_buffers],
         )
     )
 

time: 74.9 us -> 66.3 us (0.89)
  the two profiles are of different devices: /device:TPU:0 before, /device:TPU:17 now
where the time goes in v3:
time: 66.3 us; the launch traced here: 65.8 us
  Pallas kernels  33 us (50%)
  starting transfers between devices  18.9 us (29%)
  waiting for transfers between devices  9.52 us (14%)
  local copies, waits for them, and re-layouts  3.44 us (5%)
  between operations  0.88 us (1%)
    pallas_call x9, Pallas kernels, local(): pl.pallas_call(kernel, out_shape=list(outs), in_specs=vmem(len(operands))...  33 us
    ppermute x18, starting transfers between devices, flipped(): return lax.ppermute(value, 'cols', [(i, i ^ mask) for i in range(count)])  13.1 us
    ppermute x4, waiting for transfers between devices, paired(): results.append(lax.ppermute(value, axis, ups + [(b, a) for a, b in ups]))  6.47 us
    ppermute x4, starting transfers between devices, paired(): results.append(lax.ppermute(value, axis, ups + [(b, a) for a, b in ups]))  5.88 us
    unnamed x56, local copies, waits for them, and re-layouts  3.44 us
    ppermute x18, waiting for transfers between devices, flipped(): return lax.ppermute(value, 'cols', [(i, i ^ mask) for i in range(count)])  3.05 us
  transfers between devices with their start and end apart: 22, of which 5 were waited for; matrix products, arithmetic and copies ran while one was open for 0% of the time, Pallas kernels for 37%

profile of v3, /device:TPU:17, one launch (start us, length us, event | category | flops | bytes accessed | tf_op | source)
XLA Modules:
  0.0 65.8 jit_solution(9920511623864457559)
XLA Ops:
  0.6 1.7 %shard_map.174 = (bf16[304,128]{1,0:T(8,128)(2,1)}, bf16[304,128]{1,0:T(8,128)(2,1)}) custom-call(bf16[32,32,48]{2,1,0:T(8,128)(2,1)} %refs_0_.1, bf16[16,16,96]{2,1,0:T(8,128)(2,1)} %refs_1_.1, bf16[8,8,192]{2,1,0:T(8,128)(2,1)} %three.3, bf16[4,4,384]{2,1,0:T(4,128)(2,1)} %four.3), custom_call_target="tpu_custom_call" | custom-call | flops 1724999936 | tf_op jit(solution)/shard_map/pallas_call | solution.py:696
  2.4 2.5 %shard_map.175 = (bf16[1392,128]{1,0:T(8,128)(2,1)}, bf16[1632,128]{1,0:T(8,128)(2,1)}, bf16[1344,128]{1,0:T(8,128)(2,1)}) custom-call(bf16[12,864]{1,0:T(8,128)(2,1)} %bitcast.20, bf16[24,1728]{1,0:T(8,128)(2,1)} %bitcast.18, bf16[204,432]{1,0:T(8,128)(2,1)} %bitcast.17, bf16[168,864]{1,0:T(8,128)(2,1)} %bitcast.16, bf16[12,96]{1,0:T(8,128)(2,1)} %bitcast.27, ...), custom_call_target="tpu_custom_call" | custom-call | flops 1724999936 | tf_op jit(solution)/shard_map/pallas_call | solution.py:696
  4.9 1.2 %collective-permute-start.11 = (bf16[1392,128]{1,0:T(8,128)(2,1)}, bf16[1392,128]{1,0:T(8,128)(2,1)S(1)}, u32[]{:S(2)}, u32[]{:S(2)}) collective-permute-start(bf16[1392,128]{1,0:T(8,128)(2,1)} %get-tuple-element.33.refs_8_.refs_4_), channel_id=1, source_target_pairs={{0,2},{1,3},{2,0},{3,1},{4,6},{5,7},{6,4},{7,5},{8,10},{9,11},{10,... | collective-permute-start | bytes 1069064 | tf_op jit(solution)/shard_map/ppermute | solution.py:663
  6.1 1.3 %collective-permute-start = (bf16[304,128]{1,0:T(8,128)(2,1)S(1)}, bf16[304,128]{1,0:T(8,128)(2,1)S(1)}, u32[]{:S(2)}, u32[]{:S(2)}) collective-permute-start(bf16[304,128]{1,0:T(8,128)(2,1)S(1)} %copy-done.18), channel_id=1, source_target_pairs={{0,4},{8,12},{4,0},{12,8},{1,5},{9,13},{5,1},{13,9},{2,6},{10,14},... | collective-permute-start | bytes 233480 | tf_op jit(solution)/shard_map/ppermute | solution.py:671
  7.4 1.9 %collective-permute-start.1 = (bf16[304,128]{1,0:T(8,128)(2,1)S(1)}, bf16[304,128]{1,0:T(8,128)(2,1)S(1)}, u32[]{:S(2)}, u32[]{:S(2)}) collective-permute-start(bf16[304,128]{1,0:T(8,128)(2,1)S(1)} %copy-done.17), channel_id=1, source_target_pairs={{4,8},{8,4},{5,9},{9,5},{6,10},{10,6},{7,11},{11,7},{20,24},{24,20... | collective-permute-start | bytes 233480 | tf_op jit(solution)/shard_map/ppermute | solution.py:671
  9.3 1.3 %collective-permute-start.10 = (bf16[1392,128]{1,0:T(8,128)(2,1)}, bf16[1392,128]{1,0:T(8,128)(2,1)S(1)}, u32[]{:S(2)}, u32[]{:S(2)}) collective-permute-start(bf16[1392,128]{1,0:T(8,128)(2,1)} %get-tuple-element.33.refs_8_.refs_4_), channel_id=1, source_target_pairs={{0,1},{1,0},{2,3},{3,2},{4,5},{5,4},{6,7},{7,6},{8,9},{9,8},{10,11... | collective-permute-start | bytes 1069064 | tf_op jit(solution)/shard_map/ppermute | solution.py:663
  10.6 0.0 collective-permute-done.even.refs_2_
  10.6 2.2 %collective-permute-done.1.odd.refs_3_ = bf16[304,128]{1,0:T(8,128)(2,1)S(1)} collective-permute-done((bf16[304,128]{1,0:T(8,128)(2,1)S(1)}, bf16[304,128]{1,0:T(8,128)(2,1)S(1)}, u32[]{:S(2)}, u32[]{:S(2)}) %collective-permute-start.1) | collective-permute-done | bytes 77856 | tf_op jit(solution)/shard_map/ppermute | solution.py:671
  12.8 0.6 copy-done.16
  13.5 1.7 %shard_map.176.after.refs_0_ = bf16[88,384]{1,0:T(8,128)(2,1)} custom-call(bf16[8,8,192]{2,1,0:T(8,128)(2,1)} %three.3, bf16[4,4,384]{2,1,0:T(4,128)(2,1)} %four.3, bf16[304,128]{1,0:T(8,128)(2,1)} %copy-done.15, bf16[304,128]{1,0:T(8,128)(2,1)} %copy-done.16, bf16[1632,128]{1,0:T(8,128)(2,1)} %get-tuple-element.27.after.refs_8_.refs_10_), custom_call_target="tpu_custom_call" | custom-call | flops 1150000000 | tf_op jit(solution)/shard_map/pallas_call | solution.py:696
  15.1 2.1 %collective-permute-start.2 = (bf16[88,384]{1,0:T(8,128)(2,1)}, bf16[88,384]{1,0:T(8,128)(2,1)S(1)}, u32[]{:S(2)}, u32[]{:S(2)}) collective-permute-start(bf16[88,384]{1,0:T(8,128)(2,1)} %shard_map.176.after.refs_0_), channel_id=1, source_target_pairs={{0,1},{1,0},{2,3},{3,2},{4,5},{5,4},{6,7},{7,6},{8,9},{9,8},{10,11... | collective-permute-start | bytes 202760 | tf_op jit(solution)/shard_map/ppermute | solution.py:663
  17.2 0.3 collective-permute-start.3
  17.5 1.4 %collective-permute-start.4 = (bf16[88,384]{1,0:T(8,128)(2,1)}, bf16[88,384]{1,0:T(8,128)(2,1)S(1)}, u32[]{:S(2)}, u32[]{:S(2)}) collective-permute-start(bf16[88,384]{1,0:T(8,128)(2,1)} %shard_map.176.after.refs_0_), channel_id=1, source_target_pairs={{0,3},{1,2},{2,1},{3,0},{4,7},{5,6},{6,5},{7,4},{8,11},{9,10},{10,... | collective-permute-start | bytes 202760 | tf_op jit(solution)/shard_map/ppermute | solution.py:663
  18.9 2.0 %shard_map.177 = (bf16[43,16,128]{2,1,0:T(8,128)(2,1)}, bf16[43,16,128]{2,1,0:T(8,128)(2,1)}) custom-call(bf16[32,32,48]{2,1,0:T(8,128)(2,1)} %refs_0_.1, bf16[16,16,96]{2,1,0:T(8,128)(2,1)} %refs_1_.1, bf16[304,128]{1,0:T(8,128)(2,1)} %copy-done.15, bf16[304,128]{1,0:T(8,128)(2,1)} %copy-done.16, bf16[88,384]{1,0:T(8,128)(2,1)} %shard_map.176.after.refs_0_), custom_call_target="tpu_custom_call" | custom-call | flops 1724999936 | tf_op jit(solution)/shard_map/pallas_call | solution.py:696
  20.9 0.0 collective-permute-done.2.refs_1_
  20.9 0.3 collective-permute-start.17
  21.2 0.0 collective-permute-done.11.refs_10_.refs_6_
  21.2 0.5 collective-permute-start.12
  21.7 0.0 collective-permute-done.3.refs_2_
  21.7 1.0 %collective-permute-done.4.refs_3_ = bf16[88,384]{1,0:T(8,128)(2,1)S(1)} collective-permute-done((bf16[88,384]{1,0:T(8,128)(2,1)}, bf16[88,384]{1,0:T(8,128)(2,1)S(1)}, u32[]{:S(2)}, u32[]{:S(2)}) %collective-permute-start.4) | collective-permute-done | bytes 67616 | tf_op jit(solution)/shard_map/ppermute | solution.py:663
  22.8 0.6 copy-done.24
  23.4 4.0 %shard_map.178 = (bf16[272,128]{1,0:T(8,128)(2,1)}, bf16[288,48]{1,0:T(8,128)(2,1)}, bf16[64,96]{1,0:T(8,128)(2,1)}) custom-call(bf16[88,384]{1,0:T(8,128)(2,1)} %shard_map.176.after.refs_0_, bf16[88,384]{1,0:T(8,128)(2,1)} %copy-done.22, bf16[88,384]{1,0:T(8,128)(2,1)} %copy-done.23, bf16[88,384]{1,0:T(8,128)(2,1)} %copy-done.24, ...), custom_call_target="tpu_custom_call" | custom-call | flops 3449999872 | tf_op jit(solution)/shard_map/pallas_call | solution.py:696
  27.3 0.0 copy-done.4
  27.3 0.2 collective-permute-start.5
  27.6 0.3 collective-permute-start.8
  27.9 1.0 %collective-permute-done.5.refs_1_ = bf16[272,128]{1,0:T(8,128)(2,1)S(1)} collective-permute-done((bf16[272,128]{1,0:T(8,128)(2,1)}, bf16[272,128]{1,0:T(8,128)(2,1)S(1)}, u32[]{:S(2)}, u32[]{:S(2)}) %collective-permute-start.5) | collective-permute-done | bytes 69664 | tf_op jit(solution)/shard_map/ppermute | solution.py:663
  28.8 2.4 %collective-permute-start.9 = (bf16[43,16,128]{2,1,0:T(8,128)(2,1)S(1)}, bf16[43,16,128]{2,1,0:T(8,128)(2,1)S(1)}, u32[]{:S(2)}, u32[]{:S(2)}) collective-permute-start(bf16[43,16,128]{2,1,0:T(8,128)(2,1)S(1)} %copy-done.12), channel_id=1, source_target_pairs={{1,2},{2,1},{5,6},{6,5},{9,10},{10,9},{13,14},{14,13},{17,18},{18,... | collective-permute-start | bytes 528392 | tf_op jit(solution)/shard_map/ppermute | solution.py:671
  31.2 0.0 collective-permute-done.8.refs_4_
  31.2 0.0 copy-start.11
  31.2 0.1 collective-permute-start.16
  31.3 4.3 %collective-permute-done.9.refs_5_ = bf16[43,16,128]{2,1,0:T(8,128)(2,1)S(1)} collective-permute-done((bf16[43,16,128]{2,1,0:T(8,128)(2,1)S(1)}, bf16[43,16,128]{2,1,0:T(8,128)(2,1)S(1)}, u32[]{:S(2)}, u32[]{:S(2)}) %collective-permute-start.9) | collective-permute-done | bytes 176160 | tf_op jit(solution)/shard_map/ppermute | solution.py:671
  35.6 0.0 copy-done.7
  35.6 0.0 collective-permute-start.20
  35.6 0.0 collective-permute-done.10.refs_9_.refs_5_
  35.6 1.4 %collective-permute-start.6 = (bf16[272,128]{1,0:T(8,128)(2,1)}, bf16[272,128]{1,0:T(8,128)(2,1)S(1)}, u32[]{:S(2)}, u32[]{:S(2)}) collective-permute-start(bf16[272,128]{1,0:T(8,128)(2,1)} %get-tuple-element.29.refs_7_.refs_0_), channel_id=1, source_target_pairs={{0,2},{1,3},{2,0},{3,1},{4,6},{5,7},{6,4},{7,5},{8,10},{9,11},{10,... | collective-permute-start | bytes 208904 | tf_op jit(solution)/shard_map/ppermute | solution.py:663
  37.1 0.0 collective-permute-done.17.refs_10_.refs_12_
  37.1 1.1 %collective-permute-start.7 = (bf16[272,128]{1,0:T(8,128)(2,1)}, bf16[272,128]{1,0:T(8,128)(2,1)S(1)}, u32[]{:S(2)}, u32[]{:S(2)}) collective-permute-start(bf16[272,128]{1,0:T(8,128)(2,1)} %get-tuple-element.29.refs_7_.refs_0_), channel_id=1, source_target_pairs={{0,3},{1,2},{2,1},{3,0},{4,7},{5,6},{6,5},{7,4},{8,11},{9,10},{10,... | collective-permute-start | bytes 208904 | tf_op jit(solution)/shard_map/ppermute | solution.py:663
  38.1 0.0 collective-permute-done.12.refs_11_.refs_7_
  38.1 0.0 collective-permute-start.18
  38.2 0.7 %copy-done.6 = bf16[1392,128]{1,0:T(8,128)(2,1)} copy-done((bf16[1392,128]{1,0:T(8,128)(2,1)}, bf16[1392,128]{1,0:T(8,128)(2,1)S(1)}, u32[]{:S(2)}) %copy-start.6) | copy-done | bytes 356376
  38.8 7.0 %shard_map.179 = (bf16[32,32,48]{2,1,0:T(8,128)(2,1)}, bf16[16,16,96]{2,1,0:T(8,128)(2,1)}, f32[39,56,128]{2,1,0:T(8,128)}, f32[19,40,128]{2,1,0:T(8,128)}) custom-call(bf16[32,32,48]{2,1,0:T(8,128)(2,1)} %refs_0_.1, bf16[16,16,96]{2,1,0:T(8,128)(2,1)} %refs_1_.1, bf16[304,128]{1,0:T(8,128)(2,1)} %copy-done.15, bf16[304,128]{1,0:T(8,128)(2,1)} %copy-done.16, ...), custom_call_target="tpu_custom_call" | custom-call | flops 5750000128 | tf_op jit(solution)/shard_map/pallas_call | solution.py:696
  45.8 1.0 %collective-permute-done.6.refs_2_ = bf16[272,128]{1,0:T(8,128)(2,1)S(1)} collective-permute-done((bf16[272,128]{1,0:T(8,128)(2,1)}, bf16[272,128]{1,0:T(8,128)(2,1)S(1)}, u32[]{:S(2)}, u32[]{:S(2)}) %collective-permute-start.6) | collective-permute-done | bytes 69664 | tf_op jit(solution)/shard_map/ppermute | solution.py:663
  46.9 0.0 collective-permute-start.19
  46.9 0.0 collective-permute-done.20.refs_16_
  46.9 0.5 collective-permute-start.21
  47.4 0.0 collective-permute-done.7.refs_3_
  47.4 0.1 copy-done.20
  47.5 0.5 copy-done.21
  48.0 4.1 %shard_map.180 = (bf16[104,128]{1,0:T(8,128)(2,1)}, bf16[104,128]{1,0:T(8,128)(2,1)}, bf16[104,128]{1,0:T(8,128)(2,1)}, bf16[104,128]{1,0:T(8,128)(2,1)}) custom-call(bf16[272,128]{1,0:T(8,128)(2,1)} %get-tuple-element.29.refs_7_.refs_0_, bf16[272,128]{1,0:T(8,128)(2,1)} %copy-done.19, bf16[272,128]{1,0:T(8,128)(2,1)} %copy-done.20, ...), custom_call_target="tpu_custom_call" | custom-call | flops 3449999872 | tf_op jit(solution)/shard_map/pallas_call | solution.py:696
  52.1 1.0 %collective-permute-start.13 = (bf16[104,128]{1,0:T(8,128)(2,1)}, bf16[104,128]{1,0:T(8,128)(2,1)S(1)}, u32[]{:S(2)}, u32[]{:S(2)}) collective-permute-start(bf16[104,128]{1,0:T(8,128)(2,1)} %get-tuple-element.36), channel_id=1, source_target_pairs={{0,1},{1,0},{2,3},{3,2},{4,5},{5,4},{6,7},{7,6},{8,9},{9,8},{10,11... | collective-permute-start | bytes 79880 | tf_op jit(solution)/shard_map/ppermute | solution.py:663
  53.1 0.0 collective-permute-done.16.refs_9_.refs_11_
  53.1 0.5 collective-permute-start.14
  53.5 0.0 collective-permute-done.18.refs_11_.refs_13_
  53.5 1.3 %collective-permute-start.15 = (bf16[104,128]{1,0:T(8,128)(2,1)}, bf16[104,128]{1,0:T(8,128)(2,1)S(1)}, u32[]{:S(2)}, u32[]{:S(2)}) collective-permute-start(bf16[104,128]{1,0:T(8,128)(2,1)} %get-tuple-element.38), channel_id=1, source_target_pairs={{0,3},{1,2},{2,1},{3,0},{4,7},{5,6},{6,5},{7,4},{8,11},{9,10},{10,... | collective-permute-start | bytes 79880 | tf_op jit(solution)/shard_map/ppermute | solution.py:663
  54.8 5.9 %shard_map.181 = (f32[16,16,96]{2,1,0:T(8,128)}, f32[8,8,192]{2,1,0:T(8,128)}, f32[4,8,384]{2,1,0:T(8,128)}) custom-call(f32[39,56,128]{2,1,0:T(8,128)} %get-tuple-element.40.refs_0_, f32[19,40,128]{2,1,0:T(8,128)} %get-tuple-element.41.refs_1_, f32[30,128]{1,0:T(8,128)} %bitcast.25, bf16[104,128]{1,0:T(8,128)(2,1)} %get-tuple-element.35.refs_3_.refs_0_, ...), custom_call_target="tpu_custom_call" | custom-call | flops 5750000128 | tf_op jit(solution)/shard_map/pallas_call | solution.py:696
  60.7 0.0 collective-permute-done.19.refs_15_
  60.7 0.0 collective-permute-done.21.refs_17_
  60.7 0.0 collective-permute-done.13.refs_1_
  60.7 0.0 collective-permute-done.14.refs_2_
  60.8 0.0 collective-permute-done.15.refs_3_
  60.8 0.6 copy-done.9
  61.4 0.1 copy-done.10
  61.6 0.0 copy-done.27
  61.6 4.3 %shard_map.182 = (bf16[32,32,48]{2,1,0:T(8,128)(2,1)}, bf16[16,16,96]{2,1,0:T(8,128)(2,1)}, bf16[8,8,192]{2,1,0:T(8,128)(2,1)}, bf16[4,4,384]{2,1,0:T(4,128)(2,1)}) custom-call(bf16[104,128]{1,0:T(8,128)(2,1)} %get-tuple-element.35.refs_3_.refs_0_, bf16[104,128]{1,0:T(8,128)(2,1)} %copy-done.25, bf16[104,128]{1,0:T(8,128)(2,1)} %copy-done.26, ...), custom_call_target="tpu_custom_call" | custom-call | flops 4600000000 | tf_op jit(solution)/shard_map/pallas_call | solution.py:696
  (45 shorter events, 0.1 us)
Async XLA Ops:
  2.4 3.7 %copy-start.18 = (bf16[304,128]{1,0:T(8,128)(2,1)S(1)}, bf16[304,128]{1,0:T(8,128)(2,1)}, u32[]{:S(2)}) copy-start(bf16[304,128]{1,0:T(8,128)(2,1)} %get-tuple-element.25.refs_8_) | copy-start | bytes 233476
  2.4 5.0 %copy-start.17 = (bf16[304,128]{1,0:T(8,128)(2,1)S(1)}, bf16[304,128]{1,0:T(8,128)(2,1)}, u32[]{:S(2)}) copy-start(bf16[304,128]{1,0:T(8,128)(2,1)} %get-tuple-element.26) | copy-start | bytes 233476
  4.9 16.3 %collective-permute-start.11 = (bf16[1392,128]{1,0:T(8,128)(2,1)}, bf16[1392,128]{1,0:T(8,128)(2,1)S(1)}, u32[]{:S(2)}, u32[]{:S(2)}) collective-permute-start(bf16[1392,128]{1,0:T(8,128)(2,1)} %get-tuple-element.33.refs_8_.refs_4_), channel_id=1, source_target_pairs={{0,2},{1,3},{2,0},{3,1},{4,6},{5,7},{6,4},{7,5},{8,10},{9,11},{10,... | collective-permute-start | bytes 1069064 | tf_op jit(solution)/shard_map/ppermute | solution.py:663
  6.1 4.5 %collective-permute-start = (bf16[304,128]{1,0:T(8,128)(2,1)S(1)}, bf16[304,128]{1,0:T(8,128)(2,1)S(1)}, u32[]{:S(2)}, u32[]{:S(2)}) collective-permute-start(bf16[304,128]{1,0:T(8,128)(2,1)S(1)} %copy-done.18), channel_id=1, source_target_pairs={{0,4},{8,12},{4,0},{12,8},{1,5},{9,13},{5,1},{13,9},{2,6},{10,14},... | collective-permute-start | bytes 233480 | tf_op jit(solution)/shard_map/ppermute | solution.py:671
  7.4 5.4 %collective-permute-start.1 = (bf16[304,128]{1,0:T(8,128)(2,1)S(1)}, bf16[304,128]{1,0:T(8,128)(2,1)S(1)}, u32[]{:S(2)}, u32[]{:S(2)}) collective-permute-start(bf16[304,128]{1,0:T(8,128)(2,1)S(1)} %copy-done.17), channel_id=1, source_target_pairs={{4,8},{8,4},{5,9},{9,5},{6,10},{10,6},{7,11},{11,7},{20,24},{24,20... | collective-permute-start | bytes 233480 | tf_op jit(solution)/shard_map/ppermute | solution.py:671
  9.3 26.3 %collective-permute-start.10 = (bf16[1392,128]{1,0:T(8,128)(2,1)}, bf16[1392,128]{1,0:T(8,128)(2,1)S(1)}, u32[]{:S(2)}, u32[]{:S(2)}) collective-permute-start(bf16[1392,128]{1,0:T(8,128)(2,1)} %get-tuple-element.33.refs_8_.refs_4_), channel_id=1, source_target_pairs={{0,1},{1,0},{2,3},{3,2},{4,5},{5,4},{6,7},{7,6},{8,9},{9,8},{10,11... | collective-permute-start | bytes 1069064 | tf_op jit(solution)/shard_map/ppermute | solution.py:663
  10.6 2.2 %copy-start.15 = (bf16[304,128]{1,0:T(8,128)(2,1)}, bf16[304,128]{1,0:T(8,128)(2,1)S(1)}, u32[]{:S(2)}) copy-start(bf16[304,128]{1,0:T(8,128)(2,1)S(1)} %collective-permute-done.even.refs_2_) | copy-start | bytes 233476
  12.8 0.6 copy-start.16
  15.1 5.7 %copy-start = (bf16[1632,128]{1,0:T(8,128)(2,1)S(1)}, bf16[1632,128]{1,0:T(8,128)(2,1)}, u32[]{:S(2)}) copy-start(bf16[1632,128]{1,0:T(8,128)(2,1)} %get-tuple-element.27.after.refs_8_.refs_10_) | copy-start | bytes 1253380
  15.1 5.7 %collective-permute-start.2 = (bf16[88,384]{1,0:T(8,128)(2,1)}, bf16[88,384]{1,0:T(8,128)(2,1)S(1)}, u32[]{:S(2)}, u32[]{:S(2)}) collective-permute-start(bf16[88,384]{1,0:T(8,128)(2,1)} %shard_map.176.after.refs_0_), channel_id=1, source_target_pairs={{0,1},{1,0},{2,3},{3,2},{4,5},{5,4},{6,7},{7,6},{8,9},{9,8},{10,11... | collective-permute-start | bytes 202760 | tf_op jit(solution)/shard_map/ppermute | solution.py:663
  17.2 4.5 %collective-permute-start.3 = (bf16[88,384]{1,0:T(8,128)(2,1)}, bf16[88,384]{1,0:T(8,128)(2,1)S(1)}, u32[]{:S(2)}, u32[]{:S(2)}) collective-permute-start(bf16[88,384]{1,0:T(8,128)(2,1)} %shard_map.176.after.refs_0_), channel_id=1, source_target_pairs={{0,2},{1,3},{2,0},{3,1},{4,6},{5,7},{6,4},{7,5},{8,10},{9,11},{10,... | collective-permute-start | bytes 202760 | tf_op jit(solution)/shard_map/ppermute | solution.py:663
  17.5 5.3 %collective-permute-start.4 = (bf16[88,384]{1,0:T(8,128)(2,1)}, bf16[88,384]{1,0:T(8,128)(2,1)S(1)}, u32[]{:S(2)}, u32[]{:S(2)}) collective-permute-start(bf16[88,384]{1,0:T(8,128)(2,1)} %shard_map.176.after.refs_0_), channel_id=1, source_target_pairs={{0,3},{1,2},{2,1},{3,0},{4,7},{5,6},{6,5},{7,4},{8,11},{9,10},{10,... | collective-permute-start | bytes 202760 | tf_op jit(solution)/shard_map/ppermute | solution.py:663
  20.9 1.9 %copy-start.22 = (bf16[88,384]{1,0:T(8,128)(2,1)}, bf16[88,384]{1,0:T(8,128)(2,1)S(1)}, u32[]{:S(2)}) copy-start(bf16[88,384]{1,0:T(8,128)(2,1)S(1)} %collective-permute-done.2.refs_1_) | copy-start | bytes 202756
  20.9 16.2 %collective-permute-start.17 = (bf16[1632,128]{1,0:T(8,128)(2,1)S(1)}, bf16[1632,128]{1,0:T(8,128)(2,1)S(1)}, u32[]{:S(2)}, u32[]{:S(2)}) collective-permute-start(bf16[1632,128]{1,0:T(8,128)(2,1)S(1)} %copy-done), channel_id=1, source_target_pairs={{0,2},{1,3},{2,0},{3,1},{4,6},{5,7},{6,4},{7,5},{8,10},{9,11},{10,... | collective-permute-start | bytes 1253384 | tf_op jit(solution)/shard_map/ppermute | solution.py:663
  21.2 6.1 %copy-start.4 = (bf16[1392,128]{1,0:T(8,128)(2,1)}, bf16[1392,128]{1,0:T(8,128)(2,1)S(1)}, u32[]{:S(2)}) copy-start(bf16[1392,128]{1,0:T(8,128)(2,1)S(1)} %collective-permute-done.11.refs_10_.refs_6_) | copy-start | bytes 1069060
  21.2 16.9 %collective-permute-start.12 = (bf16[1392,128]{1,0:T(8,128)(2,1)S(1)}, bf16[1392,128]{1,0:T(8,128)(2,1)S(1)}, u32[]{:S(2)}, u32[]{:S(2)}) collective-permute-start(bf16[1392,128]{1,0:T(8,128)(2,1)S(1)} %collective-permute-done.11.refs_10_.refs_6_), channel_id=1, source_target_pairs={{0,1},{1,0},{2,3},{3,2},{4,5},{5,4},{6,7},{7,6},{8,9},{9,8},{10,11... | collective-permute-start | bytes 1069064 | tf_op jit(solution)/shard_map/ppermute | solution.py:663
  21.7 1.0 %copy-start.23 = (bf16[88,384]{1,0:T(8,128)(2,1)}, bf16[88,384]{1,0:T(8,128)(2,1)S(1)}, u32[]{:S(2)}) copy-start(bf16[88,384]{1,0:T(8,128)(2,1)S(1)} %collective-permute-done.3.refs_2_) | copy-start | bytes 202756
  22.8 0.6 copy-start.24
  23.4 4.2 %copy-start.14 = (bf16[43,16,128]{2,1,0:T(8,128)(2,1)S(1)}, bf16[43,16,128]{2,1,0:T(8,128)(2,1)}, u32[]{:S(2)}) copy-start(bf16[43,16,128]{2,1,0:T(8,128)(2,1)} %get-tuple-element.28.refs_7_) | copy-start | bytes 528388
  23.4 5.4 %copy-start.12 = (bf16[43,16,128]{2,1,0:T(8,128)(2,1)S(1)}, bf16[43,16,128]{2,1,0:T(8,128)(2,1)}, u32[]{:S(2)}) copy-start(bf16[43,16,128]{2,1,0:T(8,128)(2,1)} %get-tuple-element.32) | copy-start | bytes 528388
  23.4 12.2 %copy-start.7 = (bf16[1344,128]{1,0:T(8,128)(2,1)S(1)}, bf16[1344,128]{1,0:T(8,128)(2,1)}, u32[]{:S(2)}) copy-start(bf16[1344,128]{1,0:T(8,128)(2,1)} %get-tuple-element.45.refs_14_) | copy-start | bytes 1032196
  27.3 1.5 %collective-permute-start.5 = (bf16[272,128]{1,0:T(8,128)(2,1)}, bf16[272,128]{1,0:T(8,128)(2,1)S(1)}, u32[]{:S(2)}, u32[]{:S(2)}) collective-permute-start(bf16[272,128]{1,0:T(8,128)(2,1)} %get-tuple-element.29.refs_7_.refs_0_), channel_id=1, source_target_pairs={{0,1},{1,0},{2,3},{3,2},{4,5},{5,4},{6,7},{7,6},{8,9},{9,8},{10,11... | collective-permute-start | bytes 208904 | tf_op jit(solution)/shard_map/ppermute | solution.py:663
  27.6 3.6 %collective-permute-start.8 = (bf16[43,16,128]{2,1,0:T(8,128)(2,1)S(1)}, bf16[43,16,128]{2,1,0:T(8,128)(2,1)S(1)}, u32[]{:S(2)}, u32[]{:S(2)}) collective-permute-start(bf16[43,16,128]{2,1,0:T(8,128)(2,1)S(1)} %copy-done.14), channel_id=1, source_target_pairs={{0,1},{2,3},{1,0},{3,2},{4,5},{6,7},{5,4},{7,6},{8,9},{10,11},{9,8... | collective-permute-start | bytes 528392 | tf_op jit(solution)/shard_map/ppermute | solution.py:671
  28.8 17.0 %copy-start.19 = (bf16[272,128]{1,0:T(8,128)(2,1)}, bf16[272,128]{1,0:T(8,128)(2,1)S(1)}, u32[]{:S(2)}) copy-start(bf16[272,128]{1,0:T(8,128)(2,1)S(1)} %collective-permute-done.5.refs_1_) | copy-start | bytes 208900
  28.8 6.8 %collective-permute-start.9 = (bf16[43,16,128]{2,1,0:T(8,128)(2,1)S(1)}, bf16[43,16,128]{2,1,0:T(8,128)(2,1)S(1)}, u32[]{:S(2)}, u32[]{:S(2)}) collective-permute-start(bf16[43,16,128]{2,1,0:T(8,128)(2,1)S(1)} %copy-done.12), channel_id=1, source_target_pairs={{1,2},{2,1},{5,6},{6,5},{9,10},{10,9},{13,14},{14,13},{17,18},{18,... | collective-permute-start | bytes 528392 | tf_op jit(solution)/shard_map/ppermute | solution.py:671
  31.2 6.9 %copy-start.11 = (bf16[43,16,128]{2,1,0:T(8,128)(2,1)}, bf16[43,16,128]{2,1,0:T(8,128)(2,1)S(1)}, u32[]{:S(2)}) copy-start(bf16[43,16,128]{2,1,0:T(8,128)(2,1)S(1)} %collective-permute-done.8.refs_4_) | copy-start | bytes 528388
  31.2 21.8 %collective-permute-start.16 = (bf16[1632,128]{1,0:T(8,128)(2,1)S(1)}, bf16[1632,128]{1,0:T(8,128)(2,1)S(1)}, u32[]{:S(2)}, u32[]{:S(2)}) collective-permute-start(bf16[1632,128]{1,0:T(8,128)(2,1)S(1)} %copy-done), channel_id=1, source_target_pairs={{0,1},{1,0},{2,3},{3,2},{4,5},{5,4},{6,7},{7,6},{8,9},{9,8},{10,11... | collective-permute-start | bytes 1253384 | tf_op jit(solution)/shard_map/ppermute | solution.py:663
  35.6 2.6 %copy-start.13 = (bf16[43,16,128]{2,1,0:T(8,128)(2,1)}, bf16[43,16,128]{2,1,0:T(8,128)(2,1)S(1)}, u32[]{:S(2)}) copy-start(bf16[43,16,128]{2,1,0:T(8,128)(2,1)S(1)} %collective-permute-done.9.refs_5_) | copy-start | bytes 528388
  35.6 11.3 %collective-permute-start.20 = (bf16[1344,128]{1,0:T(8,128)(2,1)S(1)}, bf16[1344,128]{1,0:T(8,128)(2,1)S(1)}, u32[]{:S(2)}, u32[]{:S(2)}) collective-permute-start(bf16[1344,128]{1,0:T(8,128)(2,1)S(1)} %copy-done.7), channel_id=1, source_target_pairs={{0,2},{1,3},{2,0},{3,1},{4,6},{5,7},{6,4},{7,5},{8,10},{9,11},{10,... | collective-permute-start | bytes 1032200 | tf_op jit(solution)/shard_map/ppermute | solution.py:663
  35.6 2.5 %copy-start.5 = (bf16[1392,128]{1,0:T(8,128)(2,1)}, bf16[1392,128]{1,0:T(8,128)(2,1)S(1)}, u32[]{:S(2)}) copy-start(bf16[1392,128]{1,0:T(8,128)(2,1)S(1)} %collective-permute-done.10.refs_9_.refs_5_) | copy-start | bytes 1069060
  35.6 11.3 %collective-permute-start.6 = (bf16[272,128]{1,0:T(8,128)(2,1)}, bf16[272,128]{1,0:T(8,128)(2,1)S(1)}, u32[]{:S(2)}, u32[]{:S(2)}) collective-permute-start(bf16[272,128]{1,0:T(8,128)(2,1)} %get-tuple-element.29.refs_7_.refs_0_), channel_id=1, source_target_pairs={{0,2},{1,3},{2,0},{3,1},{4,6},{5,7},{6,4},{7,5},{8,10},{9,11},{10,... | collective-permute-start | bytes 208904 | tf_op jit(solution)/shard_map/ppermute | solution.py:663
  37.1 8.8 %copy-start.1 = (bf16[1632,128]{1,0:T(8,128)(2,1)}, bf16[1632,128]{1,0:T(8,128)(2,1)S(1)}, u32[]{:S(2)}) copy-start(bf16[1632,128]{1,0:T(8,128)(2,1)S(1)} %collective-permute-done.17.refs_10_.refs_12_) | copy-start | bytes 1253380
  37.1 10.3 %collective-permute-start.7 = (bf16[272,128]{1,0:T(8,128)(2,1)}, bf16[272,128]{1,0:T(8,128)(2,1)S(1)}, u32[]{:S(2)}, u32[]{:S(2)}) collective-permute-start(bf16[272,128]{1,0:T(8,128)(2,1)} %get-tuple-element.29.refs_7_.refs_0_), channel_id=1, source_target_pairs={{0,3},{1,2},{2,1},{3,0},{4,7},{5,6},{6,5},{7,4},{8,11},{9,10},{10,... | collective-permute-start | bytes 208904 | tf_op jit(solution)/shard_map/ppermute | solution.py:663
  38.1 0.7 %copy-start.6 = (bf16[1392,128]{1,0:T(8,128)(2,1)}, bf16[1392,128]{1,0:T(8,128)(2,1)S(1)}, u32[]{:S(2)}) copy-start(bf16[1392,128]{1,0:T(8,128)(2,1)S(1)} %collective-permute-done.12.refs_11_.refs_7_) | copy-start | bytes 1069060
  38.1 15.4 %collective-permute-start.18 = (bf16[1632,128]{1,0:T(8,128)(2,1)S(1)}, bf16[1632,128]{1,0:T(8,128)(2,1)S(1)}, u32[]{:S(2)}, u32[]{:S(2)}) collective-permute-start(bf16[1632,128]{1,0:T(8,128)(2,1)S(1)} %collective-permute-done.17.refs_10_.refs_12_), channel_id=1, source_target_pairs={{0,1},{1,0},{2,3},{3,2},{4,5},{5,4},{6,7},{7,6},{8,9},{9,8},{10,11... | collective-permute-start | bytes 1253384 | tf_op jit(solution)/shard_map/ppermute | solution.py:663
  46.9 0.6 copy-start.20
  46.9 13.8 %collective-permute-start.19 = (bf16[1344,128]{1,0:T(8,128)(2,1)S(1)}, bf16[1344,128]{1,0:T(8,128)(2,1)S(1)}, u32[]{:S(2)}, u32[]{:S(2)}) collective-permute-start(bf16[1344,128]{1,0:T(8,128)(2,1)S(1)} %copy-done.7), channel_id=1, source_target_pairs={{0,1},{1,0},{2,3},{3,2},{4,5},{5,4},{6,7},{7,6},{8,9},{9,8},{10,11... | collective-permute-start | bytes 1032200 | tf_op jit(solution)/shard_map/ppermute | solution.py:663
  46.9 5.2 %copy-start.8 = (bf16[1344,128]{1,0:T(8,128)(2,1)}, bf16[1344,128]{1,0:T(8,128)(2,1)S(1)}, u32[]{:S(2)}) copy-start(bf16[1344,128]{1,0:T(8,128)(2,1)S(1)} %collective-permute-done.20.refs_16_) | copy-start | bytes 1032196
  46.9 13.8 %collective-permute-start.21 = (bf16[1344,128]{1,0:T(8,128)(2,1)S(1)}, bf16[1344,128]{1,0:T(8,128)(2,1)S(1)}, u32[]{:S(2)}, u32[]{:S(2)}) collective-permute-start(bf16[1344,128]{1,0:T(8,128)(2,1)S(1)} %collective-permute-done.20.refs_16_), channel_id=1, source_target_pairs={{0,1},{1,0},{2,3},{3,2},{4,5},{5,4},{6,7},{7,6},{8,9},{9,8},{10,11... | collective-permute-start | bytes 1032200 | tf_op jit(solution)/shard_map/ppermute | solution.py:663
  47.4 0.6 copy-start.21
  52.1 8.6 %collective-permute-start.13 = (bf16[104,128]{1,0:T(8,128)(2,1)}, bf16[104,128]{1,0:T(8,128)(2,1)S(1)}, u32[]{:S(2)}, u32[]{:S(2)}) collective-permute-start(bf16[104,128]{1,0:T(8,128)(2,1)} %get-tuple-element.36), channel_id=1, source_target_pairs={{0,1},{1,0},{2,3},{3,2},{4,5},{5,4},{6,7},{7,6},{8,9},{9,8},{10,11... | collective-permute-start | bytes 79880 | tf_op jit(solution)/shard_map/ppermute | solution.py:663
  53.1 1.7 %copy-start.2 = (bf16[1632,128]{1,0:T(8,128)(2,1)}, bf16[1632,128]{1,0:T(8,128)(2,1)S(1)}, u32[]{:S(2)}) copy-start(bf16[1632,128]{1,0:T(8,128)(2,1)S(1)} %collective-permute-done.16.refs_9_.refs_11_) | copy-start | bytes 1253380
  53.1 7.7 %collective-permute-start.14 = (bf16[104,128]{1,0:T(8,128)(2,1)}, bf16[104,128]{1,0:T(8,128)(2,1)S(1)}, u32[]{:S(2)}, u32[]{:S(2)}) collective-permute-start(bf16[104,128]{1,0:T(8,128)(2,1)} %get-tuple-element.37), channel_id=1, source_target_pairs={{0,2},{1,3},{2,0},{3,1},{4,6},{5,7},{6,4},{7,5},{8,10},{9,11},{10,... | collective-permute-start | bytes 79880 | tf_op jit(solution)/shard_map/ppermute | solution.py:663
  53.5 1.3 %copy-start.3 = (bf16[1632,128]{1,0:T(8,128)(2,1)}, bf16[1632,128]{1,0:T(8,128)(2,1)S(1)}, u32[]{:S(2)}) copy-start(bf16[1632,128]{1,0:T(8,128)(2,1)S(1)} %collective-permute-done.18.refs_11_.refs_13_) | copy-start | bytes 1253380
  53.5 7.2 %collective-permute-start.15 = (bf16[104,128]{1,0:T(8,128)(2,1)}, bf16[104,128]{1,0:T(8,128)(2,1)S(1)}, u32[]{:S(2)}, u32[]{:S(2)}) collective-permute-start(bf16[104,128]{1,0:T(8,128)(2,1)} %get-tuple-element.38), channel_id=1, source_target_pairs={{0,3},{1,2},{2,1},{3,0},{4,7},{5,6},{6,5},{7,4},{8,11},{9,10},{10,... | collective-permute-start | bytes 79880 | tf_op jit(solution)/shard_map/ppermute | solution.py:663
  60.7 0.7 %copy-start.9 = (bf16[1344,128]{1,0:T(8,128)(2,1)}, bf16[1344,128]{1,0:T(8,128)(2,1)S(1)}, u32[]{:S(2)}) copy-start(bf16[1344,128]{1,0:T(8,128)(2,1)S(1)} %collective-permute-done.19.refs_15_) | copy-start | bytes 1032196
  60.7 0.8 %copy-start.10 = (bf16[1344,128]{1,0:T(8,128)(2,1)}, bf16[1344,128]{1,0:T(8,128)(2,1)S(1)}, u32[]{:S(2)}) copy-start(bf16[1344,128]{1,0:T(8,128)(2,1)S(1)} %collective-permute-done.21.refs_17_) | copy-start | bytes 1032196
  60.7 0.8 %copy-start.25 = (bf16[104,128]{1,0:T(8,128)(2,1)}, bf16[104,128]{1,0:T(8,128)(2,1)S(1)}, u32[]{:S(2)}) copy-start(bf16[104,128]{1,0:T(8,128)(2,1)S(1)} %collective-permute-done.13.refs_1_) | copy-start | bytes 79876
  60.7 0.8 %copy-start.26 = (bf16[104,128]{1,0:T(8,128)(2,1)}, bf16[104,128]{1,0:T(8,128)(2,1)S(1)}, u32[]{:S(2)}) copy-start(bf16[104,128]{1,0:T(8,128)(2,1)S(1)} %collective-permute-done.14.refs_2_) | copy-start | bytes 79876
  60.8 0.8 %copy-start.27 = (bf16[104,128]{1,0:T(8,128)(2,1)}, bf16[104,128]{1,0:T(8,128)(2,1)S(1)}, u32[]{:S(2)}) copy-start(bf16[104,128]{1,0:T(8,128)(2,1)S(1)} %collective-permute-done.15.refs_3_) | copy-start | bytes 79876
